TPU v7x, 512 devices: a whole 4x8x8 slice. The times are simulated.
512 devices in a mesh: ctx: 64 (over z_hi, y, core), dp: 8 (over x, z_lo).
Axes of the slice: x: 4, y: 8, z: 8 (z_hi: 4, z_lo: 2; z = z_hi * 2 + z_lo), core: 2. Of those that a mesh axis runs over, the one named last changes fastest.
Arguments:
- tokens_in: bfloat16 [8, 8192, 8192], P('dp', 'ctx')
- queries_in: bfloat16 [8, 8192, 2048], P('dp', 'ctx'), may hold values from -6 to 6
- kv_weight: bfloat16 [8192, 256], P(('ctx', 'dp')), may hold values from -0.0625 to 0.0625
- out_grad: bfloat16 [8, 8192, 2048], P('dp', 'ctx'), may hold values from -6 to 6
- doc_lengths: int32 [8, 32], P('dp'), may hold values from 1 to 512, 8192 in all within a row
Outputs:
- attn_out: bfloat16 [8, 8192, 2048], P('dp', 'ctx')
- query_grad: bfloat16 [8, 8192, 2048], P('dp', 'ctx')
- weight_grad: float32 [8192, 256], P(('ctx', 'dp'))
Inputs may be any that keep to these rules, and one draw needn't show every extreme that they name: `doc_lengths`: each row holds the lengths of the 32 documents of one sequence; they sum to 8192 and the longest is exactly 512.
All inputs are finite; a program needn't handle non-finite values.
Results may differ from a plain program's by a relative error of at most 0.034.
Values may be sent and summed in bfloat16 or wider, within the bound.
No kernel may reach another device: no remote copies, remote signals or barrier semaphores. Data moves between devices by JAX's collectives and lax.ppermute only.
A program may use at most 64 MiB of HBM per device.

v0:
```python
import jax
import jax.numpy as jnp
from jax import lax
from jax.sharding import PartitionSpec as P


def passed_along(block, axis, distance):
    devices = range(lax.axis_size(axis))
    route = [(i - distance, i) for i in devices if i - distance in devices]
    return lax.ppermute(block, axis, route)


def doc_index(positions, doc_ends):
    return jnp.sum((positions[:, None] >= doc_ends[None, :]).astype(jnp.int32), axis=1)


def per_device(tokens_in, queries_in, kv_weight, out_grad, doc_lengths):
    local_rows = tokens_in[0]
    doc_lens = doc_lengths[0]
    tok_count = local_rows.shape[0]
    head_dim = kv_weight.shape[1] // 2
    heads = queries_in.shape[2] // head_dim
    queries = queries_in[0].reshape(tok_count, heads, head_dim)
    grads_out = out_grad[0].reshape(tok_count, heads, head_dim)
    reach = lax.axis_size("ctx") // 16
    qk_scale = head_dim ** (-0.5)
    doc_ends = jnp.cumsum(doc_lens)
    first_pos = lax.axis_index("ctx") * tok_count
    query_pos = first_pos + jnp.arange(tok_count, dtype=jnp.int32)
    query_doc = doc_index(query_pos, doc_ends)
    projected = jnp.dot(
        local_rows,
        lax.all_gather(kv_weight, ("ctx", "dp"), axis=0, tiled=True),
        preferred_element_type=jnp.float32,
    )
    kv_rows = projected.astype(jnp.bfloat16)
    key_rows = kv_rows[:, :head_dim]
    values = kv_rows[:, head_dim:]

    def piece_mask(hop):
        key_pos = first_pos - hop * tok_count + jnp.arange(tok_count, dtype=jnp.int32)
        key_doc = doc_index(key_pos, doc_ends)
        allowed = (
            (key_pos[None, :] >= 0)
            & (key_pos[None, :] <= query_pos[:, None])
            & (key_doc[None, :] == query_doc[:, None])
        )
        return allowed[:, None, :]

    def forward_step(running, shard_part, mask3):
        run_max, run_sum, run_acc = running
        key_part, value_part = shard_part
        scores = (
            jnp.einsum("tgd,nd->tgn", queries, key_part, preferred_element_type=jnp.float32)
            * qk_scale
        )
        new_max = jnp.maximum(
            run_max, jnp.max(jnp.where(mask3, scores, jnp.float32(-1e30)), axis=2)
        )
        factor = jnp.exp(run_max - new_max)
        weights = jnp.where(mask3, jnp.exp(scores - new_max[:, :, None]), jnp.float32(0.0))
        new_sum = run_sum * factor + jnp.sum(weights, axis=2)
        new_acc = run_acc * factor[:, :, None] + jnp.einsum(
            "tgn,nd->tgd",
            weights.astype(jnp.bfloat16),
            value_part,
            preferred_element_type=jnp.float32,
        )
        return (new_max, new_sum, new_acc)

    start_fwd = (
        jnp.full((tok_count, heads), -1e30, jnp.float32),
        jnp.zeros((tok_count, heads), jnp.float32),
        jnp.zeros((tok_count, heads, head_dim), jnp.float32),
    )
    state = forward_step(start_fwd, (key_rows, values), piece_mask(0))
    for hop in range(1, reach + 1):
        near_part = passed_along((key_rows, values), "ctx", hop)
        state = forward_step(state, near_part, piece_mask(hop))
    run_max, run_sum, run_acc = state
    attn = (run_acc / run_sum[:, :, None]).astype(jnp.bfloat16)
    log_sum = run_max + jnp.log(run_sum)
    out_dot = jnp.sum(grads_out.astype(jnp.float32) * attn.astype(jnp.float32), axis=2)

    def backward_step(running, shard_part, mask3):
        grad_q = running[0]
        key_part, value_part = shard_part
        scores = (
            jnp.einsum("tgd,nd->tgn", queries, key_part, preferred_element_type=jnp.float32)
            * qk_scale
        )
        probs = jnp.where(mask3, jnp.exp(scores - log_sum[:, :, None]), jnp.float32(0.0))
        dprobs = jnp.einsum(
            "tgd,nd->tgn", grads_out, value_part, preferred_element_type=jnp.float32
        )
        dscores = (probs * (dprobs - out_dot[:, :, None])).astype(jnp.bfloat16)
        new_q = (
            grad_q
            + jnp.einsum("tgn,nd->tgd", dscores, key_part, preferred_element_type=jnp.float32)
            * qk_scale
        )
        part_k = (
            jnp.einsum("tgn,tgd->nd", dscores, queries, preferred_element_type=jnp.float32)
            * qk_scale
        )
        part_v = jnp.einsum(
            "tgn,tgd->nd", probs.astype(jnp.bfloat16), grads_out, preferred_element_type=jnp.float32
        )
        return (new_q, part_k, part_v)

    zeros_part = jnp.zeros((tok_count, head_dim), jnp.float32)
    start_bwd = (jnp.zeros((tok_count, heads, head_dim), jnp.float32), zeros_part, zeros_part)
    grad_q, grad_k, grad_v = backward_step(start_bwd, (key_rows, values), piece_mask(0))
    for hop in range(1, reach + 1):
        near_part = passed_along((key_rows, values), "ctx", hop)
        grad_q, part_k, part_v = backward_step(
            (grad_q, zeros_part, zeros_part), near_part, piece_mask(hop)
        )
        back_k, back_v = (
            passed_along(part_k.astype(jnp.bfloat16), "ctx", -hop).astype(part_k.dtype),
            passed_along(part_v.astype(jnp.bfloat16), "ctx", -hop).astype(part_v.dtype),
        )
        grad_k = grad_k + back_k
        grad_v = grad_v + back_v
    query_grad = grad_q.astype(jnp.bfloat16).reshape(tok_count, heads * head_dim)
    kv_grad = jnp.concatenate([grad_k, grad_v], axis=1).astype(jnp.bfloat16)
    feature_cols = lax.all_to_all(local_rows, "ctx", split_axis=1, concat_axis=0, tiled=True)
    owned_grad = lax.dot_general(
        feature_cols,
        lax.all_gather(kv_grad, "ctx", axis=0, tiled=True),
        (((0,), (0,)), ((), ())),
        preferred_element_type=jnp.float32,
    )
    weight_grad = lax.psum_scatter(
        owned_grad.astype(jnp.bfloat16), "dp", scatter_dimension=0, tiled=True
    ).astype(jnp.float32)
    return (attn.reshape(tok_count, heads * head_dim)[None], query_grad[None], weight_grad)


def solution(mesh):
    return jax.shard_map(
        per_device,
        mesh=mesh,
        in_specs=(
            P("dp", "ctx", None),
            P("dp", "ctx", None),
            P(("ctx", "dp"), None),
            P("dp", "ctx", None),
            P("dp", None),
        ),
        out_specs=(P("dp", "ctx", None), P("dp", "ctx", None), P(("ctx", "dp"), None)),
        check_vma=False,
    )
```

profile of v0, /device:TPU:6, one launch (start us, length us, event | category | flops | bytes accessed | tf_op | source)
XLA Modules:
  0.0 1677.3 jit_solution(14888641591318195408)
XLA Ops:
  10.0 1.3 copy.206
  11.9 1382.5 %all-gather.3.cloned.1.call-done = bf16[8192,256]{1,0:T(8,128)(2,1)} async-done(((bf16[16,256]{1,0:T(8,128)(2,1)}), bf16[8192,256]{1,0:T(8,128)(2,1)}) %all-gather.3.cloned.1.call-update) | async-done | bytes 4194320 | tf_op jit(solution)/shard_map/all_gather | solution.py:33
  1394.4 2.9 fusion.35
  1397.3 1.3 collective-permute-start.5
  1398.6 10.1 collective-permute-start.3
  1408.6 1.8 collective-permute-start.1
  1410.4 4.8 collective-permute-start.7
  1415.2 2.2 collective-permute-start
  1418.2 4.6 collective-permute-start.2
  1427.2 7.1 collective-permute-start.6
  1438.6 1.3 collective-permute-start.15
  1440.3 1.3 collective-permute-start.14
  1441.9 1.3 collective-permute-start.13
  1443.6 1.3 collective-permute-start.12
  1445.2 1.5 multiply_reduce_fusion
  1450.1 1.3 collective-permute-start.8
  1451.4 1.3 collective-permute-start.9
  1452.7 1.3 collective-permute-start.10
  1454.1 1.3 collective-permute-start.11
  1455.7 3.7 collective-permute-done.9
  1459.4 1.7 collective-permute-done.10
  1461.1 5.7 collective-permute-done.11
  1467.9 2.5 copy.241
  1470.4 92.8 %all_to_all.19 = bf16[128,64,128]{0,2,1:T(8,128)(2,1)} all-to-all(bf16[128,64,128]{0,2,1:T(8,128)(2,1)} %bitcast.226), channel_id=1, replica_groups=mesh['ctx'=64,'dp'=8] {'ctx'}, dimensions={1} | all-to-all | bytes 4194304 | tf_op jit(solution)/shard_map/all_to_all | solution.py:127
  1563.2 3.3 copy.242
  1566.9 1.4 fusion.117
  1568.2 1.3 fusion.112
  1569.6 1.3 convolution_add_fusion.1
  1570.9 59.4 %all-gather.5.cloned.1.call-done = bf16[8192,256]{0,1:T(8,128)(2,1)} async-done(((bf16[128,256]{0,1:T(8,128)(2,1)}), bf16[8192,256]{0,1:T(8,128)(2,1)}) %all-gather.5.cloned.1.call-update) | async-done | bytes 4194320 | tf_op jit(solution)/shard_map/all_gather | solution.py:130
  1630.3 3.5 fusion.43
  1634.6 2.3 fusion.32
  1639.0 30.3 %reduce-scatter.4.cloned.1.call-done = bf16[16,256]{1,0:T(8,128)(2,1)} async-done(((bf16[128,256]{1,0:T(8,128)(2,1)}), bf16[16,256]{1,0:T(8,128)(2,1)}) %reduce-scatter.4.cloned.1.call-update) | async-done | bytes 8208
  (95 shorter events, 23.4 us)
Async XLA Ops:
  7.2 1387.2 %copy-start = (bf16[1,128,8192]{2,1,0:T(8,128)(2,1)S(1)}, bf16[1,128,8192]{2,1,0:T(8,128)(2,1)}, u32[]{:S(2)}) copy-start(bf16[1,128,8192]{2,1,0:T(8,128)(2,1)} %param.5) | copy-start | bytes 6291460
  7.2 1387.2 %all-gather.3.cloned.1.call-start = ((), (), s32[]{:S(2)}) async-start(), calls=%async_computation.2 | async-start | bytes 4202496 | tf_op jit(solution)/shard_map/all_gather | solution.py:33
  7.9 1622.4 %all-gather.5.cloned.1.call-start = ((), (), s32[]{:S(2)}) async-start(), calls=%async_computation.3 | async-start | bytes 4259840 | tf_op jit(solution)/shard_map/all_gather | solution.py:130
  1397.3 43.0 %collective-permute-start.5 = (bf16[128,128]{1,0:T(8,128)(2,1)S(1)}, bf16[128,128]{1,0:T(8,128)(2,1)S(1)}, u32[]{:S(2)}, u32[]{:S(2)}) collective-permute-start(bf16[128,128]{1,0:T(8,128)(2,1)S(1)} %get-tuple-element.33), channel_id=1, source_target_pairs={{0,24},{8,32},{16,40},{24,48},{32,56},{40,64},{48,72},{56,80},{64,... | collective-permute-start | bytes 98312 | tf_op jit(solution)/shard_map/ppermute | solution.py:10
  1398.6 43.3 %collective-permute-start.3 = (bf16[128,128]{1,0:T(8,128)(2,1)S(1)}, bf16[128,128]{1,0:T(8,128)(2,1)S(1)}, u32[]{:S(2)}, u32[]{:S(2)}) collective-permute-start(bf16[128,128]{1,0:T(8,128)(2,1)S(1)} %get-tuple-element.33), channel_id=1, source_target_pairs={{0,16},{8,24},{16,32},{24,40},{32,48},{40,56},{48,64},{56,72},{64,... | collective-permute-start | bytes 98312 | tf_op jit(solution)/shard_map/ppermute | solution.py:10
  1408.6 36.6 %collective-permute-start.1 = (bf16[128,128]{1,0:T(8,128)(2,1)S(1)}, bf16[128,128]{1,0:T(8,128)(2,1)S(1)}, u32[]{:S(2)}, u32[]{:S(2)}) collective-permute-start(bf16[128,128]{1,0:T(8,128)(2,1)S(1)} %get-tuple-element.33), channel_id=1, source_target_pairs={{0,8},{8,16},{16,24},{24,32},{32,40},{40,48},{48,56},{56,64},{64,7... | collective-permute-start | bytes 98312 | tf_op jit(solution)/shard_map/ppermute | solution.py:10
  1410.4 33.2 %collective-permute-start.7 = (bf16[128,128]{1,0:T(8,128)(2,1)S(1)}, bf16[128,128]{1,0:T(8,128)(2,1)S(1)}, u32[]{:S(2)}, u32[]{:S(2)}) collective-permute-start(bf16[128,128]{1,0:T(8,128)(2,1)S(1)} %get-tuple-element.33), channel_id=1, source_target_pairs={{0,32},{8,40},{16,48},{24,56},{32,64},{40,72},{48,80},{56,88},{64,... | collective-permute-start | bytes 98312 | tf_op jit(solution)/shard_map/ppermute | solution.py:10
  1415.2 3.0 collective-permute-start
  1418.2 6.1 collective-permute-start.2
  1424.4 2.9 collective-permute-start.4
  1427.2 8.6 collective-permute-start.6
  1438.6 12.8 collective-permute-start.15
  1440.3 12.5 collective-permute-start.14
  1441.9 12.1 collective-permute-start.13
  1443.6 11.8 collective-permute-start.12
  1447.1 19.7 %copy-start.1 = (bf16[128,16,128]{0,2,1:T(8,128)(2,1)}, bf16[128,16,128]{0,2,1:T(8,128)(2,1)S(1)}, u32[]{:S(2)}) copy-start(bf16[128,16,128]{0,2,1:T(8,128)(2,1)S(1)} %fusion.29) | copy-start | bytes 1572868
  1447.5 1.1 copy-start.3
  1448.2 1.1 copy-start.5
  1449.0 1.1 copy-start.9
  1449.7 17.4 %copy-start.7 = (bf16[128,16,128]{0,2,1:T(8,128)(2,1)}, bf16[128,16,128]{0,2,1:T(8,128)(2,1)S(1)}, u32[]{:S(2)}) copy-start(bf16[128,16,128]{0,2,1:T(8,128)(2,1)S(1)} %fusion.30) | copy-start | bytes 1572868
  1450.1 5.6 collective-permute-start.8
  1451.4 7.9 collective-permute-start.9
  1452.7 8.4 collective-permute-start.10
  1454.1 12.8 collective-permute-start.11
  1467.9 201.4 %reduce-scatter.4.cloned.1.call-start = ((), (), s32[]{:S(2)}) async-start(), calls=%async_computation.4 | async-start | bytes 73728
  1563.2 3.3 copy-start.2
  1563.2 3.7 copy-start.6
  1566.5 1.7 copy-start.4
  1566.5 3.1 copy-start.8
  1630.3 4.3 copy-start.10
  1634.6 2.3 copy-start.11
Sparse Core Ops, SparseCore 0:
  10.2 1384.0 all-gather.2
  1468.0 162.3 all-gather.4
  1634.7 34.5 reduce-scatter.3
where the time goes:
time: 1680 us
  waiting for transfers between devices  1490 us (89%)
  blocking collectives  92.8 us (6%)
  starting transfers between devices  43.4 us (3%)
  matrix products  22.8 us (1%)
    all_gather x1, waiting for transfers between devices, per_device(): lax.all_gather(kv_weight, ('ctx', 'dp'), axis=0, tiled=True)  1380 us
    all_to_all x1, blocking collectives, per_device(): lax.all_to_all(local_rows, 'ctx', split_axis=1, concat_axis=0, tiled=True)  92.8 us
    all_gather x1, waiting for transfers between devices, per_device(): lax.all_gather(kv_grad, 'ctx', axis=0, tiled=True)  59.4 us
    ppermute x16, starting transfers between devices, passed_along(): return lax.ppermute(block, axis, route)  43.3 us
  transfers between devices with their start and end apart: 19, of which 10 were waited for; matrix products, arithmetic and copies ran while one was open for 2% of the time, Pallas kernels for 0%

commit v1 on v0

v1 whole, which is shorter than its diff:
```python
import jax
import jax.numpy as jnp
from jax import lax
from jax.sharding import Mesh, PartitionSpec as P

AXES = ("zh", "y", "core", "x", "zl")
CTX = ("zh", "y", "core")
DP = ("x", "zl")
TEAM = ("core", "x")
RING = ("zh", "y", "zl")


def exchanged(blocks, axes):
    return lax.all_to_all(blocks, axes, 0, 0, tiled=False)


def swapped(block):
    route = []
    for y in range(8):
        for x in range(4):
            hi, lo = divmod(y, 4)
            route.append((y * 4 + x, (hi * 4 + x) * 4 + lo))
    return lax.ppermute(block, ("y", "x"), route)


def shifted(block, hop):
    devices = range(64)
    return lax.ppermute(block, CTX, [(i, i + hop) for i in devices if i + hop in devices])


def doc_index(positions, doc_ends):
    return jnp.sum((positions[:, None] >= doc_ends[None, :]).astype(jnp.int32), axis=1)


def attention(queries, grads_out, keys, values, mask):
    scale = queries.shape[-1] ** -0.5
    mask3 = mask[:, None, :]
    scores = jnp.einsum("tgd,nd->tgn", queries, keys, preferred_element_type=jnp.float32) * scale
    top = jnp.max(jnp.where(mask3, scores, jnp.float32(-1e30)), axis=2, keepdims=True)
    weights = jnp.where(mask3, jnp.exp(scores - top), jnp.float32(0.0))
    total = jnp.sum(weights, axis=2, keepdims=True)
    attn = jnp.einsum("tgn,nd->tgd", weights.astype(jnp.bfloat16), values, preferred_element_type=jnp.float32)
    attn = (attn / total).astype(jnp.bfloat16)
    out_dot = jnp.sum(grads_out.astype(jnp.float32) * attn.astype(jnp.float32), axis=2, keepdims=True)
    probs = weights / total
    dprobs = jnp.einsum("tgd,nd->tgn", grads_out, values, preferred_element_type=jnp.float32)
    dscores = (probs * (dprobs - out_dot)).astype(jnp.bfloat16)
    grad_q = jnp.einsum("tgn,nd->tgd", dscores, keys, preferred_element_type=jnp.float32) * scale
    grad_k = jnp.einsum("tgn,tgd->nd", dscores, queries, preferred_element_type=jnp.float32) * scale
    grad_v = jnp.einsum("tgn,tgd->nd", probs.astype(jnp.bfloat16), grads_out, preferred_element_type=jnp.float32)
    return attn, grad_q.astype(jnp.bfloat16), jnp.concatenate([grad_k, grad_v], axis=1)


def per_device(tokens_in, queries_in, kv_weight, out_grad, doc_lengths):
    rows = tokens_in[0]
    count, features = rows.shape
    width = kv_weight.shape[1]
    head_dim = width // 2
    heads = queries_in.shape[2] // head_dim
    queries = queries_in[0].reshape(count, heads, head_dim)
    grads_out = out_grad[0].reshape(count, heads, head_dim)

    pieces = rows.reshape(count, 8, 4, 2, 128).transpose(3, 2, 0, 1, 4).reshape(8, count, features // 8)
    team_rows = exchanged(pieces, TEAM).reshape(8 * count, features // 8)
    held = swapped(kv_weight)
    weight = exchanged(jnp.broadcast_to(held[None], (64,) + held.shape), RING).reshape(features // 8, width)
    part = jnp.dot(team_rows, weight, preferred_element_type=jnp.float32)
    part = exchanged(part.astype(jnp.bfloat16).reshape(8, count, width), TEAM)
    kv = jnp.sum(part.astype(jnp.float32), axis=0).astype(jnp.bfloat16)

    doc_ends = jnp.cumsum(doc_lengths[0])
    first_pos = lax.axis_index(CTX) * count
    query_pos = first_pos + jnp.arange(count, dtype=jnp.int32)
    key_pos = first_pos - 4 * count + jnp.arange(5 * count, dtype=jnp.int32)
    mask = (
        (key_pos[None, :] >= 0)
        & (key_pos[None, :] <= query_pos[:, None])
        & (doc_index(key_pos, doc_ends)[None, :] == doc_index(query_pos, doc_ends)[:, None])
    )
    near = jnp.concatenate([shifted(kv, hop) for hop in (4, 3, 2, 1)] + [kv], axis=0)
    attn, query_grad, part_grad = attention(queries, grads_out, near[:, :head_dim], near[:, head_dim:], mask)
    kv_grad = part_grad[4 * count :]
    for hop in (1, 2, 3, 4):
        part = part_grad[(4 - hop) * count : (5 - hop) * count].astype(jnp.bfloat16)
        kv_grad = kv_grad + shifted(part, -hop).astype(jnp.float32)
    kv_grad = kv_grad.astype(jnp.bfloat16)

    team_grad = exchanged(jnp.broadcast_to(kv_grad[None], (8,) + kv_grad.shape), TEAM).reshape(8 * count, width)
    grad = lax.dot_general(team_rows, team_grad, (((0,), (0,)), ((), ())), preferred_element_type=jnp.float32)
    grad = exchanged(grad.astype(jnp.bfloat16).reshape(64, 16, width), RING)
    grad = jnp.sum(grad.astype(jnp.float32), axis=0)
    weight_grad = swapped(grad)
    shape = (1, count, heads * head_dim)
    return attn.reshape(shape), query_grad.reshape(shape), weight_grad


def solution(mesh):
    fine = Mesh(mesh.devices.reshape(4, 8, 2, 4, 2), AXES)
    return jax.shard_map(
        per_device,
        mesh=fine,
        in_specs=(P(DP, CTX, None), P(DP, CTX, None), P(AXES, None), P(DP, CTX, None), P(DP, None)),
        out_specs=(P(DP, CTX, None), P(DP, CTX, None), P(AXES, None)),
        check_vma=False,
    )
```

time: 1680 us -> 195 us (0.12)
  waiting for transfers between devices: 1490 us -> 54.1 us
  blocking collectives: 92.8 us -> 48.7 us
    all_gather x2 -> x0, waiting for transfers between devices: 1440 us -> none  [the longest x1 1380 us: per_device(): lax.all_gather(kv_weight, ('ctx', 'dp'), axis=0, tiled=True)]
    all_to_all x1 -> x2, blocking collectives: 92.8 us -> 48.7 us  [exchanged(): return lax.all_to_all(blocks, axes, 0, 0, tiled=False)]
    all_to_all x0 -> x3, waiting for transfers between devices: none -> 41.5 us  [exchanged(): return lax.all_to_all(blocks, axes, 0, 0, tiled=False)]
    unnamed x4 -> x0, waiting for transfers between devices: 31 us -> none
    all_to_all x0 -> x3, starting transfers between devices: none -> 26 us  [exchanged(): return lax.all_to_all(blocks, axes, 0, 0, tiled=False)]
    ppermute x16 -> x10, starting transfers between devices: 43.3 us -> 29.5 us  [the longest x8 17.6 us: shifted(): lax.ppermute(block, CTX, [(i, i + hop) for i in devices if i + hop in dev...]
  transfers between devices with their start and end apart: 19 -> 13, of which waited for: 10 -> 8; matrix products, arithmetic and copies ran while one was open for 2% -> 8% of each run, Pallas kernels for 0% -> 0%
where the time goes in v1:
time: 195 us; the launch traced here: 194 us
  starting transfers between devices  55.5 us (28%)
  waiting for transfers between devices  54.1 us (28%)
  blocking collectives  48.7 us (25%)
  local copies, waits for them, and re-layouts  17.6 us (9%)
  matrix products  16 us (8%)
    all_to_all x2, blocking collectives, exchanged(): return lax.all_to_all(blocks, axes, 0, 0, tiled=False)  48.7 us
    all_to_all x3, waiting for transfers between devices, exchanged(): return lax.all_to_all(blocks, axes, 0, 0, tiled=False)  41.5 us
    all_to_all x3, starting transfers between devices, exchanged(): return lax.all_to_all(blocks, axes, 0, 0, tiled=False)  26 us
    ppermute x8, starting transfers between devices, shifted(): lax.ppermute(block, CTX, [(i, i + hop) for i in devices if i + hop in dev...  17.6 us
    ppermute x2, starting transfers between devices, swapped(): return lax.ppermute(block, ('y', 'x'), route)  11.9 us
    ppermute x8, waiting for transfers between devices, shifted(): lax.ppermute(block, CTX, [(i, i + hop) for i in devices if i + hop in dev...  8.35 us
    another operation x2, local copies, waits for them, and re-layouts, per_device(): rows.reshape(count, 8, 4, 2, 128).transpose(3, 2, 0, 1, 4)  6.3 us
    unnamed x24, local copies, waits for them, and re-layouts  5.66 us
  transfers between devices with their start and end apart: 13, of which 8 were waited for; matrix products, arithmetic and copies ran while one was open for 8% of the time, Pallas kernels for 0%

profile of v1, /device:TPU:6, one launch (start us, length us, event | category | flops | bytes accessed | tf_op | source)
XLA Modules:
  0.0 193.8 jit_solution(11235572774001283733)
XLA Ops:
  0.6 5.4 %collective-permute-start = (bf16[16,256]{1,0:T(8,128)(2,1)}, bf16[16,256]{1,0:T(8,128)(2,1)S(1)}, u32[]{:S(2)}, u32[]{:S(2)}) collective-permute-start(bf16[16,256]{1,0:T(8,128)(2,1)} %param.7), channel_id=1, source_target_pairs={{0,0},{2,16},{4,32},{6,48},{16,2},{18,18},{20,34},{22,50},{32,4},{... | collective-permute-start | bytes 24584 | tf_op jit(solution)/shard_map/ppermute | solution.py:23
  6.1 4.2 %collective-permute-done = bf16[16,256]{1,0:T(8,128)(2,1)S(1)} collective-permute-done((bf16[16,256]{1,0:T(8,128)(2,1)}, bf16[16,256]{1,0:T(8,128)(2,1)S(1)}, u32[]{:S(2)}, u32[]{:S(2)}) %collective-permute-start) | collective-permute-done | bytes 8224 | tf_op jit(solution)/shard_map/ppermute | solution.py:23
  11.1 16.6 %all-to-all-start.1 = ((bf16[64,16,256]{2,1,0:T(8,128)(2,1)}), bf16[64,16,256]{2,1,0:T(8,128)(2,1)S(1)}, u32[]{:S(2)}, u32[]{:S(2)}) async-start(bf16[64,16,256]{2,1,0:T(8,128)(2,1)} %broadcast_in_dim.23), calls=%async_computation.1 | async-start | bytes 1048576 | tf_op jit(solution)/shard_map/all_to_all | solution.py:14
  27.7 4.4 %reshape_squeeze.9 = bf16[128,8,4,2,128]{4,3,2,1,0:T(2,128)(2,1)} reshape(bf16[1,128,8192]{2,1,0:T(8,128)(2,1)} %param.5) | data formatting | bytes 4194304 | tf_op jit(solution)/shard_map/reshape;squeeze | solution.py:63
  32.2 1.9 copy.63
  34.0 2.3 %reshape.134 = bf16[8,128,1024]{2,1,0:T(8,128)(2,1)} reshape(bf16[2,4,128,8,128]{4,3,2,1,0:T(8,128)(2,1)S(1)} %bitcast.78) | data formatting | bytes 4194304 | tf_op jit(solution)/shard_map/reshape | solution.py:63
  36.3 8.5 %all-to-all-done.1 = bf16[64,16,256]{2,1,0:T(8,128)(2,1)S(1)} async-done(((bf16[64,16,256]{2,1,0:T(8,128)(2,1)}), bf16[64,16,256]{2,1,0:T(8,128)(2,1)S(1)}, u32[]{:S(2)}, u32[]{:S(2)}) %all-to-all-start.1) | async-done | bytes 524320 | tf_op jit(solution)/shard_map/all_to_all | solution.py:14
  44.9 4.5 %all-to-all-start = ((bf16[8,128,1024]{2,1,0:T(8,128)(2,1)}), bf16[8,128,1024]{2,1,0:T(8,128)(2,1)S(1)}, u32[]{:S(2)}, u32[]{:S(2)}) async-start(bf16[8,128,1024]{2,1,0:T(8,128)(2,1)} %reshape.134), calls=%async_computation | async-start | bytes 4194304 | tf_op jit(solution)/shard_map/all_to_all | solution.py:14
  49.4 25.1 %all-to-all-done = bf16[8,128,1024]{2,1,0:T(8,128)(2,1)S(1)} async-done(((bf16[8,128,1024]{2,1,0:T(8,128)(2,1)}), bf16[8,128,1024]{2,1,0:T(8,128)(2,1)S(1)}, u32[]{:S(2)}, u32[]{:S(2)}) %all-to-all-start) | async-done | bytes 2097184 | tf_op jit(solution)/shard_map/all_to_all | solution.py:14
  74.5 1.5 convolution_convert_fusion
  76.0 4.9 %all-to-all-start.2 = ((bf16[8,128,256]{2,1,0:T(8,128)(2,1)}), bf16[8,128,256]{2,1,0:T(8,128)(2,1)S(1)}, u32[]{:S(2)}, u32[]{:S(2)}) async-start(bf16[8,128,256]{2,1,0:T(8,128)(2,1)} %bitcast.88), calls=%async_computation.2 | async-start | bytes 1048576 | tf_op jit(solution)/shard_map/all_to_all | solution.py:14
  81.4 7.8 %all-to-all-done.2 = bf16[8,128,256]{2,1,0:T(8,128)(2,1)S(1)} async-done(((bf16[8,128,256]{2,1,0:T(8,128)(2,1)}), bf16[8,128,256]{2,1,0:T(8,128)(2,1)S(1)}, u32[]{:S(2)}, u32[]{:S(2)}) %all-to-all-start.2) | async-done | bytes 524320 | tf_op jit(solution)/shard_map/all_to_all | solution.py:14
  89.3 4.2 %collective-permute-start.1 = (bf16[128,256]{1,0:T(8,128)(2,1)S(1)}, bf16[128,256]{1,0:T(8,128)(2,1)S(1)}, u32[]{:S(2)}, u32[]{:S(2)}) collective-permute-start(bf16[128,256]{1,0:T(8,128)(2,1)S(1)} %reduce_sum.59), channel_id=1, source_target_pairs={{0,32},{8,40},{16,48},{24,56},{32,64},{40,72},{48,80},{56,88},{64,... | collective-permute-start | bytes 196616 | tf_op jit(solution)/shard_map/ppermute | solution.py:28
  94.1 1.5 copy.42
  95.7 1.3 collective-permute-start.4
  97.0 3.8 %collective-permute-start.3 = (bf16[128,256]{1,0:T(8,128)(2,1)S(1)}, bf16[128,256]{1,0:T(8,128)(2,1)S(1)}, u32[]{:S(2)}, u32[]{:S(2)}) collective-permute-start(bf16[128,256]{1,0:T(8,128)(2,1)S(1)} %reduce_sum.59), channel_id=1, source_target_pairs={{0,16},{8,24},{16,32},{24,40},{32,48},{40,56},{48,64},{56,72},{64,... | collective-permute-start | bytes 196616 | tf_op jit(solution)/shard_map/ppermute | solution.py:28
  100.7 3.1 %collective-permute-start.2 = (bf16[128,256]{1,0:T(8,128)(2,1)S(1)}, bf16[128,256]{1,0:T(8,128)(2,1)S(1)}, u32[]{:S(2)}, u32[]{:S(2)}) collective-permute-start(bf16[128,256]{1,0:T(8,128)(2,1)S(1)} %reduce_sum.59), channel_id=1, source_target_pairs={{0,24},{8,32},{16,40},{24,48},{32,56},{40,64},{48,72},{56,80},{64,... | collective-permute-start | bytes 196616 | tf_op jit(solution)/shard_map/ppermute | solution.py:28
  103.9 1.9 collective-permute-done.2
  105.8 4.3 %fusion.39 = (f32[128,16]{0,1:T(8,128)S(1)}, f32[128,16,640]{0,2,1:T(8,128)}) fusion(pred[128,640]{0,1:T(8,128)(4,1)S(1)} %compare_and_fusion, bf16[128,16,128]{0,2,1:T(8,128)(2,1)S(1)} %bitcast.80, bf16[640,256]{1,0:T(8,128)(2,1)S(1)} %constant_dynamic-update-slice_fusion), kind=kOutput, calls=%fused_computation.59 | convolution fusion | flops 678953600 | bytes 6791168 | tf_op jit(solution)/shard_map/sub | solution.py:40
  110.2 3.6 %fusion.23 = f32[640,128]{0,1:T(8,128)S(1)} fusion(bf16[128,16,128]{0,2,1:T(8,128)(2,1)S(1)} %bitcast.82, f32[128,16,640]{0,2,1:T(8,128)} %get-tuple-element.17, f32[128,16]{0,1:T(8,128)S(1)} %get-tuple-element.16), kind=kOutput, calls=%fused_computation.28 | convolution fusion | flops 338165760 | bytes 6103040 | tf_op jit(solution)/shard_map/tgn,tgd->nd/dot_general | solution.py:50
  114.9 2.0 %fusion.1 = bf16[128,16,640]{0,2,1:T(8,128)(2,1)S(1)} fusion(f32[128,16]{0,1:T(8,128)S(1)} %get-tuple-element.18, bf16[128,16,128]{0,2,1:T(8,128)(2,1)} %bitcast.84, f32[128,16,640]{0,2,1:T(8,128)S(1)} %copy-done, f32[128,16]{0,1:T(8,128)S(1)} %get-tuple-element.16, bf16[640,256]{1,0:T(8,128)(2,1)S(1)} %constant_dynamic-update-slice_fusion), kind=kOutput, calls=%fused_computation.2 | convolution fusion | flops 340787200 | bytes 8568832 | tf_op jit(solution)/shard_map/tgd,nd->tgn/dot_general | solution.py:46
  118.0 1.3 collective-permute-start.5
  119.3 1.3 collective-permute-start.8
  120.6 1.3 collective-permute-start.7
  123.2 4.9 %collective-permute-done.8 = bf16[128,256]{0,1:T(8,128)(2,1)S(1)} collective-permute-done((bf16[128,256]{0,1:T(8,128)(2,1)S(1)}, bf16[128,256]{0,1:T(8,128)(2,1)S(1)}, u32[]{:S(2)}, u32[]{:S(2)}) %collective-permute-start.8) | collective-permute-done | bytes 65568 | tf_op jit(solution)/shard_map/ppermute | solution.py:28
  129.8 13.1 %all_to_all.25 = bf16[8,128,256]{1,2,0:T(8,128)(2,1)S(1)} all-to-all(bf16[8,128,256]{1,2,0:T(8,128)(2,1)S(1)} %broadcast_in_dim.26), channel_id=1, replica_groups=mesh['zh'=4,'y'=8,'core'=2,'x'=4,'zl'=2] {'core','x'}, dimensions={0} | all-to-all | bytes 1048576 | tf_op jit(solution)/shard_map/all_to_all | solution.py:14
  143.0 1.5 fusion.21
  144.5 2.0 %copy.49 = bf16[1024,256]{1,0:T(8,128)(2,1)} copy(bf16[1024,256]{0,1:T(8,128)(2,1)} %fusion.21) | data formatting | bytes 1048576 | tf_op jit(solution)/shard_map/convert_element_type | solution.py:90
  146.5 35.6 %all_to_all.26 = bf16[64,16,256]{2,1,0:T(8,128)(2,1)S(1)} all-to-all(bf16[64,16,256]{2,1,0:T(8,128)(2,1)} %bitcast.86), channel_id=1, replica_groups=mesh['zh'=4,'y'=8,'core'=2,'x'=4,'zl'=2] {'zh','y','zl'}, dimensions={0} | all-to-all | bytes 1048576 | tf_op jit(solution)/shard_map/all_to_all | solution.py:14
  182.2 6.5 %collective-permute-start.9 = (f32[16,256]{1,0:T(8,128)S(1)}, f32[16,256]{1,0:T(8,128)S(1)}, u32[]{:S(2)}, u32[]{:S(2)}) collective-permute-start(f32[16,256]{1,0:T(8,128)S(1)} %convert_reduce_fusion), channel_id=1, source_target_pairs={{0,0},{2,16},{4,32},{6,48},{16,2},{18,18},{20,34},{22,50},{32,4},{... | collective-permute-start | bytes 49160 | tf_op jit(solution)/shard_map/ppermute | solution.py:23
  188.7 1.4 fusion.20
  190.1 2.0 %copy.51 = bf16[1,128,2048]{2,1,0:T(8,128)(2,1)} copy(bf16[1,128,2048]{1,2,0:T(8,128)(2,1)} %bitcast.89) | data formatting | bytes 1048576
  (50 shorter events, 8.9 us)
Async XLA Ops:
  0.6 9.7 %collective-permute-start = (bf16[16,256]{1,0:T(8,128)(2,1)}, bf16[16,256]{1,0:T(8,128)(2,1)S(1)}, u32[]{:S(2)}, u32[]{:S(2)}) collective-permute-start(bf16[16,256]{1,0:T(8,128)(2,1)} %param.7), channel_id=1, source_target_pairs={{0,0},{2,16},{4,32},{6,48},{16,2},{18,18},{20,34},{22,50},{32,4},{... | collective-permute-start | bytes 24584 | tf_op jit(solution)/shard_map/ppermute | solution.py:23
  11.1 33.8 %all-to-all-start.1 = ((bf16[64,16,256]{2,1,0:T(8,128)(2,1)}), bf16[64,16,256]{2,1,0:T(8,128)(2,1)S(1)}, u32[]{:S(2)}, u32[]{:S(2)}) async-start(bf16[64,16,256]{2,1,0:T(8,128)(2,1)} %broadcast_in_dim.23), calls=%async_computation.1 | async-start | bytes 1048576 | tf_op jit(solution)/shard_map/all_to_all | solution.py:14
  36.3 44.6 %copy-start.7 = (s32[1,32]{1,0:T(1,128)S(1)}, s32[1,32]{1,0:T(1,128)}, u32[]{:S(2)}) copy-start(s32[1,32]{1,0:T(1,128)} %param.9) | copy-start | bytes 388
  36.3 57.5 %copy-start.6 = (bf16[1,128,2048]{2,1,0:T(8,128)(2,1)S(1)}, bf16[1,128,2048]{2,1,0:T(8,128)(2,1)}, u32[]{:S(2)}) copy-start(bf16[1,128,2048]{2,1,0:T(8,128)(2,1)} %param.6) | copy-start | bytes 1572868
  44.9 29.6 %all-to-all-start = ((bf16[8,128,1024]{2,1,0:T(8,128)(2,1)}), bf16[8,128,1024]{2,1,0:T(8,128)(2,1)S(1)}, u32[]{:S(2)}, u32[]{:S(2)}) async-start(bf16[8,128,1024]{2,1,0:T(8,128)(2,1)} %reshape.134), calls=%async_computation | async-start | bytes 4194304 | tf_op jit(solution)/shard_map/all_to_all | solution.py:14
  74.5 19.0 %copy-start.4 = (bf16[8,128,1024]{2,1,0:T(8,128)(2,1)}, bf16[8,128,1024]{2,1,0:T(8,128)(2,1)S(1)}, u32[]{:S(2)}) copy-start(bf16[8,128,1024]{2,1,0:T(8,128)(2,1)S(1)} %all-to-all-done) | copy-start | bytes 6291460
  76.0 13.1 %all-to-all-start.2 = ((bf16[8,128,256]{2,1,0:T(8,128)(2,1)}), bf16[8,128,256]{2,1,0:T(8,128)(2,1)S(1)}, u32[]{:S(2)}, u32[]{:S(2)}) async-start(bf16[8,128,256]{2,1,0:T(8,128)(2,1)} %bitcast.88), calls=%async_computation.2 | async-start | bytes 1048576 | tf_op jit(solution)/shard_map/all_to_all | solution.py:14
  89.3 14.6 %collective-permute-start.1 = (bf16[128,256]{1,0:T(8,128)(2,1)S(1)}, bf16[128,256]{1,0:T(8,128)(2,1)S(1)}, u32[]{:S(2)}, u32[]{:S(2)}) collective-permute-start(bf16[128,256]{1,0:T(8,128)(2,1)S(1)} %reduce_sum.59), channel_id=1, source_target_pairs={{0,32},{8,40},{16,48},{24,56},{32,64},{40,72},{48,80},{56,88},{64,... | collective-permute-start | bytes 196616 | tf_op jit(solution)/shard_map/ppermute | solution.py:28
  94.1 16.0 %copy-start.1 = (bf16[1,128,2048]{1,2,0:T(8,128)(2,1)}, bf16[1,128,2048]{1,2,0:T(8,128)(2,1)S(1)}, u32[]{:S(2)}) copy-start(bf16[1,128,2048]{1,2,0:T(8,128)(2,1)S(1)} %copy.61) | copy-start | bytes 1572868
  95.7 18.1 %copy-start.3 = (bf16[1,128,2048]{1,2,0:T(8,128)(2,1)}, bf16[1,128,2048]{1,2,0:T(8,128)(2,1)S(1)}, u32[]{:S(2)}) copy-start(bf16[1,128,2048]{1,2,0:T(8,128)(2,1)S(1)} %copy.42) | copy-start | bytes 1572868
  95.7 10.1 %collective-permute-start.4 = (bf16[128,256]{1,0:T(8,128)(2,1)S(1)}, bf16[128,256]{1,0:T(8,128)(2,1)S(1)}, u32[]{:S(2)}, u32[]{:S(2)}) collective-permute-start(bf16[128,256]{1,0:T(8,128)(2,1)S(1)} %reduce_sum.59), channel_id=1, source_target_pairs={{0,8},{8,16},{16,24},{24,32},{32,40},{40,48},{48,56},{56,64},{64,7... | collective-permute-start | bytes 196616 | tf_op jit(solution)/shard_map/ppermute | solution.py:28
  97.0 8.8 %collective-permute-start.3 = (bf16[128,256]{1,0:T(8,128)(2,1)S(1)}, bf16[128,256]{1,0:T(8,128)(2,1)S(1)}, u32[]{:S(2)}, u32[]{:S(2)}) collective-permute-start(bf16[128,256]{1,0:T(8,128)(2,1)S(1)} %reduce_sum.59), channel_id=1, source_target_pairs={{0,16},{8,24},{16,32},{24,40},{32,48},{40,56},{48,64},{56,72},{64,... | collective-permute-start | bytes 196616 | tf_op jit(solution)/shard_map/ppermute | solution.py:28
  100.7 5.0 %collective-permute-start.2 = (bf16[128,256]{1,0:T(8,128)(2,1)S(1)}, bf16[128,256]{1,0:T(8,128)(2,1)S(1)}, u32[]{:S(2)}, u32[]{:S(2)}) collective-permute-start(bf16[128,256]{1,0:T(8,128)(2,1)S(1)} %reduce_sum.59), channel_id=1, source_target_pairs={{0,24},{8,32},{16,40},{24,48},{32,56},{40,64},{48,72},{56,80},{64,... | collective-permute-start | bytes 196616 | tf_op jit(solution)/shard_map/ppermute | solution.py:28
  110.2 4.0 %copy-start = (f32[128,16,640]{0,2,1:T(8,128)S(1)}, f32[128,16,640]{0,2,1:T(8,128)}, u32[]{:S(2)}) copy-start(f32[128,16,640]{0,2,1:T(8,128)} %get-tuple-element.17) | copy-start | bytes 15728644
  114.9 2.1 %copy-start.2 = (bf16[1,128,2048]{1,2,0:T(8,128)(2,1)S(1)}, bf16[1,128,2048]{1,2,0:T(8,128)(2,1)}, u32[]{:S(2)}) copy-start(bf16[1,128,2048]{1,2,0:T(8,128)(2,1)} %copy-done.1) | copy-start | bytes 1572868
  117.0 26.0 %copy-start.5 = (bf16[8,128,1024]{2,1,0:T(8,128)(2,1)S(1)}, bf16[8,128,1024]{2,1,0:T(8,128)(2,1)}, u32[]{:S(2)}) copy-start(bf16[8,128,1024]{2,1,0:T(8,128)(2,1)} %copy-done.4) | copy-start | bytes 6291460
  118.0 5.2 %collective-permute-start.5 = (bf16[128,256]{0,1:T(8,128)(2,1)S(1)}, bf16[128,256]{0,1:T(8,128)(2,1)S(1)}, u32[]{:S(2)}, u32[]{:S(2)}) collective-permute-start(bf16[128,256]{0,1:T(8,128)(2,1)S(1)} %get-tuple-element.12), channel_id=1, source_target_pairs={{8,0},{16,8},{24,16},{32,24},{40,32},{48,40},{56,48},{64,56},{72,6... | collective-permute-start | bytes 196616 | tf_op jit(solution)/shard_map/ppermute | solution.py:28
  119.3 8.8 %collective-permute-start.8 = (bf16[128,256]{0,1:T(8,128)(2,1)S(1)}, bf16[128,256]{0,1:T(8,128)(2,1)S(1)}, u32[]{:S(2)}, u32[]{:S(2)}) collective-permute-start(bf16[128,256]{0,1:T(8,128)(2,1)S(1)} %get-tuple-element.13), channel_id=1, source_target_pairs={{32,0},{40,8},{48,16},{56,24},{64,32},{72,40},{80,48},{88,56},{96,... | collective-permute-start | bytes 196616 | tf_op jit(solution)/shard_map/ppermute | solution.py:28
  120.6 8.7 %collective-permute-start.7 = (bf16[128,256]{0,1:T(8,128)(2,1)S(1)}, bf16[128,256]{0,1:T(8,128)(2,1)S(1)}, u32[]{:S(2)}, u32[]{:S(2)}) collective-permute-start(bf16[128,256]{0,1:T(8,128)(2,1)S(1)} %get-tuple-element.14), channel_id=1, source_target_pairs={{24,0},{32,8},{40,16},{48,24},{56,32},{64,40},{72,48},{80,56},{88,... | collective-permute-start | bytes 196616 | tf_op jit(solution)/shard_map/ppermute | solution.py:28
  121.9 7.8 %collective-permute-start.6 = (bf16[128,256]{0,1:T(8,128)(2,1)S(1)}, bf16[128,256]{0,1:T(8,128)(2,1)S(1)}, u32[]{:S(2)}, u32[]{:S(2)}) collective-permute-start(bf16[128,256]{0,1:T(8,128)(2,1)S(1)} %get-tuple-element.15), channel_id=1, source_target_pairs={{16,0},{24,8},{32,16},{40,24},{48,32},{56,40},{64,48},{72,56},{80,... | collective-permute-start | bytes 196616 | tf_op jit(solution)/shard_map/ppermute | solution.py:28
  182.2 11.0 %collective-permute-start.9 = (f32[16,256]{1,0:T(8,128)S(1)}, f32[16,256]{1,0:T(8,128)S(1)}, u32[]{:S(2)}, u32[]{:S(2)}) collective-permute-start(f32[16,256]{1,0:T(8,128)S(1)} %convert_reduce_fusion), channel_id=1, source_target_pairs={{0,0},{2,16},{4,32},{6,48},{16,2},{18,18},{20,34},{22,50},{32,4},{... | collective-permute-start | bytes 49160 | tf_op jit(solution)/shard_map/ppermute | solution.py:23

commit v2 on v1

v2 whole, which is shorter than its diff:
```python
import jax
import jax.numpy as jnp
from jax import lax
from jax.experimental import pallas as pl
from jax.experimental.pallas import tpu as pltpu
from jax.sharding import Mesh, PartitionSpec as P

AXES = ("zh", "y", "core", "x", "zl")
CTX = ("zh", "y", "core")
DP = ("x", "zl")
TEAM = ("core", "x")
RING = ("zh", "y", "zl")
ZH, Y, CORE, X, ZL = 4, 8, 2, 4, 2
MEMBERS = CORE * X
CHIPS = ZH * Y
COUNT = 128
HEAD = 128
WIDTH = 2 * HEAD
BF16, F32 = jnp.bfloat16, jnp.float32
VMEM_LIMIT = 40 << 20


def vmem():
    return pl.BlockSpec(memory_space=pltpu.VMEM)


def smem():
    return pl.BlockSpec(memory_space=pltpu.SMEM)


def params():
    return pltpu.CompilerParams(vmem_limit_bytes=VMEM_LIMIT)


def exchanged(blocks, axes):
    return lax.all_to_all(blocks, axes, 0, 0, tiled=False)


def target(core, x, step):
    return (core + step // X) % CORE, (x + step) % X


def source(core, x, step):
    return (core + step // X) % CORE, (x + X - step % X) % X


def to_team(piece, step):
    route = []
    for core in range(CORE):
        for x in range(X):
            to_core, to_x = target(core, x, step)
            route.append((core * X + x, to_core * X + to_x))
    return lax.ppermute(piece, TEAM, route)


def to_chip(block, hop):
    chips = range(CHIPS)
    return lax.ppermute(block, ("zh", "y"), [(i, i + hop) for i in chips if i + hop in chips])


def to_other_core(block):
    return lax.ppermute(block, "core", [(0, 1), (1, 0)])


def pieces_kernel(place, rows, *outs):
    group = pl.program_id(0)
    core, x = place[0], place[1]
    span = 32 * X
    for c in range(CORE):
        tiles = [rows[:, (b * CORE + c) * span : (b * CORE + c + 1) * span] for b in range(4)]
        for j in range(X):
            tile = jnp.concatenate([t[:, j * 32 : (j + 1) * 32] for t in tiles], axis=1)
            for step in range(MEMBERS):
                to_core, to_x = target(core, x, step)

                @pl.when((to_core == c) & (to_x == j))
                def _(step=step, tile=tile):
                    outs[step][...] = tile


def make_pieces(place, rows):
    features = rows.shape[1]
    groups = features // 1024
    return pl.pallas_call(
        pieces_kernel,
        grid_spec=pltpu.PrefetchScalarGridSpec(
            num_scalar_prefetch=1,
            grid=(groups,),
            in_specs=[pl.BlockSpec((COUNT, 1024), lambda i, s: (0, i))],
            out_specs=[pl.BlockSpec((COUNT, 128), lambda i, s: (0, i))] * MEMBERS,
        ),
        out_shape=[jax.ShapeDtypeStruct((COUNT, features // MEMBERS), BF16)] * MEMBERS,
        compiler_params=params(),
        cost_estimate=pl.CostEstimate(flops=0, bytes_accessed=4 << 20, transcendentals=0),
        name="pieces",
    )(place, rows)


def project_kernel(place, weight, *refs):
    pieces, out = refs[:MEMBERS], refs[MEMBERS]
    for step in range(MEMBERS):
        core, x = source(place[0], place[1], step)
        part = jnp.dot(pieces[step][...], weight[...], preferred_element_type=F32)
        out[core * X + x] = part.astype(BF16)


def project(place, weight, pieces):
    return pl.pallas_call(
        project_kernel,
        in_specs=[smem()] + [vmem()] * (1 + MEMBERS),
        out_specs=vmem(),
        out_shape=jax.ShapeDtypeStruct((MEMBERS, COUNT, WIDTH), BF16),
        compiler_params=params(),
        cost_estimate=pl.CostEstimate(flops=1 << 29, bytes_accessed=3 << 20, transcendentals=0),
        name="project",
    )(place, weight, *pieces)


def weight_grad_kernel(place, grads, *refs):
    pieces, out, total = refs[:MEMBERS], refs[MEMBERS], refs[MEMBERS + 1]
    turned, rows = [], []
    for step in range(MEMBERS):
        core, x = source(place[0], place[1], step)
        turned.append(grads[core * X + x].T)
        rows.append(pieces[step][...])
    total[...] = jnp.dot(
        jnp.concatenate(turned, axis=1), jnp.concatenate(rows, axis=0), preferred_element_type=F32
    )
    for chip in range(CHIPS):
        zh, y = divmod(chip, Y)
        if chip % 4 == 0:
            block = total[:, chip * 32 : chip * 32 + 128].T.astype(BF16)
        out[y, zh] = block[chip % 4 * 32 : chip % 4 * 32 + 32]


def weight_grad_parts(place, grads, pieces):
    features = pieces[0].shape[1]
    return pl.pallas_call(
        weight_grad_kernel,
        in_specs=[smem()] + [vmem()] * (1 + MEMBERS),
        out_specs=vmem(),
        out_shape=jax.ShapeDtypeStruct((Y, ZH, 32, WIDTH), BF16),
        scratch_shapes=[pltpu.VMEM((WIDTH, features), F32)],
        compiler_params=params(),
        cost_estimate=pl.CostEstimate(flops=1 << 29, bytes_accessed=3 << 20, transcendentals=0),
        name="weight_grad",
    )(place, grads, *pieces)


def attention_kernel(place, lengths, queries, grads, own, near, far, other, attn, grad_q, grad_own, grad_other):
    core, chip_pos = place[0], place[1]
    scale = HEAD ** -0.5
    blocks = [own[...], near[...], far[...], other[1 - core], other[2 - core]]
    starts = [chip_pos + core * COUNT - 2 * COUNT * i for i in range(3)]
    starts += [chip_pos + (1 - core) * COUNT - 2 * COUNT * (1 - core + i) for i in range(2)]
    keys = jnp.concatenate([b[:, :HEAD] for b in blocks], axis=0)
    values = jnp.concatenate([b[:, HEAD:] for b in blocks], axis=0)
    keys_t, values_t = keys.T, values.T

    query_pos = starts[0] + lax.broadcasted_iota(jnp.int32, (1, COUNT), 1)
    doc_start = jnp.zeros((1, COUNT), jnp.int32)
    end = jnp.int32(0)
    for doc in range(lengths.shape[1]):
        end = end + lengths[0, doc]
        doc_start = jnp.where(query_pos >= end, end, doc_start)
    row = lax.broadcasted_iota(jnp.int32, (COUNT, COUNT), 0)
    masks = []
    for start in starts:
        key_pos = start + row
        masks.append((key_pos >= doc_start) & (key_pos <= query_pos))
    mask = jnp.concatenate(masks, axis=0)
    mask = jnp.concatenate([mask, mask], axis=1)

    nt = (((1,), (1,)), ((), ()))
    total_k = total_v = None
    for pair in range(queries.shape[1] // WIDTH):
        cols = [slice((2 * pair + i) * HEAD, (2 * pair + i + 1) * HEAD) for i in range(2)]
        q = jnp.concatenate([queries[:, c] for c in cols], axis=0)
        g = jnp.concatenate([grads[:, c] for c in cols], axis=0)
        scores = lax.dot_general(keys, q, nt, preferred_element_type=F32) * scale
        scores = jnp.where(mask, scores, F32(-1e30))
        top = jnp.max(scores, axis=0, keepdims=True)
        weights = jnp.where(mask, jnp.exp(scores - top), F32(0.0))
        inverse = 1.0 / jnp.sum(weights, axis=0, keepdims=True)
        out = jnp.dot(values_t, weights.astype(BF16), preferred_element_type=F32) * inverse
        dprobs = lax.dot_general(values, g, nt, preferred_element_type=F32)
        probs = weights * inverse
        out_dot = jnp.sum(probs * dprobs, axis=0, keepdims=True)
        dscores = (probs * (dprobs - out_dot)).astype(BF16)
        dq = jnp.dot(keys_t, dscores, preferred_element_type=F32) * scale
        out, dq = out.T.astype(BF16), dq.T.astype(BF16)
        for i in range(2):
            attn[:, cols[i]] = out[i * COUNT : (i + 1) * COUNT]
            grad_q[:, cols[i]] = dq[i * COUNT : (i + 1) * COUNT]
        part_k = jnp.dot(dscores, q, preferred_element_type=F32)
        part_v = jnp.dot(probs.astype(BF16), g, preferred_element_type=F32)
        total_k = part_k if pair == 0 else total_k + part_k
        total_v = part_v if pair == 0 else total_v + part_v
    total = jnp.concatenate([total_k * scale, total_v], axis=1)
    for i in range(3):
        grad_own[i] = total[i * COUNT : (i + 1) * COUNT]
    for i in range(2):
        grad_other[i] = total[(3 + i) * COUNT : (4 + i) * COUNT].astype(BF16)


def attention(place, lengths, queries, grads, own, near, far, other):
    shape = jax.ShapeDtypeStruct(queries.shape, BF16)
    return pl.pallas_call(
        attention_kernel,
        in_specs=[smem(), smem()] + [vmem()] * 6,
        out_specs=[vmem()] * 4,
        out_shape=[
            shape,
            shape,
            jax.ShapeDtypeStruct((3, COUNT, WIDTH), F32),
            jax.ShapeDtypeStruct((2, COUNT, WIDTH), BF16),
        ],
        compiler_params=params(),
        cost_estimate=pl.CostEstimate(flops=2 << 30, bytes_accessed=3 << 20, transcendentals=5 << 18),
        name="attention",
    )(place, lengths, queries, grads, own, near, far, other)


def per_device(tokens_in, queries_in, kv_weight, out_grad, doc_lengths):
    core = lax.axis_index("core")
    chip = lax.axis_index(("zh", "y"))
    team_place = jnp.stack([core, lax.axis_index("x")]).astype(jnp.int32)
    ctx_place = jnp.stack([core, chip * (CORE * COUNT)]).astype(jnp.int32)
    ring = ZH * Y * ZL

    weight = exchanged(jnp.broadcast_to(kv_weight[None], (ring,) + kv_weight.shape), RING)
    weight = weight.reshape(ring * kv_weight.shape[0], WIDTH)
    pieces = make_pieces(team_place, tokens_in[0])
    pieces = [pieces[0]] + [to_team(pieces[step], step) for step in range(1, MEMBERS)]
    part = exchanged(project(team_place, weight, pieces), TEAM)
    kv = jnp.sum(part.astype(F32), axis=0).astype(BF16)

    near, far = to_chip(kv, 1), to_chip(kv, 2)
    other = to_other_core(jnp.stack([kv, near, far]))
    attn, query_grad, grad_own, grad_other = attention(
        ctx_place, doc_lengths, queries_in[0], out_grad[0], kv, near, far, other
    )

    back = to_other_core(grad_other).astype(F32)
    first = core == 0
    far_grad = grad_own[2] + jnp.where(first, F32(0.0), back[1])
    near_grad = grad_own[1] + jnp.where(first, back[1], back[0])
    own_grad = grad_own[0] + jnp.where(first, back[0], F32(0.0))
    far_grad, near_grad = to_chip(far_grad.astype(BF16), -2), to_chip(near_grad.astype(BF16), -1)
    kv_grad = (own_grad + near_grad.astype(F32) + far_grad.astype(F32)).astype(BF16)

    team_grad = exchanged(jnp.broadcast_to(kv_grad[None], (MEMBERS,) + kv_grad.shape), TEAM)
    parts = weight_grad_parts(team_place, team_grad, pieces)
    parts = jnp.sum(exchanged(parts, "y").astype(F32), axis=0).astype(BF16)
    parts = exchanged(parts.reshape(ZH * ZL, 16, WIDTH), ("zh", "zl"))
    weight_grad = jnp.sum(parts.astype(F32), axis=0)
    return attn[None], query_grad[None], weight_grad


def solution(mesh):
    fine = Mesh(mesh.devices.reshape(ZH, Y, CORE, X, ZL), AXES)
    return jax.shard_map(
        per_device,
        mesh=fine,
        in_specs=(P(DP, CTX, None), P(DP, CTX, None), P(AXES, None), P(DP, CTX, None), P(DP, None)),
        out_specs=(P(DP, CTX, None), P(DP, CTX, None), P(AXES, None)),
        check_vma=False,
    )
```

time: 195 us -> 175 us (0.90)
  waiting for transfers between devices: 54.1 us -> 26.5 us
  Pallas kernels: 0 us -> 23 us
  matrix products: 16 us -> 0 us
  blocking collectives: 48.7 us -> 64.4 us
  local copies, waits for them, and re-layouts: 17.6 us -> 4.2 us
  starting transfers between devices: 55.5 us -> 51.7 us
    all_to_all x3 -> x1, waiting for transfers between devices: 41.5 us -> 0.01 us  [exchanged(): return lax.all_to_all(blocks, axes, 0, 0, tiled=False)]
    pallas_call x0 -> x4, Pallas kernels: none -> 23 us  [the longest x1 10.7 us: attention(): pl.pallas_call(attention_kernel, in_specs=[smem(), smem()] + [vmem()] * 6...]
    all_to_all x2 -> x4, blocking collectives: 48.7 us -> 64.4 us  [exchanged(): return lax.all_to_all(blocks, axes, 0, 0, tiled=False)]
    ppermute x10 -> x13, waiting for transfers between devices: 12.6 us -> 26.5 us  [the longest x7 12.6 us: to_team(): return lax.ppermute(piece, TEAM, route)]
    dot_general x7 -> x0, matrix products: 11.7 us -> none  [the longest x1 3.57 us: attention(): jnp.einsum('tgn,tgd->nd', probs.astype(jnp.bfloat16), grads_out, preferre...]
    all_to_all x3 -> x1, starting transfers between devices: 26 us -> 16.6 us  [exchanged(): return lax.all_to_all(blocks, axes, 0, 0, tiled=False)]
    another operation x4 -> x0, local copies, waits for them, and re-layouts: 6.66 us -> none  [the longest x2 6.3 us: per_device(): rows.reshape(count, 8, 4, 2, 128).transpose(3, 2, 0, 1, 4)]
    ppermute x10 -> x13, starting transfers between devices: 29.5 us -> 35.1 us  [the longest x7 20.8 us: to_team(): return lax.ppermute(piece, TEAM, route)]
  transfers between devices with their start and end apart: 13 -> 14, of which waited for: 8 -> 8; matrix products, arithmetic and copies ran while one was open for 8% -> 0% of each run, Pallas kernels for 0% -> 6%
where the time goes in v2:
time: 175 us; the launch traced here: 173 us
  blocking collectives  64.4 us (37%)
  starting transfers between devices  51.7 us (30%)
  waiting for transfers between devices  26.5 us (15%)
  Pallas kernels  23 us (13%)
  local copies, waits for them, and re-layouts  4.2 us (2%)
  other arithmetic  2.07 us (1%)
    all_to_all x4, blocking collectives, exchanged(): return lax.all_to_all(blocks, axes, 0, 0, tiled=False)  64.4 us
    ppermute x7, starting transfers between devices, to_team(): return lax.ppermute(piece, TEAM, route)  20.8 us
    all_to_all x1, starting transfers between devices, exchanged(): return lax.all_to_all(blocks, axes, 0, 0, tiled=False)  16.6 us
    ppermute x7, waiting for transfers between devices, to_team(): return lax.ppermute(piece, TEAM, route)  12.6 us
    ppermute x4, waiting for transfers between devices, to_chip(): lax.ppermute(block, ('zh', 'y'), [(i, i + hop) for i in chips if i + hop...  11.4 us
    pallas_call x1, Pallas kernels, attention(): pl.pallas_call(attention_kernel, in_specs=[smem(), smem()] + [vmem()] * 6...  10.7 us
    ppermute x4, starting transfers between devices, to_chip(): lax.ppermute(block, ('zh', 'y'), [(i, i + hop) for i in chips if i + hop...  10.3 us
    pallas_call x1, Pallas kernels, make_pieces(): pl.pallas_call(pieces_kernel, grid_spec=pltpu.PrefetchScalarGridSpec(num_...  9.55 us
  transfers between devices with their start and end apart: 14, of which 8 were waited for; matrix products, arithmetic and copies ran while one was open for 0% of the time, Pallas kernels for 6%

profile of v2, /device:TPU:6, one launch (start us, length us, event | category | flops | bytes accessed | tf_op | source)
XLA Modules:
  0.0 172.7 jit_solution(13664098436328110314)
XLA Ops:
  0.6 1.5 broadcast_in_dim.24
  2.2 16.6 %all-to-all-start = ((bf16[64,16,256]{2,1,0:T(8,128)(2,1)}), bf16[64,16,256]{2,1,0:T(8,128)(2,1)S(1)}, u32[]{:S(2)}, u32[]{:S(2)}) async-start(bf16[64,16,256]{2,1,0:T(8,128)(2,1)} %broadcast_in_dim.24), calls=%async_computation | async-start | bytes 1048576 | tf_op jit(solution)/shard_map/all_to_all | solution.py:36
  18.8 1.6 copy-done
  20.4 9.5 %pieces.1 = (bf16[128,1024]{1,0:T(8,128)(2,1)S(1)}, bf16[128,1024]{1,0:T(8,128)(2,1)S(1)}, bf16[128,1024]{1,0:T(8,128)(2,1)S(1)}, bf16[128,1024]{1,0:T(8,128)(2,...) custom-call(s32[2]{0:T(128)S(1)} %pad_add_fusion.1.place, ...), custom_call_target="tpu_custom_call" | custom-call | bytes 4194304 | tf_op jit(solution)/shard_map/pieces/pallas_call | solution.py:84
  30.0 2.4 %collective-permute-start = (bf16[128,1024]{1,0:T(8,128)(2,1)S(1)}, bf16[128,1024]{1,0:T(8,128)(2,1)S(1)}, u32[]{:S(2)}, u32[]{:S(2)}) collective-permute-start(bf16[128,1024]{1,0:T(8,128)(2,1)S(1)} %get-tuple-element.16), channel_id=1, source_target_pairs={{0,2},{2,4},{4,6},{6,0},{8,10},{10,12},{12,14},{14,8},{1,3},{3,5},... | collective-permute-start | bytes 786440 | tf_op jit(solution)/shard_map/ppermute | solution.py:53
  32.4 4.3 %collective-permute-start.1 = (bf16[128,1024]{1,0:T(8,128)(2,1)S(1)}, bf16[128,1024]{1,0:T(8,128)(2,1)S(1)}, u32[]{:S(2)}, u32[]{:S(2)}) collective-permute-start(bf16[128,1024]{1,0:T(8,128)(2,1)S(1)} %get-tuple-element.17), channel_id=1, source_target_pairs={{0,4},{2,6},{4,0},{6,2},{8,12},{10,14},{12,8},{14,10},{1,5},{3,7},... | collective-permute-start | bytes 786440 | tf_op jit(solution)/shard_map/ppermute | solution.py:53
  36.7 1.9 %collective-permute-start.2 = (bf16[128,1024]{1,0:T(8,128)(2,1)S(1)}, bf16[128,1024]{1,0:T(8,128)(2,1)S(1)}, u32[]{:S(2)}, u32[]{:S(2)}) collective-permute-start(bf16[128,1024]{1,0:T(8,128)(2,1)S(1)} %get-tuple-element.18), channel_id=1, source_target_pairs={{0,6},{2,0},{4,2},{6,4},{8,14},{10,8},{12,10},{14,12},{1,7},{3,1},... | collective-permute-start | bytes 786440 | tf_op jit(solution)/shard_map/ppermute | solution.py:53
  38.6 1.9 %collective-permute-start.3 = (bf16[128,1024]{1,0:T(8,128)(2,1)S(1)}, bf16[128,1024]{1,0:T(8,128)(2,1)S(1)}, u32[]{:S(2)}, u32[]{:S(2)}) collective-permute-start(bf16[128,1024]{1,0:T(8,128)(2,1)S(1)} %get-tuple-element.19), channel_id=1, source_target_pairs={{0,8},{2,10},{4,12},{6,14},{8,0},{10,2},{12,4},{14,6},{1,9},{3,11}... | collective-permute-start | bytes 786440 | tf_op jit(solution)/shard_map/ppermute | solution.py:53
  40.6 5.2 %collective-permute-start.4 = (bf16[128,1024]{1,0:T(8,128)(2,1)S(1)}, bf16[128,1024]{1,0:T(8,128)(2,1)S(1)}, u32[]{:S(2)}, u32[]{:S(2)}) collective-permute-start(bf16[128,1024]{1,0:T(8,128)(2,1)S(1)} %get-tuple-element.20), channel_id=1, source_target_pairs={{0,10},{2,12},{4,14},{6,8},{8,2},{10,4},{12,6},{14,0},{1,11},{3,13... | collective-permute-start | bytes 786440 | tf_op jit(solution)/shard_map/ppermute | solution.py:53
  45.8 1.9 %collective-permute-start.5 = (bf16[128,1024]{1,0:T(8,128)(2,1)S(1)}, bf16[128,1024]{1,0:T(8,128)(2,1)S(1)}, u32[]{:S(2)}, u32[]{:S(2)}) collective-permute-start(bf16[128,1024]{1,0:T(8,128)(2,1)S(1)} %get-tuple-element.21), channel_id=1, source_target_pairs={{0,12},{2,14},{4,8},{6,10},{8,4},{10,6},{12,0},{14,2},{1,13},{3,15... | collective-permute-start | bytes 786440 | tf_op jit(solution)/shard_map/ppermute | solution.py:53
  47.8 3.0 %collective-permute-start.6 = (bf16[128,1024]{1,0:T(8,128)(2,1)S(1)}, bf16[128,1024]{1,0:T(8,128)(2,1)S(1)}, u32[]{:S(2)}, u32[]{:S(2)}) collective-permute-start(bf16[128,1024]{1,0:T(8,128)(2,1)S(1)} %get-tuple-element.22), channel_id=1, source_target_pairs={{0,14},{2,8},{4,10},{6,12},{8,6},{10,0},{12,2},{14,4},{1,15},{3,9}... | collective-permute-start | bytes 786440 | tf_op jit(solution)/shard_map/ppermute | solution.py:53
  50.9 6.6 %collective-permute-done.4.refs_5_ = bf16[128,1024]{1,0:T(8,128)(2,1)S(1)} collective-permute-done((bf16[128,1024]{1,0:T(8,128)(2,1)S(1)}, bf16[128,1024]{1,0:T(8,128)(2,1)S(1)}, u32[]{:S(2)}, u32[]{:S(2)}) %collective-permute-start.4) | collective-permute-done | bytes 262176 | tf_op jit(solution)/shard_map/ppermute | solution.py:53
  57.7 5.7 %collective-permute-done.6.refs_7_ = bf16[128,1024]{1,0:T(8,128)(2,1)S(1)} collective-permute-done((bf16[128,1024]{1,0:T(8,128)(2,1)S(1)}, bf16[128,1024]{1,0:T(8,128)(2,1)S(1)}, u32[]{:S(2)}, u32[]{:S(2)}) %collective-permute-start.6) | collective-permute-done | bytes 262176 | tf_op jit(solution)/shard_map/ppermute | solution.py:53
  63.4 1.3 project.1
  64.7 12.7 %all_to_all.25 = bf16[8,128,256]{2,1,0:T(8,128)(2,1)} all-to-all(bf16[8,128,256]{2,1,0:T(8,128)(2,1)S(1)} %project.1), channel_id=1, replica_groups=mesh['zh'=4,'y'=8,'core'=2,'x'=4,'zl'=2] {'core','x'}, dimensions={0} | all-to-all | bytes 1048576 | tf_op jit(solution)/shard_map/all_to_all | solution.py:36
  77.4 1.1 reduce_sum.33.own
  78.5 4.4 %collective-permute-start.8 = (bf16[128,256]{1,0:T(8,128)(2,1)S(1)}, bf16[128,256]{1,0:T(8,128)(2,1)S(1)}, u32[]{:S(2)}, u32[]{:S(2)}) collective-permute-start(bf16[128,256]{1,0:T(8,128)(2,1)S(1)} %reduce_sum.33.own), channel_id=1, source_target_pairs={{0,32},{16,48},{32,64},{48,80},{64,96},{80,112},{96,128},{112,144}... | collective-permute-start | bytes 196616 | tf_op jit(solution)/shard_map/ppermute | solution.py:58
  82.9 3.4 %collective-permute-start.7 = (bf16[128,256]{1,0:T(8,128)(2,1)S(1)}, bf16[128,256]{1,0:T(8,128)(2,1)S(1)}, u32[]{:S(2)}, u32[]{:S(2)}) collective-permute-start(bf16[128,256]{1,0:T(8,128)(2,1)S(1)} %reduce_sum.33.own), channel_id=1, source_target_pairs={{0,16},{16,32},{32,48},{48,64},{64,80},{80,96},{96,112},{112,128},... | collective-permute-start | bytes 196616 | tf_op jit(solution)/shard_map/ppermute | solution.py:58
  86.3 2.5 %collective-permute-done.7.near = bf16[128,256]{1,0:T(8,128)(2,1)S(1)} collective-permute-done((bf16[128,256]{1,0:T(8,128)(2,1)S(1)}, bf16[128,256]{1,0:T(8,128)(2,1)S(1)}, u32[]{:S(2)}, u32[]{:S(2)}) %collective-permute-start.7) | collective-permute-done | bytes 65568 | tf_op jit(solution)/shard_map/ppermute | solution.py:58
  88.8 1.9 %collective-permute-start.9 = (bf16[3,128,256]{2,1,0:T(8,128)(2,1)S(1)}, bf16[3,128,256]{2,1,0:T(8,128)(2,1)S(1)}, u32[]{:S(2)}, u32[]{:S(2)}) collective-permute-start(bf16[3,128,256]{2,1,0:T(8,128)(2,1)S(1)} %pad_maximum_fusion), channel_id=1, source_target_pairs={{0,8},{8,0},{1,9},{9,1},{2,10},{10,2},{3,11},{11,3},{4,12},{12,4},... | collective-permute-start | bytes 589832 | tf_op jit(solution)/shard_map/ppermute | solution.py:62
  90.8 1.3 collective-permute-done.9.other
  93.2 10.7 %attention.1 = (bf16[128,2048]{1,0:T(8,128)(2,1)}, bf16[128,2048]{1,0:T(8,128)(2,1)}, f32[3,128,256]{2,1,0:T(8,128)S(1)}, bf16[2,128,256]{2,1,0:T(8,128)(2,1)S(1)}) custom-call(s32[2]{0:T(128)S(1)} %pad_add_fusion.place, s32[1,32]{1,0:T(1,128)S(1)} %copy-done.3, bf16[128,2048]{1,0:T(8,128)(2,1)S(1)} %bitcast.28, bf16[128,2048]{1,0:T(8,128)(2,1)S(1)} %bitcast.29, ...), custom_call_target="tpu_custom_call" | custom-call | flops 2147483648 | bytes 3145728 | tf_op jit(solution)/shard_map/attention/pallas_call | solution.py:208
  103.9 2.0 %collective-permute-start.10 = (bf16[2,128,256]{2,1,0:T(8,128)(2,1)S(1)}, bf16[2,128,256]{2,1,0:T(8,128)(2,1)S(1)}, u32[]{:S(2)}, u32[]{:S(2)}) collective-permute-start(bf16[2,128,256]{2,1,0:T(8,128)(2,1)S(1)} %get-tuple-element.26), channel_id=1, source_target_pairs={{0,8},{8,0},{1,9},{9,1},{2,10},{10,2},{3,11},{11,3},{4,12},{12,4},... | collective-permute-start | bytes 393224 | tf_op jit(solution)/shard_map/ppermute | solution.py:62
  106.0 1.2 collective-permute-done.10
  107.2 1.3 collective-permute-start.11
  108.5 1.3 collective-permute-start.12
  109.8 4.2 %collective-permute-done.11 = bf16[128,256]{1,0:T(8,128)(2,1)S(1)} collective-permute-done((bf16[128,256]{1,0:T(8,128)(2,1)S(1)}, bf16[128,256]{1,0:T(8,128)(2,1)S(1)}, u32[]{:S(2)}, u32[]{:S(2)}) %collective-permute-start.11) | collective-permute-done | bytes 65568 | tf_op jit(solution)/shard_map/ppermute | solution.py:58
  114.0 4.7 %collective-permute-done.12 = bf16[128,256]{1,0:T(8,128)(2,1)S(1)} collective-permute-done((bf16[128,256]{1,0:T(8,128)(2,1)S(1)}, bf16[128,256]{1,0:T(8,128)(2,1)S(1)}, u32[]{:S(2)}, u32[]{:S(2)}) %collective-permute-start.12) | collective-permute-done | bytes 65568 | tf_op jit(solution)/shard_map/ppermute | solution.py:58
  118.8 12.6 %all_to_all.26.grads = bf16[8,128,256]{2,1,0:T(8,128)(2,1)S(1)} all-to-all(bf16[8,128,256]{2,1,0:T(8,128)(2,1)S(1)} %broadcast_in_dim.28), channel_id=1, replica_groups=mesh['zh'=4,'y'=8,'core'=2,'x'=4,'zl'=2] {'core','x'}, dimensions={0} | all-to-all | bytes 1048576 | tf_op jit(solution)/shard_map/all_to_all | solution.py:36
  131.4 1.4 weight_grad.1
  132.8 24.7 %all_to_all.27 = bf16[8,4,32,256]{3,2,1,0:T(8,128)(2,1)S(1)} all-to-all(bf16[8,4,32,256]{3,2,1,0:T(8,128)(2,1)S(1)} %weight_grad.1), channel_id=1, replica_groups=mesh['zh'=4,'y'=8,'core'=2,'x'=4,'zl'=2] {'y'}, dimensions={0} | all-to-all | bytes 1048576 | tf_op jit(solution)/shard_map/all_to_all | solution.py:36
  157.6 14.4 %all_to_all.28 = bf16[8,16,256]{2,1,0:T(8,128)(2,1)S(1)} all-to-all(bf16[8,16,256]{2,1,0:T(8,128)(2,1)S(1)} %bitcast.30), channel_id=1, replica_groups=mesh['zh'=4,'y'=8,'core'=2,'x'=4,'zl'=2] {'zh','zl'}, dimensions={0} | all-to-all | bytes 131072 | tf_op jit(solution)/shard_map/all_to_all | solution.py:36
  (23 shorter events, 2.4 us)
Async XLA Ops:
  2.2 61.3 %all-to-all-start = ((bf16[64,16,256]{2,1,0:T(8,128)(2,1)}), bf16[64,16,256]{2,1,0:T(8,128)(2,1)S(1)}, u32[]{:S(2)}, u32[]{:S(2)}) async-start(bf16[64,16,256]{2,1,0:T(8,128)(2,1)} %broadcast_in_dim.24), calls=%async_computation | async-start | bytes 1048576 | tf_op jit(solution)/shard_map/all_to_all | solution.py:36
  18.8 1.6 copy-start
  30.0 15.8 %collective-permute-start = (bf16[128,1024]{1,0:T(8,128)(2,1)S(1)}, bf16[128,1024]{1,0:T(8,128)(2,1)S(1)}, u32[]{:S(2)}, u32[]{:S(2)}) collective-permute-start(bf16[128,1024]{1,0:T(8,128)(2,1)S(1)} %get-tuple-element.16), channel_id=1, source_target_pairs={{0,2},{2,4},{4,6},{6,0},{8,10},{10,12},{12,14},{14,8},{1,3},{3,5},... | collective-permute-start | bytes 786440 | tf_op jit(solution)/shard_map/ppermute | solution.py:53
  32.4 15.4 %collective-permute-start.1 = (bf16[128,1024]{1,0:T(8,128)(2,1)S(1)}, bf16[128,1024]{1,0:T(8,128)(2,1)S(1)}, u32[]{:S(2)}, u32[]{:S(2)}) collective-permute-start(bf16[128,1024]{1,0:T(8,128)(2,1)S(1)} %get-tuple-element.17), channel_id=1, source_target_pairs={{0,4},{2,6},{4,0},{6,2},{8,12},{10,14},{12,8},{14,10},{1,5},{3,7},... | collective-permute-start | bytes 786440 | tf_op jit(solution)/shard_map/ppermute | solution.py:53
  36.7 14.1 %collective-permute-start.2 = (bf16[128,1024]{1,0:T(8,128)(2,1)S(1)}, bf16[128,1024]{1,0:T(8,128)(2,1)S(1)}, u32[]{:S(2)}, u32[]{:S(2)}) collective-permute-start(bf16[128,1024]{1,0:T(8,128)(2,1)S(1)} %get-tuple-element.18), channel_id=1, source_target_pairs={{0,6},{2,0},{4,2},{6,4},{8,14},{10,8},{12,10},{14,12},{1,7},{3,1},... | collective-permute-start | bytes 786440 | tf_op jit(solution)/shard_map/ppermute | solution.py:53
  38.6 12.2 %collective-permute-start.3 = (bf16[128,1024]{1,0:T(8,128)(2,1)S(1)}, bf16[128,1024]{1,0:T(8,128)(2,1)S(1)}, u32[]{:S(2)}, u32[]{:S(2)}) collective-permute-start(bf16[128,1024]{1,0:T(8,128)(2,1)S(1)} %get-tuple-element.19), channel_id=1, source_target_pairs={{0,8},{2,10},{4,12},{6,14},{8,0},{10,2},{12,4},{14,6},{1,9},{3,11}... | collective-permute-start | bytes 786440 | tf_op jit(solution)/shard_map/ppermute | solution.py:53
  40.6 16.9 %collective-permute-start.4 = (bf16[128,1024]{1,0:T(8,128)(2,1)S(1)}, bf16[128,1024]{1,0:T(8,128)(2,1)S(1)}, u32[]{:S(2)}, u32[]{:S(2)}) collective-permute-start(bf16[128,1024]{1,0:T(8,128)(2,1)S(1)} %get-tuple-element.20), channel_id=1, source_target_pairs={{0,10},{2,12},{4,14},{6,8},{8,2},{10,4},{12,6},{14,0},{1,11},{3,13... | collective-permute-start | bytes 786440 | tf_op jit(solution)/shard_map/ppermute | solution.py:53
  45.8 11.9 %collective-permute-start.5 = (bf16[128,1024]{1,0:T(8,128)(2,1)S(1)}, bf16[128,1024]{1,0:T(8,128)(2,1)S(1)}, u32[]{:S(2)}, u32[]{:S(2)}) collective-permute-start(bf16[128,1024]{1,0:T(8,128)(2,1)S(1)} %get-tuple-element.21), channel_id=1, source_target_pairs={{0,12},{2,14},{4,8},{6,10},{8,4},{10,6},{12,0},{14,2},{1,13},{3,15... | collective-permute-start | bytes 786440 | tf_op jit(solution)/shard_map/ppermute | solution.py:53
  47.8 15.6 %collective-permute-start.6 = (bf16[128,1024]{1,0:T(8,128)(2,1)S(1)}, bf16[128,1024]{1,0:T(8,128)(2,1)S(1)}, u32[]{:S(2)}, u32[]{:S(2)}) collective-permute-start(bf16[128,1024]{1,0:T(8,128)(2,1)S(1)} %get-tuple-element.22), channel_id=1, source_target_pairs={{0,14},{2,8},{4,10},{6,12},{8,6},{10,0},{12,2},{14,4},{1,15},{3,9}... | collective-permute-start | bytes 786440 | tf_op jit(solution)/shard_map/ppermute | solution.py:53
  63.4 28.7 %copy-start.1 = (bf16[1,128,2048]{2,1,0:T(8,128)(2,1)S(1)}, bf16[1,128,2048]{2,1,0:T(8,128)(2,1)}, u32[]{:S(2)}) copy-start(bf16[1,128,2048]{2,1,0:T(8,128)(2,1)} %param.6) | copy-start | bytes 1572868
  63.4 28.7 %copy-start.3 = (s32[1,32]{1,0:T(1,128)S(1)}, s32[1,32]{1,0:T(1,128)}, u32[]{:S(2)}) copy-start(s32[1,32]{1,0:T(1,128)} %lengths.1) | copy-start | bytes 388
  78.5 7.8 %collective-permute-start.8 = (bf16[128,256]{1,0:T(8,128)(2,1)S(1)}, bf16[128,256]{1,0:T(8,128)(2,1)S(1)}, u32[]{:S(2)}, u32[]{:S(2)}) collective-permute-start(bf16[128,256]{1,0:T(8,128)(2,1)S(1)} %reduce_sum.33.own), channel_id=1, source_target_pairs={{0,32},{16,48},{32,64},{48,80},{64,96},{80,112},{96,128},{112,144}... | collective-permute-start | bytes 196616 | tf_op jit(solution)/shard_map/ppermute | solution.py:58
  82.9 5.9 %collective-permute-start.7 = (bf16[128,256]{1,0:T(8,128)(2,1)S(1)}, bf16[128,256]{1,0:T(8,128)(2,1)S(1)}, u32[]{:S(2)}, u32[]{:S(2)}) collective-permute-start(bf16[128,256]{1,0:T(8,128)(2,1)S(1)} %reduce_sum.33.own), channel_id=1, source_target_pairs={{0,16},{16,32},{32,48},{48,64},{64,80},{80,96},{96,112},{112,128},... | collective-permute-start | bytes 196616 | tf_op jit(solution)/shard_map/ppermute | solution.py:58
  88.8 3.3 %collective-permute-start.9 = (bf16[3,128,256]{2,1,0:T(8,128)(2,1)S(1)}, bf16[3,128,256]{2,1,0:T(8,128)(2,1)S(1)}, u32[]{:S(2)}, u32[]{:S(2)}) collective-permute-start(bf16[3,128,256]{2,1,0:T(8,128)(2,1)S(1)} %pad_maximum_fusion), channel_id=1, source_target_pairs={{0,8},{8,0},{1,9},{9,1},{2,10},{10,2},{3,11},{11,3},{4,12},{12,4},... | collective-permute-start | bytes 589832 | tf_op jit(solution)/shard_map/ppermute | solution.py:62
  92.2 1.0 copy-start.2
  103.9 3.2 %collective-permute-start.10 = (bf16[2,128,256]{2,1,0:T(8,128)(2,1)S(1)}, bf16[2,128,256]{2,1,0:T(8,128)(2,1)S(1)}, u32[]{:S(2)}, u32[]{:S(2)}) collective-permute-start(bf16[2,128,256]{2,1,0:T(8,128)(2,1)S(1)} %get-tuple-element.26), channel_id=1, source_target_pairs={{0,8},{8,0},{1,9},{9,1},{2,10},{10,2},{3,11},{11,3},{4,12},{12,4},... | collective-permute-start | bytes 393224 | tf_op jit(solution)/shard_map/ppermute | solution.py:62
  107.2 6.8 %collective-permute-start.11 = (bf16[128,256]{1,0:T(8,128)(2,1)S(1)}, bf16[128,256]{1,0:T(8,128)(2,1)S(1)}, u32[]{:S(2)}, u32[]{:S(2)}) collective-permute-start(bf16[128,256]{1,0:T(8,128)(2,1)S(1)} %get-tuple-element.27), channel_id=1, source_target_pairs={{16,0},{32,16},{48,32},{64,48},{80,64},{96,80},{112,96},{128,112},... | collective-permute-start | bytes 196616 | tf_op jit(solution)/shard_map/ppermute | solution.py:58
  108.5 10.2 %collective-permute-start.12 = (bf16[128,256]{1,0:T(8,128)(2,1)S(1)}, bf16[128,256]{1,0:T(8,128)(2,1)S(1)}, u32[]{:S(2)}, u32[]{:S(2)}) collective-permute-start(bf16[128,256]{1,0:T(8,128)(2,1)S(1)} %get-tuple-element.28), channel_id=1, source_target_pairs={{32,0},{48,16},{64,32},{80,48},{96,64},{112,80},{128,96},{144,112}... | collective-permute-start | bytes 196616 | tf_op jit(solution)/shard_map/ppermute | solution.py:58

commit v3 on v2

v3 whole, which is shorter than its diff:
```python
import functools

import jax
import jax.numpy as jnp
from jax import lax
from jax.experimental import pallas as pl
from jax.experimental.pallas import tpu as pltpu
from jax.sharding import Mesh, PartitionSpec as P

AXES = ("zh", "y", "core", "x", "zl")
CTX = ("zh", "y", "core")
DP = ("x", "zl")
ZH, Y, CORE, X, ZL = 4, 8, 2, 4, 2
CHIPS = ZH * Y
COUNT = 128
HEAD = 128
WIDTH = 2 * HEAD
BF16, F32 = jnp.bfloat16, jnp.float32
LOG2E = 1.4426950408889634
VMEM_LIMIT = 40 << 20


def vmem():
    return pl.BlockSpec(memory_space=pltpu.VMEM)


def smem():
    return pl.BlockSpec(memory_space=pltpu.SMEM)


def params():
    return pltpu.CompilerParams(vmem_limit_bytes=VMEM_LIMIT)


def exchanged(blocks, axes):
    return lax.all_to_all(blocks, axes, 0, 0, tiled=False)


def to_team(piece, step):
    return lax.ppermute(piece, "x", [(x, (x + step) % X) for x in range(X)])


def to_chip(block, hop):
    chips = range(CHIPS)
    return lax.ppermute(block, ("zh", "y"), [(i, i + hop) for i in chips if i + hop in chips])


def to_other_core(block):
    return lax.ppermute(block, "core", [(0, 1), (1, 0)])


def pieces_kernel(place, rows, own, ahead, behind, over, under, sorted_rows):
    core, x = place[0], place[1]
    span = 32 * X
    old = lax.broadcasted_iota(jnp.int32, (4 * span, 4 * span), 0)
    new = lax.broadcasted_iota(jnp.int32, (4 * span, 4 * span), 1)
    moved = (old // 32 % X) * span + (old // span) * 32 + old % 32
    turn = (new == moved).astype(F32).astype(BF16)
    for group in range(CHIPS // 4):
        for c in range(CORE):
            tiles = [rows[:, ((group * 4 + b) * CORE + c) * span :][:, :span] for b in range(4)]
            tile = jnp.dot(jnp.concatenate(tiles, axis=1), turn, preferred_element_type=F32).astype(BF16)
            for j in range(X):
                sorted_rows[c * X + j, :, group * span : (group + 1) * span] = tile[:, j * span : (j + 1) * span]
    for half in range(2):
        first = (core + half) % CORE * X
        own[half] = sorted_rows[first + x]
        ahead[half] = sorted_rows[first + (x + 1) % X]
        behind[half] = sorted_rows[first + (x + 3) % X]
        (over, under)[half][...] = sorted_rows[first + (x + 2) % X]


def make_pieces(place, rows):
    features = rows.shape[1] // (CORE * X)
    piece = (COUNT, features)
    return pl.pallas_call(
        pieces_kernel,
        in_specs=[smem(), vmem()],
        out_specs=[vmem()] * 5,
        out_shape=[jax.ShapeDtypeStruct(shape, BF16) for shape in [(2,) + piece] * 3 + [piece] * 2],
        scratch_shapes=[
            pltpu.VMEM((CORE * X,) + piece, BF16),
        ],
        compiler_params=params(),
        cost_estimate=pl.CostEstimate(flops=1 << 30, bytes_accessed=4 << 20, transcendentals=0),
        name="pieces",
    )(place, rows)


def team_pieces(own, ahead, behind, over, under):
    halfway = to_team(over, 1), to_team(under, -1)
    pieces = own, to_team(behind, -1), to_team(ahead, 1), to_team(halfway[0], 1), to_team(halfway[1], -1)
    return pieces, halfway


def halves(refs, half):
    own, after, before, over, under = refs
    return [(0, own[half]), (1, after[half]), (3, before[half]), (2, (over, under)[half][...])]


def project_kernel(place, weight, weight_other, own, after, before, over, under, out):
    refs = (own, after, before, over, under)
    rows = [w[...].reshape(ZH * Y * 32, WIDTH) for w in (weight, weight_other)]
    for (step, first), (_, second) in zip(halves(refs, 0), halves(refs, 1)):
        part = jnp.dot(first, rows[0], preferred_element_type=F32)
        part += jnp.dot(second, rows[1], preferred_element_type=F32)
        out[(place[1] + step) % X] = part.astype(BF16)


def project(place, weight, weight_other, pieces):
    return pl.pallas_call(
        project_kernel,
        in_specs=[smem()] + [vmem()] * 7,
        out_specs=vmem(),
        out_shape=jax.ShapeDtypeStruct((X, COUNT, WIDTH), BF16),
        compiler_params=params(),
        cost_estimate=pl.CostEstimate(flops=1 << 29, bytes_accessed=3 << 20, transcendentals=0),
        name="project",
    )(place, weight, weight_other, *pieces)


def weight_grad_kernel(half, place, grads, own, after, before, over, under, out, total):
    turned, rows = [], []
    for step, piece in halves((own, after, before, over, under), half):
        turned.append(grads[(place[1] + step) % X].T)
        rows.append(piece)
    total[...] = jnp.dot(
        jnp.concatenate(turned, axis=1), jnp.concatenate(rows, axis=0), preferred_element_type=F32
    )
    for four in range(CHIPS // 4):
        block = total[:, four * 128 : four * 128 + 128].T
        for i in range(4):
            zh, y = divmod(four * 4 + i, Y)
            out[y, zh] = block[i * 32 : i * 32 + 32].astype(BF16)


def weight_grad_parts(half, place, grads, pieces):
    features = pieces[0].shape[2]
    return pl.pallas_call(
        functools.partial(weight_grad_kernel, half),
        in_specs=[smem()] + [vmem()] * 6,
        out_specs=vmem(),
        out_shape=jax.ShapeDtypeStruct((Y, ZH, 32, WIDTH), BF16),
        scratch_shapes=[pltpu.VMEM((WIDTH, features), F32)],
        compiler_params=params(),
        cost_estimate=pl.CostEstimate(flops=1 << 28, bytes_accessed=2 << 20, transcendentals=0),
        name="weight_grad",
    )(place, grads, *pieces)


def summed_kernel(parts, out):
    total = parts[0].astype(F32)
    for i in range(1, parts.shape[0]):
        total = total + parts[i].astype(F32)
    out[...] = total.astype(out.dtype)


def summed(parts, kind):
    return pl.pallas_call(
        summed_kernel,
        in_specs=[vmem()],
        out_specs=vmem(),
        out_shape=jax.ShapeDtypeStruct(parts.shape[1:], kind),
        compiler_params=params(),
        name="summed",
    )(parts)


def attention_kernel(place, lengths, queries, grads, own, near, far, other, attn, grad_q, grad_own, grad_other):
    core, chip_pos = place[0], place[1]
    scale = HEAD ** -0.5
    blocks = [own[...], near[...], far[...], other[1 - core], other[2 - core]]
    starts = [chip_pos + core * COUNT - 2 * COUNT * i for i in range(3)]
    starts += [chip_pos + (1 - core) * COUNT - 2 * COUNT * (1 - core + i) for i in range(2)]
    keys = jnp.concatenate([b[:, :HEAD] for b in blocks], axis=0)
    values = jnp.concatenate([b[:, HEAD:] for b in blocks], axis=0)
    keys_t, values_t = keys.T, values.T

    query_pos = starts[0] + lax.broadcasted_iota(jnp.int32, (1, COUNT), 1)
    doc_start = jnp.zeros((1, COUNT), jnp.int32)
    end = jnp.int32(0)
    for doc in range(lengths.shape[1]):
        end = end + lengths[0, doc]
        doc_start = jnp.where(query_pos >= end, end, doc_start)
    row = lax.broadcasted_iota(jnp.int32, (COUNT, COUNT), 0)
    masks = []
    for start in starts:
        key_pos = start + row
        masks.append((key_pos >= doc_start) & (key_pos <= query_pos))
    cap = jnp.where(jnp.concatenate(masks, axis=0), F32(jnp.inf), F32(-1e30))
    cap = jnp.concatenate([cap, cap], axis=1)

    nt = (((1,), (1,)), ((), ()))
    total_k = total_v = None
    for pair in range(queries.shape[1] // WIDTH):
        cols = [slice((2 * pair + i) * HEAD, (2 * pair + i + 1) * HEAD) for i in range(2)]
        q = jnp.concatenate([queries[:, c] for c in cols], axis=0)
        g = jnp.concatenate([grads[:, c] for c in cols], axis=0)
        scores = lax.dot_general(keys, q, nt, preferred_element_type=F32) * F32(scale * LOG2E)
        scores = jnp.minimum(scores, cap)
        top = jnp.max(scores, axis=0, keepdims=True)
        weights = jnp.exp2(scores - top)
        inverse = 1.0 / jnp.sum(weights, axis=0, keepdims=True)
        dprobs = lax.dot_general(values, g, nt, preferred_element_type=F32)
        out_dot = jnp.sum(weights * dprobs, axis=0, keepdims=True) * inverse
        dscores = (weights * (dprobs - out_dot)).astype(BF16)
        weights = weights.astype(BF16)
        out = jnp.dot(values_t, weights, preferred_element_type=F32) * inverse
        dq = jnp.dot(keys_t, dscores, preferred_element_type=F32) * (inverse * scale)
        out, dq = out.T.astype(BF16), dq.T.astype(BF16)
        for i in range(2):
            attn[:, cols[i]] = out[i * COUNT : (i + 1) * COUNT]
            grad_q[:, cols[i]] = dq[i * COUNT : (i + 1) * COUNT]
        column = jnp.broadcast_to(inverse, (HEAD, WIDTH)).T
        part_k = jnp.dot(dscores, (q.astype(F32) * column).astype(BF16), preferred_element_type=F32)
        part_v = jnp.dot(weights, (g.astype(F32) * column).astype(BF16), preferred_element_type=F32)
        total_k = part_k if pair == 0 else total_k + part_k
        total_v = part_v if pair == 0 else total_v + part_v
    total = jnp.concatenate([total_k * scale, total_v], axis=1)
    for i in range(3):
        grad_own[i] = total[i * COUNT : (i + 1) * COUNT]
    for i in range(2):
        grad_other[i] = total[(3 + i) * COUNT : (4 + i) * COUNT].astype(BF16)


def attention(place, lengths, queries, grads, own, near, far, other):
    shape = jax.ShapeDtypeStruct(queries.shape, BF16)
    return pl.pallas_call(
        attention_kernel,
        in_specs=[smem(), smem()] + [vmem()] * 6,
        out_specs=[vmem()] * 4,
        out_shape=[
            shape,
            shape,
            jax.ShapeDtypeStruct((3, COUNT, WIDTH), F32),
            jax.ShapeDtypeStruct((2, COUNT, WIDTH), BF16),
        ],
        compiler_params=params(),
        cost_estimate=pl.CostEstimate(flops=2 << 30, bytes_accessed=3 << 20, transcendentals=5 << 18),
        name="attention",
    )(place, lengths, queries, grads, own, near, far, other)


def per_device(tokens_in, queries_in, kv_weight, out_grad, doc_lengths):
    core = lax.axis_index("core")
    chip = lax.axis_index(("zh", "y"))
    team_place = jnp.stack([core, lax.axis_index("x")]).astype(jnp.int32)
    ctx_place = jnp.stack([core, chip * (CORE * COUNT)]).astype(jnp.int32)

    pieces = make_pieces(team_place, tokens_in[0])
    ring = ZH * Y * ZL
    weight = exchanged(jnp.broadcast_to(kv_weight[None], (ring,) + kv_weight.shape), ("zh", "y", "zl"))
    pieces, halfway = team_pieces(*pieces)
    weight, _ = lax.optimization_barrier((weight, halfway))
    weight_other = to_other_core(weight)
    part = exchanged(project(team_place, weight, weight_other, pieces), "x")
    kv = summed(part, BF16)

    near, far = to_chip(kv, 1), to_chip(kv, 2)
    other = to_other_core(jnp.stack([kv, near, far]))
    attn, query_grad, grad_own, grad_other = attention(
        ctx_place, doc_lengths, queries_in[0], out_grad[0], kv, near, far, other
    )

    back = to_other_core(grad_other).astype(F32)
    first = core == 0
    far_grad = grad_own[2] + jnp.where(first, F32(0.0), back[1])
    near_grad = grad_own[1] + jnp.where(first, back[1], back[0])
    own_grad = grad_own[0] + jnp.where(first, back[0], F32(0.0))
    far_grad, near_grad = to_chip(far_grad.astype(BF16), -2), to_chip(near_grad.astype(BF16), -1)
    kv_grad = (own_grad + near_grad.astype(F32) + far_grad.astype(F32)).astype(BF16)

    team_grad = exchanged(jnp.broadcast_to(kv_grad[None], (X,) + kv_grad.shape), "x")
    theirs = to_other_core(weight_grad_parts(1, team_place, team_grad, pieces))
    ours = weight_grad_parts(0, team_place, team_grad, pieces)
    parts = exchanged((ours.astype(F32) + theirs.astype(F32)).astype(BF16), "y")
    parts = summed(parts, BF16).reshape(ZH * ZL, 16, WIDTH)
    weight_grad = summed(exchanged(parts, ("zh", "zl")), F32)
    return attn[None], query_grad[None], weight_grad


def solution(mesh):
    fine = Mesh(mesh.devices.reshape(ZH, Y, CORE, X, ZL), AXES)
    return jax.shard_map(
        per_device,
        mesh=fine,
        in_specs=(P(DP, CTX, None), P(DP, CTX, None), P(AXES, None), P(DP, CTX, None), P(DP, None)),
        out_specs=(P(DP, CTX, None), P(DP, CTX, None), P(AXES, None)),
        check_vma=False,
    )
```

time: 175 us -> 158 us (0.903)
  Pallas kernels: 23 us -> 15.2 us
  blocking collectives: 64.4 us -> 57.6 us
  waiting for transfers between devices: 26.5 us -> 24.6 us
    all_to_all x4, blocking collectives: 64.4 us -> 57.6 us  [exchanged(): return lax.all_to_all(blocks, axes, 0, 0, tiled=False)]
    pallas_call x3 -> x7, Pallas kernels: 12.2 us -> 7.2 us  [the longest x1 2.96 us: make_pieces(): pl.pallas_call(pieces_kernel, in_specs=[smem(), vmem()], out_specs=[vmem(...]
    ppermute x2 -> x4, starting transfers between devices: 3.95 us -> 7.78 us  [to_other_core(): return lax.ppermute(block, 'core', [(0, 1), (1, 0)])]
    pallas_call x1, Pallas kernels: 10.7 us -> 7.97 us  [attention(): pl.pallas_call(attention_kernel, in_specs=[smem(), smem()] + [vmem()] * 6...]
    ppermute x7 -> x6, waiting for transfers between devices: 12.6 us -> 10 us  [to_team(): return lax.ppermute(piece, 'x', [(x, (x + step) % X) for x in range(X)])]
    ppermute x7 -> x6, starting transfers between devices: 20.8 us -> 18.7 us  [to_team(): return lax.ppermute(piece, 'x', [(x, (x + step) % X) for x in range(X)])]
    reduce_sum x3 -> x0, other arithmetic: 1.81 us -> none  [the longest x1 1.12 us: per_device(): kv = jnp.sum(part.astype(F32), axis=0).astype(BF16)]
  transfers between devices with their start and end apart: 14 -> 15, of which waited for: 8 -> 9; matrix products, arithmetic and copies ran while one was open for 0% -> 0% of each run, Pallas kernels for 6% -> 3%
where the time goes in v3:
time: 158 us; the launch traced here: 156 us
  blocking collectives  57.6 us (36%)
  starting transfers between devices  53.4 us (34%)
  waiting for transfers between devices  24.6 us (16%)
  Pallas kernels  15.2 us (10%)
  local copies, waits for them, and re-layouts  4.19 us (3%)
    all_to_all x4, blocking collectives, exchanged(): return lax.all_to_all(blocks, axes, 0, 0, tiled=False)  57.6 us
    ppermute x6, starting transfers between devices, to_team(): return lax.ppermute(piece, 'x', [(x, (x + step) % X) for x in range(X)])  18.7 us
    all_to_all x1, starting transfers between devices, exchanged(): return lax.all_to_all(blocks, axes, 0, 0, tiled=False)  16.6 us
    ppermute x4, waiting for transfers between devices, to_chip(): lax.ppermute(block, ('zh', 'y'), [(i, i + hop) for i in chips if i + hop...  11.4 us
    ppermute x4, starting transfers between devices, to_chip(): lax.ppermute(block, ('zh', 'y'), [(i, i + hop) for i in chips if i + hop...  10.3 us
    ppermute x6, waiting for transfers between devices, to_team(): return lax.ppermute(piece, 'x', [(x, (x + step) % X) for x in range(X)])  10 us
    pallas_call x1, Pallas kernels, attention(): pl.pallas_call(attention_kernel, in_specs=[smem(), smem()] + [vmem()] * 6...  7.97 us
    ppermute x4, starting transfers between devices, to_other_core(): return lax.ppermute(block, 'core', [(0, 1), (1, 0)])  7.78 us
  transfers between devices with their start and end apart: 15, of which 9 were waited for; matrix products, arithmetic and copies ran while one was open for 0% of the time, Pallas kernels for 3%

profile of v3, /device:TPU:6, one launch (start us, length us, event | category | flops | bytes accessed | tf_op | source)
XLA Modules:
  0.0 156.3 jit_solution(12465356673956470161)
XLA Ops:
  0.6 1.5 broadcast_in_dim.24
  2.2 16.6 %all-to-all-start = ((bf16[64,16,256]{2,1,0:T(8,128)(2,1)}), bf16[64,16,256]{2,1,0:T(8,128)(2,1)S(1)}, u32[]{:S(2)}, u32[]{:S(2)}) async-start(bf16[64,16,256]{2,1,0:T(8,128)(2,1)} %broadcast_in_dim.24), calls=%async_computation | async-start | bytes 1048576 | tf_op jit(solution)/shard_map/all_to_all | solution.py:36
  18.8 1.6 %copy-done = bf16[1,128,8192]{2,1,0:T(8,128)(2,1)S(1)} copy-done((bf16[1,128,8192]{2,1,0:T(8,128)(2,1)S(1)}, bf16[1,128,8192]{2,1,0:T(8,128)(2,1)}, u32[]{:S(2)}) %copy-start) | copy-done | bytes 2097176
  20.4 3.0 %pieces.1 = (bf16[2,128,1024]{2,1,0:T(8,128)(2,1)S(1)}, bf16[2,128,1024]{2,1,0:T(8,128)(2,1)S(1)}, bf16[2,128,1024]{2,1,0:T(8,128)(2,1)}, bf16[128,1024]{1,0:T(8,128)(2,1)S(1)}, bf16[128,1024]{1,0:T(8,128)(2,1)S(1)}) custom-call(s32[2]{0:T(128)S(1)} %pad_add_fusion.1.place, bf16[128,8192]{1,0:T(8,128)(2,1)S(1)} %bitcast.26), custom_call_target="tpu_custom_call" | custom-call | flops 1073741824 | bytes 4194304 | tf_op jit(solution)/shard_map/pieces/pallas_call | solution.py:76
  23.4 2.4 %collective-permute-start = (bf16[128,1024]{1,0:T(8,128)(2,1)S(1)}, bf16[128,1024]{1,0:T(8,128)(2,1)S(1)}, u32[]{:S(2)}, u32[]{:S(2)}) collective-permute-start(bf16[128,1024]{1,0:T(8,128)(2,1)S(1)} %get-tuple-element.13), channel_id=1, source_target_pairs={{0,2},{2,4},{4,6},{6,0},{1,3},{3,5},{5,7},{7,1},{8,10},{10,12},{12... | collective-permute-start | bytes 786440 | tf_op jit(solution)/shard_map/ppermute | solution.py:40
  25.8 3.5 %collective-permute-start.1 = (bf16[128,1024]{1,0:T(8,128)(2,1)S(1)}, bf16[128,1024]{1,0:T(8,128)(2,1)}, u32[]{:S(2)}, u32[]{:S(2)}) collective-permute-start(bf16[128,1024]{1,0:T(8,128)(2,1)S(1)} %get-tuple-element.14), channel_id=1, source_target_pairs={{0,6},{2,0},{4,2},{6,4},{1,7},{3,1},{5,3},{7,5},{8,14},{10,8},{12,... | collective-permute-start | bytes 786440 | tf_op jit(solution)/shard_map/ppermute | solution.py:40
  29.2 2.7 %collective-permute-start.3 = (bf16[2,128,1024]{2,1,0:T(8,128)(2,1)}, bf16[2,128,1024]{2,1,0:T(8,128)(2,1)S(1)}, u32[]{:S(2)}, u32[]{:S(2)}) collective-permute-start(bf16[2,128,1024]{2,1,0:T(8,128)(2,1)} %get-tuple-element.17), channel_id=1, source_target_pairs={{0,6},{2,0},{4,2},{6,4},{1,7},{3,1},{5,3},{7,5},{8,14},{10,8},{12,... | collective-permute-start | bytes 1572872 | tf_op jit(solution)/shard_map/ppermute | solution.py:40
  32.0 4.3 %collective-permute-start.4 = (bf16[2,128,1024]{2,1,0:T(8,128)(2,1)S(1)}, bf16[2,128,1024]{2,1,0:T(8,128)(2,1)S(1)}, u32[]{:S(2)}, u32[]{:S(2)}) collective-permute-start(bf16[2,128,1024]{2,1,0:T(8,128)(2,1)S(1)} %get-tuple-element.18), channel_id=1, source_target_pairs={{0,2},{2,4},{4,6},{6,0},{1,3},{3,5},{5,7},{7,1},{8,10},{10,12},{12... | collective-permute-start | bytes 1572872 | tf_op jit(solution)/shard_map/ppermute | solution.py:40
  36.3 1.9 %collective-permute-done.1 = bf16[128,1024]{1,0:T(8,128)(2,1)} collective-permute-done((bf16[128,1024]{1,0:T(8,128)(2,1)S(1)}, bf16[128,1024]{1,0:T(8,128)(2,1)}, u32[]{:S(2)}, u32[]{:S(2)}) %collective-permute-start.1) | collective-permute-done | bytes 262176 | tf_op jit(solution)/shard_map/ppermute | solution.py:40
  38.2 1.9 %collective-permute-start.2 = (bf16[64,16,256]{2,1,0:T(8,128)(2,1)S(1)}, bf16[64,16,256]{2,1,0:T(8,128)(2,1)S(1)}, u32[]{:S(2)}, u32[]{:S(2)}) collective-permute-start(bf16[64,16,256]{2,1,0:T(8,128)(2,1)S(1)} %all-to-all-done.weight), channel_id=1, source_target_pairs={{0,8},{8,0},{1,9},{9,1},{2,10},{10,2},{3,11},{11,3},{4,12},{12,4},... | collective-permute-start | bytes 1572872 | tf_op jit(solution)/shard_map/ppermute | solution.py:49
  40.1 2.2 %collective-permute-start.5 = (bf16[128,1024]{1,0:T(8,128)(2,1)S(1)}, bf16[128,1024]{1,0:T(8,128)(2,1)S(1)}, u32[]{:S(2)}, u32[]{:S(2)}) collective-permute-start(bf16[128,1024]{1,0:T(8,128)(2,1)S(1)} %collective-permute-done), channel_id=1, source_target_pairs={{0,2},{2,4},{4,6},{6,0},{1,3},{3,5},{5,7},{7,1},{8,10},{10,12},{12... | collective-permute-start | bytes 786440 | tf_op jit(solution)/shard_map/ppermute | solution.py:40
  42.3 3.7 %collective-permute-start.6 = (bf16[128,1024]{1,0:T(8,128)(2,1)}, bf16[128,1024]{1,0:T(8,128)(2,1)S(1)}, u32[]{:S(2)}, u32[]{:S(2)}) collective-permute-start(bf16[128,1024]{1,0:T(8,128)(2,1)} %collective-permute-done.1), channel_id=1, source_target_pairs={{0,6},{2,0},{4,2},{6,4},{1,7},{3,1},{5,3},{7,5},{8,14},{10,8},{12,... | collective-permute-start | bytes 786440 | tf_op jit(solution)/shard_map/ppermute | solution.py:40
  46.0 6.0 %collective-permute-done.5.over = bf16[128,1024]{1,0:T(8,128)(2,1)S(1)} collective-permute-done((bf16[128,1024]{1,0:T(8,128)(2,1)S(1)}, bf16[128,1024]{1,0:T(8,128)(2,1)S(1)}, u32[]{:S(2)}, u32[]{:S(2)}) %collective-permute-start.5) | collective-permute-done | bytes 262176 | tf_op jit(solution)/shard_map/ppermute | solution.py:40
  52.0 2.1 %collective-permute-done.6.under = bf16[128,1024]{1,0:T(8,128)(2,1)S(1)} collective-permute-done((bf16[128,1024]{1,0:T(8,128)(2,1)}, bf16[128,1024]{1,0:T(8,128)(2,1)S(1)}, u32[]{:S(2)}, u32[]{:S(2)}) %collective-permute-start.6) | collective-permute-done | bytes 262176 | tf_op jit(solution)/shard_map/ppermute | solution.py:40
  54.1 1.3 project.1
  55.4 8.9 %all_to_all.25.parts = bf16[4,128,256]{2,1,0:T(8,128)(2,1)S(1)} all-to-all(bf16[4,128,256]{2,1,0:T(8,128)(2,1)S(1)} %project.1), channel_id=1, replica_groups=mesh['zh'=4,'y'=8,'core'=2,'x'=4,'zl'=2] {'x'}, dimensions={0} | all-to-all | bytes 524288 | tf_op jit(solution)/shard_map/all_to_all | solution.py:36
  64.4 4.4 %collective-permute-start.8 = (bf16[128,256]{1,0:T(8,128)(2,1)S(1)}, bf16[128,256]{1,0:T(8,128)(2,1)S(1)}, u32[]{:S(2)}, u32[]{:S(2)}) collective-permute-start(bf16[128,256]{1,0:T(8,128)(2,1)S(1)} %summed.3.own), channel_id=1, source_target_pairs={{0,32},{16,48},{32,64},{48,80},{64,96},{80,112},{96,128},{112,144}... | collective-permute-start | bytes 196616 | tf_op jit(solution)/shard_map/ppermute | solution.py:45
  68.7 3.4 %collective-permute-start.7 = (bf16[128,256]{1,0:T(8,128)(2,1)S(1)}, bf16[128,256]{1,0:T(8,128)(2,1)S(1)}, u32[]{:S(2)}, u32[]{:S(2)}) collective-permute-start(bf16[128,256]{1,0:T(8,128)(2,1)S(1)} %summed.3.own), channel_id=1, source_target_pairs={{0,16},{16,32},{32,48},{48,64},{64,80},{80,96},{96,112},{112,128},... | collective-permute-start | bytes 196616 | tf_op jit(solution)/shard_map/ppermute | solution.py:45
  72.1 2.0 %collective-permute-done.7.near = bf16[128,256]{1,0:T(8,128)(2,1)S(1)} collective-permute-done((bf16[128,256]{1,0:T(8,128)(2,1)S(1)}, bf16[128,256]{1,0:T(8,128)(2,1)S(1)}, u32[]{:S(2)}, u32[]{:S(2)}) %collective-permute-start.7) | collective-permute-done | bytes 65568 | tf_op jit(solution)/shard_map/ppermute | solution.py:45
  74.1 1.9 %collective-permute-start.9 = (bf16[3,128,256]{2,1,0:T(8,128)(2,1)S(1)}, bf16[3,128,256]{2,1,0:T(8,128)(2,1)S(1)}, u32[]{:S(2)}, u32[]{:S(2)}) collective-permute-start(bf16[3,128,256]{2,1,0:T(8,128)(2,1)S(1)} %pad_maximum_fusion), channel_id=1, source_target_pairs={{0,8},{8,0},{1,9},{9,1},{2,10},{10,2},{3,11},{11,3},{4,12},{12,4},... | collective-permute-start | bytes 589832 | tf_op jit(solution)/shard_map/ppermute | solution.py:49
  76.1 1.3 collective-permute-done.9.other
  78.5 8.0 %attention.1 = (bf16[128,2048]{1,0:T(8,128)(2,1)}, bf16[128,2048]{1,0:T(8,128)(2,1)}, f32[3,128,256]{2,1,0:T(8,128)S(1)}, bf16[2,128,256]{2,1,0:T(8,128)(2,1)S(1)}) custom-call(s32[2]{0:T(128)S(1)} %pad_add_fusion.place, s32[1,32]{1,0:T(1,128)S(1)} %copy-done.3, bf16[128,2048]{1,0:T(8,128)(2,1)S(1)} %bitcast.27, bf16[128,2048]{1,0:T(8,128)(2,1)S(1)} %bitcast.28, ...), custom_call_target="tpu_custom_call" | custom-call | flops 2147483648 | bytes 3145728 | tf_op jit(solution)/shard_map/attention/pallas_call | solution.py:228
  86.5 2.0 %collective-permute-start.10 = (bf16[2,128,256]{2,1,0:T(8,128)(2,1)S(1)}, bf16[2,128,256]{2,1,0:T(8,128)(2,1)S(1)}, u32[]{:S(2)}, u32[]{:S(2)}) collective-permute-start(bf16[2,128,256]{2,1,0:T(8,128)(2,1)S(1)} %get-tuple-element.22), channel_id=1, source_target_pairs={{0,8},{8,0},{1,9},{9,1},{2,10},{10,2},{3,11},{11,3},{4,12},{12,4},... | collective-permute-start | bytes 393224 | tf_op jit(solution)/shard_map/ppermute | solution.py:49
  88.5 1.2 collective-permute-done.10
  89.8 1.3 collective-permute-start.11
  91.1 1.3 collective-permute-start.12
  92.4 4.3 %collective-permute-done.11 = bf16[128,256]{1,0:T(8,128)(2,1)S(1)} collective-permute-done((bf16[128,256]{1,0:T(8,128)(2,1)S(1)}, bf16[128,256]{1,0:T(8,128)(2,1)S(1)}, u32[]{:S(2)}, u32[]{:S(2)}) %collective-permute-start.11) | collective-permute-done | bytes 65568 | tf_op jit(solution)/shard_map/ppermute | solution.py:45
  96.7 5.1 %collective-permute-done.12 = bf16[128,256]{1,0:T(8,128)(2,1)S(1)} collective-permute-done((bf16[128,256]{1,0:T(8,128)(2,1)S(1)}, bf16[128,256]{1,0:T(8,128)(2,1)S(1)}, u32[]{:S(2)}, u32[]{:S(2)}) %collective-permute-start.12) | collective-permute-done | bytes 65568 | tf_op jit(solution)/shard_map/ppermute | solution.py:45
  101.9 9.1 %all_to_all.26.grads = bf16[4,128,256]{2,1,0:T(8,128)(2,1)S(1)} all-to-all(bf16[4,128,256]{2,1,0:T(8,128)(2,1)S(1)} %broadcast_in_dim.28), channel_id=1, replica_groups=mesh['zh'=4,'y'=8,'core'=2,'x'=4,'zl'=2] {'x'}, dimensions={0} | all-to-all | bytes 524288 | tf_op jit(solution)/shard_map/all_to_all | solution.py:36
  112.1 1.9 %collective-permute-start.13 = (bf16[8,4,32,256]{3,2,1,0:T(8,128)(2,1)S(1)}, bf16[8,4,32,256]{3,2,1,0:T(8,128)(2,1)S(1)}, u32[]{:S(2)}, u32[]{:S(2)}) collective-permute-start(bf16[8,4,32,256]{3,2,1,0:T(8,128)(2,1)S(1)} %weight_grad.3), channel_id=1, source_target_pairs={{0,8},{8,0},{1,9},{9,1},{2,10},{10,2},{3,11},{11,3},{4,12},{12,4},... | collective-permute-start | bytes 1572872 | tf_op jit(solution)/shard_map/ppermute | solution.py:49
  116.1 25.3 %all_to_all.27.parts = bf16[8,4,32,256]{3,2,1,0:T(8,128)(2,1)S(1)} all-to-all(bf16[8,4,32,256]{3,2,1,0:T(8,128)(2,1)S(1)} %add_convert_fusion), channel_id=1, replica_groups=mesh['zh'=4,'y'=8,'core'=2,'x'=4,'zl'=2] {'y'}, dimensions={0} | all-to-all | bytes 1048576 | tf_op jit(solution)/shard_map/all_to_all | solution.py:36
  141.5 14.2 %all_to_all.28.parts = bf16[8,16,256]{2,1,0:T(8,128)(2,1)S(1)} all-to-all(bf16[8,16,256]{2,1,0:T(8,128)(2,1)S(1)} %bitcast.22), channel_id=1, replica_groups=mesh['zh'=4,'y'=8,'core'=2,'x'=4,'zl'=2] {'zh','zl'}, dimensions={0} | all-to-all | bytes 131072 | tf_op jit(solution)/shard_map/all_to_all | solution.py:36
  (27 shorter events, 5.3 us)
Async XLA Ops:
  2.2 36.1 %all-to-all-start = ((bf16[64,16,256]{2,1,0:T(8,128)(2,1)}), bf16[64,16,256]{2,1,0:T(8,128)(2,1)S(1)}, u32[]{:S(2)}, u32[]{:S(2)}) async-start(bf16[64,16,256]{2,1,0:T(8,128)(2,1)} %broadcast_in_dim.24), calls=%async_computation | async-start | bytes 1048576 | tf_op jit(solution)/shard_map/all_to_all | solution.py:36
  18.8 1.6 %copy-start = (bf16[1,128,8192]{2,1,0:T(8,128)(2,1)S(1)}, bf16[1,128,8192]{2,1,0:T(8,128)(2,1)}, u32[]{:S(2)}) copy-start(bf16[1,128,8192]{2,1,0:T(8,128)(2,1)} %param.5) | copy-start | bytes 6291460
  23.4 12.9 %collective-permute-start = (bf16[128,1024]{1,0:T(8,128)(2,1)S(1)}, bf16[128,1024]{1,0:T(8,128)(2,1)S(1)}, u32[]{:S(2)}, u32[]{:S(2)}) collective-permute-start(bf16[128,1024]{1,0:T(8,128)(2,1)S(1)} %get-tuple-element.13), channel_id=1, source_target_pairs={{0,2},{2,4},{4,6},{6,0},{1,3},{3,5},{5,7},{7,1},{8,10},{10,12},{12... | collective-permute-start | bytes 786440 | tf_op jit(solution)/shard_map/ppermute | solution.py:40
  25.8 12.5 %collective-permute-start.1 = (bf16[128,1024]{1,0:T(8,128)(2,1)S(1)}, bf16[128,1024]{1,0:T(8,128)(2,1)}, u32[]{:S(2)}, u32[]{:S(2)}) collective-permute-start(bf16[128,1024]{1,0:T(8,128)(2,1)S(1)} %get-tuple-element.14), channel_id=1, source_target_pairs={{0,6},{2,0},{4,2},{6,4},{1,7},{3,1},{5,3},{7,5},{8,14},{10,8},{12,... | collective-permute-start | bytes 786440 | tf_op jit(solution)/shard_map/ppermute | solution.py:40
  29.2 24.9 %collective-permute-start.3 = (bf16[2,128,1024]{2,1,0:T(8,128)(2,1)}, bf16[2,128,1024]{2,1,0:T(8,128)(2,1)S(1)}, u32[]{:S(2)}, u32[]{:S(2)}) collective-permute-start(bf16[2,128,1024]{2,1,0:T(8,128)(2,1)} %get-tuple-element.17), channel_id=1, source_target_pairs={{0,6},{2,0},{4,2},{6,4},{1,7},{3,1},{5,3},{7,5},{8,14},{10,8},{12,... | collective-permute-start | bytes 1572872 | tf_op jit(solution)/shard_map/ppermute | solution.py:40
  32.0 22.1 %collective-permute-start.4 = (bf16[2,128,1024]{2,1,0:T(8,128)(2,1)S(1)}, bf16[2,128,1024]{2,1,0:T(8,128)(2,1)S(1)}, u32[]{:S(2)}, u32[]{:S(2)}) collective-permute-start(bf16[2,128,1024]{2,1,0:T(8,128)(2,1)S(1)} %get-tuple-element.18), channel_id=1, source_target_pairs={{0,2},{2,4},{4,6},{6,0},{1,3},{3,5},{5,7},{7,1},{8,10},{10,12},{12... | collective-permute-start | bytes 1572872 | tf_op jit(solution)/shard_map/ppermute | solution.py:40
  38.2 15.9 %collective-permute-start.2 = (bf16[64,16,256]{2,1,0:T(8,128)(2,1)S(1)}, bf16[64,16,256]{2,1,0:T(8,128)(2,1)S(1)}, u32[]{:S(2)}, u32[]{:S(2)}) collective-permute-start(bf16[64,16,256]{2,1,0:T(8,128)(2,1)S(1)} %all-to-all-done.weight), channel_id=1, source_target_pairs={{0,8},{8,0},{1,9},{9,1},{2,10},{10,2},{3,11},{11,3},{4,12},{12,4},... | collective-permute-start | bytes 1572872 | tf_op jit(solution)/shard_map/ppermute | solution.py:49
  40.1 11.9 %collective-permute-start.5 = (bf16[128,1024]{1,0:T(8,128)(2,1)S(1)}, bf16[128,1024]{1,0:T(8,128)(2,1)S(1)}, u32[]{:S(2)}, u32[]{:S(2)}) collective-permute-start(bf16[128,1024]{1,0:T(8,128)(2,1)S(1)} %collective-permute-done), channel_id=1, source_target_pairs={{0,2},{2,4},{4,6},{6,0},{1,3},{3,5},{5,7},{7,1},{8,10},{10,12},{12... | collective-permute-start | bytes 786440 | tf_op jit(solution)/shard_map/ppermute | solution.py:40
  42.3 11.8 %collective-permute-start.6 = (bf16[128,1024]{1,0:T(8,128)(2,1)}, bf16[128,1024]{1,0:T(8,128)(2,1)S(1)}, u32[]{:S(2)}, u32[]{:S(2)}) collective-permute-start(bf16[128,1024]{1,0:T(8,128)(2,1)} %collective-permute-done.1), channel_id=1, source_target_pairs={{0,6},{2,0},{4,2},{6,4},{1,7},{3,1},{5,3},{7,5},{8,14},{10,8},{12,... | collective-permute-start | bytes 786440 | tf_op jit(solution)/shard_map/ppermute | solution.py:40
  54.1 23.4 %copy-start.1 = (bf16[1,128,2048]{2,1,0:T(8,128)(2,1)S(1)}, bf16[1,128,2048]{2,1,0:T(8,128)(2,1)}, u32[]{:S(2)}) copy-start(bf16[1,128,2048]{2,1,0:T(8,128)(2,1)} %param.6) | copy-start | bytes 1572868
  54.1 23.4 %copy-start.3 = (s32[1,32]{1,0:T(1,128)S(1)}, s32[1,32]{1,0:T(1,128)}, u32[]{:S(2)}) copy-start(s32[1,32]{1,0:T(1,128)} %lengths.1) | copy-start | bytes 388
  64.4 7.8 %collective-permute-start.8 = (bf16[128,256]{1,0:T(8,128)(2,1)S(1)}, bf16[128,256]{1,0:T(8,128)(2,1)S(1)}, u32[]{:S(2)}, u32[]{:S(2)}) collective-permute-start(bf16[128,256]{1,0:T(8,128)(2,1)S(1)} %summed.3.own), channel_id=1, source_target_pairs={{0,32},{16,48},{32,64},{48,80},{64,96},{80,112},{96,128},{112,144}... | collective-permute-start | bytes 196616 | tf_op jit(solution)/shard_map/ppermute | solution.py:45
  68.7 5.3 %collective-permute-start.7 = (bf16[128,256]{1,0:T(8,128)(2,1)S(1)}, bf16[128,256]{1,0:T(8,128)(2,1)S(1)}, u32[]{:S(2)}, u32[]{:S(2)}) collective-permute-start(bf16[128,256]{1,0:T(8,128)(2,1)S(1)} %summed.3.own), channel_id=1, source_target_pairs={{0,16},{16,32},{32,48},{48,64},{64,80},{80,96},{96,112},{112,128},... | collective-permute-start | bytes 196616 | tf_op jit(solution)/shard_map/ppermute | solution.py:45
  74.1 3.3 %collective-permute-start.9 = (bf16[3,128,256]{2,1,0:T(8,128)(2,1)S(1)}, bf16[3,128,256]{2,1,0:T(8,128)(2,1)S(1)}, u32[]{:S(2)}, u32[]{:S(2)}) collective-permute-start(bf16[3,128,256]{2,1,0:T(8,128)(2,1)S(1)} %pad_maximum_fusion), channel_id=1, source_target_pairs={{0,8},{8,0},{1,9},{9,1},{2,10},{10,2},{3,11},{11,3},{4,12},{12,4},... | collective-permute-start | bytes 589832 | tf_op jit(solution)/shard_map/ppermute | solution.py:49
  77.5 1.0 copy-start.2
  86.5 3.2 %collective-permute-start.10 = (bf16[2,128,256]{2,1,0:T(8,128)(2,1)S(1)}, bf16[2,128,256]{2,1,0:T(8,128)(2,1)S(1)}, u32[]{:S(2)}, u32[]{:S(2)}) collective-permute-start(bf16[2,128,256]{2,1,0:T(8,128)(2,1)S(1)} %get-tuple-element.22), channel_id=1, source_target_pairs={{0,8},{8,0},{1,9},{9,1},{2,10},{10,2},{3,11},{11,3},{4,12},{12,4},... | collective-permute-start | bytes 393224 | tf_op jit(solution)/shard_map/ppermute | solution.py:49
  89.8 6.9 %collective-permute-start.11 = (bf16[128,256]{1,0:T(8,128)(2,1)S(1)}, bf16[128,256]{1,0:T(8,128)(2,1)S(1)}, u32[]{:S(2)}, u32[]{:S(2)}) collective-permute-start(bf16[128,256]{1,0:T(8,128)(2,1)S(1)} %get-tuple-element.23), channel_id=1, source_target_pairs={{16,0},{32,16},{48,32},{64,48},{80,64},{96,80},{112,96},{128,112},... | collective-permute-start | bytes 196616 | tf_op jit(solution)/shard_map/ppermute | solution.py:45
  91.1 10.7 %collective-permute-start.12 = (bf16[128,256]{1,0:T(8,128)(2,1)S(1)}, bf16[128,256]{1,0:T(8,128)(2,1)S(1)}, u32[]{:S(2)}, u32[]{:S(2)}) collective-permute-start(bf16[128,256]{1,0:T(8,128)(2,1)S(1)} %get-tuple-element.24), channel_id=1, source_target_pairs={{32,0},{48,16},{64,32},{80,48},{96,64},{112,80},{128,96},{144,112}... | collective-permute-start | bytes 196616 | tf_op jit(solution)/shard_map/ppermute | solution.py:45
  112.1 3.8 %collective-permute-start.13 = (bf16[8,4,32,256]{3,2,1,0:T(8,128)(2,1)S(1)}, bf16[8,4,32,256]{3,2,1,0:T(8,128)(2,1)S(1)}, u32[]{:S(2)}, u32[]{:S(2)}) collective-permute-start(bf16[8,4,32,256]{3,2,1,0:T(8,128)(2,1)S(1)} %weight_grad.3), channel_id=1, source_target_pairs={{0,8},{8,0},{1,9},{9,1},{2,10},{10,2},{3,11},{11,3},{4,12},{12,4},... | collective-permute-start | bytes 1572872 | tf_op jit(solution)/shard_map/ppermute | solution.py:49

commit v4 on v3

--- a/solution.py
+++ b/solution.py
@@ -7,17 +7,20 @@
 from jax.experimental.pallas import tpu as pltpu
 from jax.sharding import Mesh, PartitionSpec as P
 
-AXES = ("zh", "y", "core", "x", "zl")
-CTX = ("zh", "y", "core")
+AXES = ("zh", "yh", "yl", "core", "x", "zl")
+CTX = ("zh", "yh", "yl", "core")
+CHIP = ("zh", "yh", "yl")
 DP = ("x", "zl")
-ZH, Y, CORE, X, ZL = 4, 8, 2, 4, 2
-CHIPS = ZH * Y
+ZH, YH, YL, CORE, X, ZL = 4, 4, 2, 2, 4, 2
+CHIPS = ZH * YH * YL
 COUNT = 128
 HEAD = 128
 WIDTH = 2 * HEAD
 BF16, F32 = jnp.bfloat16, jnp.float32
+TOGETHER = 8
 LOG2E = 1.4426950408889634
-VMEM_LIMIT = 40 << 20
+VMEM_LIMIT = 20 << 20
+SMALL_LIMIT = 8 << 20
 
 
 def vmem():
@@ -28,8 +31,20 @@
     return pl.BlockSpec(memory_space=pltpu.SMEM)
 
 
-def params():
-    return pltpu.CompilerParams(vmem_limit_bytes=VMEM_LIMIT)
+def params(limit=VMEM_LIMIT):
+    return pltpu.CompilerParams(vmem_limit_bytes=limit)
+
+
+def small_call(kernel, *args, outs, name, places=0):
+    return pl.pallas_call(
+        kernel,
+        in_specs=[smem()] * places + [vmem()] * (len(args) - places),
+        out_specs=[vmem()] * len(outs),
+        out_shape=[jax.ShapeDtypeStruct(shape, kind) for shape, kind in outs],
+        compiler_params=params(SMALL_LIMIT),
+        cost_estimate=pl.CostEstimate(flops=1 << 18, bytes_accessed=1 << 19, transcendentals=0),
+        name=name,
+    )(*args)
 
 
 def exchanged(blocks, axes):
@@ -42,7 +57,7 @@
 
 def to_chip(block, hop):
     chips = range(CHIPS)
-    return lax.ppermute(block, ("zh", "y"), [(i, i + hop) for i in chips if i + hop in chips])
+    return lax.ppermute(block, CHIP, [(i, i + hop) for i in chips if i + hop in chips])
 
 
 def to_other_core(block):
@@ -98,25 +113,26 @@
     return [(0, own[half]), (1, after[half]), (3, before[half]), (2, (over, under)[half][...])]
 
 
-def project_kernel(place, weight, weight_other, own, after, before, over, under, out):
+def project_kernel(place, weight, weight_other, own, after, before, over, under, early_q, early_g, out):
+    del early_q, early_g
     refs = (own, after, before, over, under)
-    rows = [w[...].reshape(ZH * Y * 32, WIDTH) for w in (weight, weight_other)]
+    rows = [w[...].reshape(CHIPS * 32, WIDTH) for w in (weight, weight_other)]
     for (step, first), (_, second) in zip(halves(refs, 0), halves(refs, 1)):
         part = jnp.dot(first, rows[0], preferred_element_type=F32)
         part += jnp.dot(second, rows[1], preferred_element_type=F32)
         out[(place[1] + step) % X] = part.astype(BF16)
 
 
-def project(place, weight, weight_other, pieces):
+def project(place, weight, weight_other, pieces, *early):
     return pl.pallas_call(
         project_kernel,
-        in_specs=[smem()] + [vmem()] * 7,
+        in_specs=[smem()] + [vmem()] * 9,
         out_specs=vmem(),
         out_shape=jax.ShapeDtypeStruct((X, COUNT, WIDTH), BF16),
         compiler_params=params(),
         cost_estimate=pl.CostEstimate(flops=1 << 29, bytes_accessed=3 << 20, transcendentals=0),
         name="project",
-    )(place, weight, weight_other, *pieces)
+    )(place, weight, weight_other, *pieces, *early)
 
 
 def weight_grad_kernel(half, place, grads, own, after, before, over, under, out, total):
@@ -128,10 +144,12 @@
         jnp.concatenate(turned, axis=1), jnp.concatenate(rows, axis=0), preferred_element_type=F32
     )
     for four in range(CHIPS // 4):
-        block = total[:, four * 128 : four * 128 + 128].T
+        block = total[:, four * 128 : four * 128 + 128].T.astype(BF16)
         for i in range(4):
-            zh, y = divmod(four * 4 + i, Y)
-            out[y, zh] = block[i * 32 : i * 32 + 32].astype(BF16)
+            far, yl = divmod(four * 4 + i, YL)
+            for zl in range(ZL):
+                row = i * 32 + zl * 16
+                out[yl * ZL + zl, far] = block[row : row + 16]
 
 
 def weight_grad_parts(half, place, grads, pieces):
@@ -140,7 +158,7 @@
         functools.partial(weight_grad_kernel, half),
         in_specs=[smem()] + [vmem()] * 6,
         out_specs=vmem(),
-        out_shape=jax.ShapeDtypeStruct((Y, ZH, 32, WIDTH), BF16),
+        out_shape=jax.ShapeDtypeStruct((YL * ZL, ZH * YH, 16, WIDTH), BF16),
         scratch_shapes=[pltpu.VMEM((WIDTH, features), F32)],
         compiler_params=params(),
         cost_estimate=pl.CostEstimate(flops=1 << 28, bytes_accessed=2 << 20, transcendentals=0),
@@ -156,18 +174,62 @@
 
 
 def summed(parts, kind):
-    return pl.pallas_call(
-        summed_kernel,
-        in_specs=[vmem()],
-        out_specs=vmem(),
-        out_shape=jax.ShapeDtypeStruct(parts.shape[1:], kind),
-        compiler_params=params(),
-        name="summed",
-    )(parts)
+    return small_call(summed_kernel, parts, outs=[(parts.shape[1:], kind)], name="summed")[0]
+
+
+def spread_kernel(block, out):
+    for i in range(out.shape[0]):
+        out[i] = block[...]
+
+
+def spread(block, count):
+    return small_call(spread_kernel, block, outs=[((count,) + block.shape, block.dtype)], name="spread")[0]
+
+
+def stacked_kernel(*refs):
+    for i, block in enumerate(refs[:-1]):
+        refs[-1][i] = block[...]
+
+
+def stacked(*blocks):
+    shape = (len(blocks),) + blocks[0].shape
+    return small_call(stacked_kernel, *blocks, outs=[(shape, blocks[0].dtype)], name="stacked")[0]
+
+
+def added_kernel(one, other, out):
+    out[...] = (one[...].astype(F32) + other[...].astype(F32)).astype(BF16)
+
+
+def added(one, other):
+    return small_call(added_kernel, one, other, outs=[(one.shape, BF16)], name="added")[0]
+
+
+def homeward_kernel(place, own, back, total_own, near, far):
+    first = place[0] == 0
+    zero, one = back[0].astype(F32), back[1].astype(F32)
+    total_own[...] = own[0] + jnp.where(first, zero, F32(0.0))
+    near[...] = (own[1] + jnp.where(first, one, zero)).astype(BF16)
+    far[...] = (own[2] + jnp.where(first, F32(0.0), one)).astype(BF16)
+
+
+def homeward(place, own, back):
+    block = own.shape[1:]
+    outs = [(block, F32), (block, BF16), (block, BF16)]
+    return small_call(homeward_kernel, place, own, back, outs=outs, name="homeward", places=1)
+
+
+def gathered_kernel(own, near, far, out):
+    total = (own[...] + near[...].astype(F32) + far[...].astype(F32)).astype(BF16)
+    for i in range(out.shape[0]):
+        out[i] = total
+
+
+def gathered(own, near, far, count):
+    return small_call(gathered_kernel, own, near, far, outs=[((count,) + own.shape, BF16)], name="gathered")[0]
 
 
 def attention_kernel(place, lengths, queries, grads, own, near, far, other, attn, grad_q, grad_own, grad_other):
-    core, chip_pos = place[0], place[1]
+    core, chip_pos = place[0], place[2]
     scale = HEAD ** -0.5
     blocks = [own[...], near[...], far[...], other[1 - core], other[2 - core]]
     starts = [chip_pos + core * COUNT - 2 * COUNT * i for i in range(3)]
@@ -188,12 +250,12 @@
         key_pos = start + row
         masks.append((key_pos >= doc_start) & (key_pos <= query_pos))
     cap = jnp.where(jnp.concatenate(masks, axis=0), F32(jnp.inf), F32(-1e30))
-    cap = jnp.concatenate([cap, cap], axis=1)
+    cap = jnp.concatenate([cap] * TOGETHER, axis=1)
 
     nt = (((1,), (1,)), ((), ()))
     total_k = total_v = None
-    for pair in range(queries.shape[1] // WIDTH):
-        cols = [slice((2 * pair + i) * HEAD, (2 * pair + i + 1) * HEAD) for i in range(2)]
+    for turn in range(queries.shape[1] // (TOGETHER * HEAD)):
+        cols = [slice(h * HEAD, (h + 1) * HEAD) for h in range(turn * TOGETHER, (turn + 1) * TOGETHER)]
         q = jnp.concatenate([queries[:, c] for c in cols], axis=0)
         g = jnp.concatenate([grads[:, c] for c in cols], axis=0)
         scores = lax.dot_general(keys, q, nt, preferred_element_type=F32) * F32(scale * LOG2E)
@@ -208,14 +270,14 @@
         out = jnp.dot(values_t, weights, preferred_element_type=F32) * inverse
         dq = jnp.dot(keys_t, dscores, preferred_element_type=F32) * (inverse * scale)
         out, dq = out.T.astype(BF16), dq.T.astype(BF16)
-        for i in range(2):
+        for i in range(TOGETHER):
             attn[:, cols[i]] = out[i * COUNT : (i + 1) * COUNT]
             grad_q[:, cols[i]] = dq[i * COUNT : (i + 1) * COUNT]
-        column = jnp.broadcast_to(inverse, (HEAD, WIDTH)).T
+        column = jnp.broadcast_to(inverse, (HEAD, TOGETHER * HEAD)).T
         part_k = jnp.dot(dscores, (q.astype(F32) * column).astype(BF16), preferred_element_type=F32)
         part_v = jnp.dot(weights, (g.astype(F32) * column).astype(BF16), preferred_element_type=F32)
-        total_k = part_k if pair == 0 else total_k + part_k
-        total_v = part_v if pair == 0 else total_v + part_v
+        total_k = part_k if turn == 0 else total_k + part_k
+        total_v = part_v if turn == 0 else total_v + part_v
     total = jnp.concatenate([total_k * scale, total_v], axis=1)
     for i in range(3):
         grad_own[i] = total[i * COUNT : (i + 1) * COUNT]
@@ -242,45 +304,36 @@
 
 
 def per_device(tokens_in, queries_in, kv_weight, out_grad, doc_lengths):
-    core = lax.axis_index("core")
-    chip = lax.axis_index(("zh", "y"))
-    team_place = jnp.stack([core, lax.axis_index("x")]).astype(jnp.int32)
-    ctx_place = jnp.stack([core, chip * (CORE * COUNT)]).astype(jnp.int32)
-
-    pieces = make_pieces(team_place, tokens_in[0])
-    ring = ZH * Y * ZL
-    weight = exchanged(jnp.broadcast_to(kv_weight[None], (ring,) + kv_weight.shape), ("zh", "y", "zl"))
-    pieces, halfway = team_pieces(*pieces)
+    core, chip = lax.axis_index("core"), lax.axis_index(CHIP)
+    place = jnp.stack([core, lax.axis_index("x"), chip * (CORE * COUNT)]).astype(jnp.int32)
+
+    cut = make_pieces(place, tokens_in[0])
+    ring = CHIPS * ZL
+    weight = exchanged(spread(kv_weight, ring), CHIP + ("zl",))
+    pieces, halfway = team_pieces(*cut)
     weight, _ = lax.optimization_barrier((weight, halfway))
     weight_other = to_other_core(weight)
-    part = exchanged(project(team_place, weight, weight_other, pieces), "x")
+    part = exchanged(project(place, weight, weight_other, pieces, queries_in[0], out_grad[0]), "x")
     kv = summed(part, BF16)
 
     near, far = to_chip(kv, 1), to_chip(kv, 2)
-    other = to_other_core(jnp.stack([kv, near, far]))
+    other = to_other_core(stacked(kv, near, far))
     attn, query_grad, grad_own, grad_other = attention(
-        ctx_place, doc_lengths, queries_in[0], out_grad[0], kv, near, far, other
+        place, doc_lengths, queries_in[0], out_grad[0], kv, near, far, other
     )
 
-    back = to_other_core(grad_other).astype(F32)
-    first = core == 0
-    far_grad = grad_own[2] + jnp.where(first, F32(0.0), back[1])
-    near_grad = grad_own[1] + jnp.where(first, back[1], back[0])
-    own_grad = grad_own[0] + jnp.where(first, back[0], F32(0.0))
-    far_grad, near_grad = to_chip(far_grad.astype(BF16), -2), to_chip(near_grad.astype(BF16), -1)
-    kv_grad = (own_grad + near_grad.astype(F32) + far_grad.astype(F32)).astype(BF16)
-
-    team_grad = exchanged(jnp.broadcast_to(kv_grad[None], (X,) + kv_grad.shape), "x")
-    theirs = to_other_core(weight_grad_parts(1, team_place, team_grad, pieces))
-    ours = weight_grad_parts(0, team_place, team_grad, pieces)
-    parts = exchanged((ours.astype(F32) + theirs.astype(F32)).astype(BF16), "y")
-    parts = summed(parts, BF16).reshape(ZH * ZL, 16, WIDTH)
-    weight_grad = summed(exchanged(parts, ("zh", "zl")), F32)
+    own_grad, near_grad, far_grad = homeward(place, grad_own, to_other_core(grad_other))
+    far_grad, near_grad = to_chip(far_grad, -2), to_chip(near_grad, -1)
+    team_grad = exchanged(gathered(own_grad, near_grad, far_grad, X), "x")
+    theirs = to_other_core(weight_grad_parts(1, place, team_grad, pieces))
+    ours = weight_grad_parts(0, place, team_grad, pieces)
+    parts = exchanged(added(ours, theirs), ("yl", "zl"))
+    weight_grad = summed(exchanged(summed(parts, BF16), ("zh", "yh")), F32)
     return attn[None], query_grad[None], weight_grad
 
 
 def solution(mesh):
-    fine = Mesh(mesh.devices.reshape(ZH, Y, CORE, X, ZL), AXES)
+    fine = Mesh(mesh.devices.reshape(ZH, YH, YL, CORE, X, ZL), AXES)
     return jax.shard_map(
         per_device,
         mesh=fine,

time: 158 us -> 153 us (0.968)
  blocking collectives: 57.6 us -> 53.9 us
  local copies, waits for them, and re-layouts: 4.19 us -> 2.37 us
    all_to_all x4, blocking collectives: 57.6 us -> 53.9 us  [exchanged(): return lax.all_to_all(blocks, axes, 0, 0, tiled=False)]
    pallas_call x4 -> x9, Pallas kernels: 2 us -> 3.58 us  [the longest x8 2.31 us: small_call(): pl.pallas_call(kernel, in_specs=[smem()] * places + [vmem()] * (len(args)...]
where the time goes in v4:
time: 153 us; the launch traced here: 151 us
  blocking collectives  53.9 us (35%)
  starting transfers between devices  53.4 us (35%)
  waiting for transfers between devices  24.7 us (16%)
  Pallas kernels  15.5 us (10%)
  local copies, waits for them, and re-layouts  2.37 us (2%)
    all_to_all x4, blocking collectives, exchanged(): return lax.all_to_all(blocks, axes, 0, 0, tiled=False)  53.9 us
    ppermute x6, starting transfers between devices, to_team(): return lax.ppermute(piece, 'x', [(x, (x + step) % X) for x in range(X)])  18.7 us
    all_to_all x1, starting transfers between devices, exchanged(): return lax.all_to_all(blocks, axes, 0, 0, tiled=False)  16.6 us
    ppermute x4, waiting for transfers between devices, to_chip(): lax.ppermute(block, CHIP, [(i, i + hop) for i in chips if i + hop in chips])  11.4 us
    ppermute x4, starting transfers between devices, to_chip(): lax.ppermute(block, CHIP, [(i, i + hop) for i in chips if i + hop in chips])  10.3 us
    ppermute x6, waiting for transfers between devices, to_team(): return lax.ppermute(piece, 'x', [(x, (x + step) % X) for x in range(X)])  10 us
    ppermute x4, starting transfers between devices, to_other_core(): return lax.ppermute(block, 'core', [(0, 1), (1, 0)])  7.79 us
    pallas_call x1, Pallas kernels, attention(): pl.pallas_call(attention_kernel, in_specs=[smem(), smem()] + [vmem()] * 6...  6.6 us
  transfers between devices with their start and end apart: 15, of which 9 were waited for; matrix products, arithmetic and copies ran while one was open for 0% of the time, Pallas kernels for 3%

profile of v4, /device:TPU:6, one launch (start us, length us, event | category | flops | bytes accessed | tf_op | source)
XLA Modules:
  0.0 150.9 jit_solution(15199096901731165375)
XLA Ops:
  2.2 16.6 %all-to-all-start = ((bf16[64,16,256]{2,1,0:T(8,128)(2,1)}), bf16[64,16,256]{2,1,0:T(8,128)(2,1)S(1)}, u32[]{:S(2)}, u32[]{:S(2)}) async-start(bf16[64,16,256]{2,1,0:T(8,128)(2,1)} %spread.1), calls=%async_computation | async-start | bytes 1048576 | tf_op jit(solution)/shard_map/all_to_all | solution.py:51
  18.9 1.7 %copy-done.3 = bf16[1,128,8192]{2,1,0:T(8,128)(2,1)S(1)} copy-done((bf16[1,128,8192]{2,1,0:T(8,128)(2,1)S(1)}, bf16[1,128,8192]{2,1,0:T(8,128)(2,1)}, u32[]{:S(2)}) %copy-start.3) | copy-done | bytes 2097176
  20.5 3.1 %pieces.1 = (bf16[2,128,1024]{2,1,0:T(8,128)(2,1)S(1)}, bf16[2,128,1024]{2,1,0:T(8,128)(2,1)}, bf16[2,128,1024]{2,1,0:T(8,128)(2,1)}, bf16[128,1024]{1,0:T(8,128)(2,1)S(1)}, bf16[128,1024]{1,0:T(8,128)(2,1)S(1)}) custom-call(s32[3]{0:T(128)S(1)} %pad_add_fusion.place, bf16[128,8192]{1,0:T(8,128)(2,1)S(1)} %bitcast.12), custom_call_target="tpu_custom_call" | custom-call | flops 1073741824 | bytes 4194304 | tf_op jit(solution)/shard_map/pieces/pallas_call | solution.py:91
  23.6 2.4 %collective-permute-start = (bf16[128,1024]{1,0:T(8,128)(2,1)S(1)}, bf16[128,1024]{1,0:T(8,128)(2,1)S(1)}, u32[]{:S(2)}, u32[]{:S(2)}) collective-permute-start(bf16[128,1024]{1,0:T(8,128)(2,1)S(1)} %get-tuple-element.16), channel_id=1, source_target_pairs={{0,2},{2,4},{4,6},{6,0},{1,3},{3,5},{5,7},{7,1},{8,10},{10,12},{12... | collective-permute-start | bytes 786440 | tf_op jit(solution)/shard_map/ppermute | solution.py:55
  26.0 3.5 %collective-permute-start.1 = (bf16[128,1024]{1,0:T(8,128)(2,1)S(1)}, bf16[128,1024]{1,0:T(8,128)(2,1)}, u32[]{:S(2)}, u32[]{:S(2)}) collective-permute-start(bf16[128,1024]{1,0:T(8,128)(2,1)S(1)} %get-tuple-element.17), channel_id=1, source_target_pairs={{0,6},{2,0},{4,2},{6,4},{1,7},{3,1},{5,3},{7,5},{8,14},{10,8},{12,... | collective-permute-start | bytes 786440 | tf_op jit(solution)/shard_map/ppermute | solution.py:55
  29.5 2.7 %collective-permute-start.3 = (bf16[2,128,1024]{2,1,0:T(8,128)(2,1)}, bf16[2,128,1024]{2,1,0:T(8,128)(2,1)S(1)}, u32[]{:S(2)}, u32[]{:S(2)}) collective-permute-start(bf16[2,128,1024]{2,1,0:T(8,128)(2,1)} %get-tuple-element.20), channel_id=1, source_target_pairs={{0,6},{2,0},{4,2},{6,4},{1,7},{3,1},{5,3},{7,5},{8,14},{10,8},{12,... | collective-permute-start | bytes 1572872 | tf_op jit(solution)/shard_map/ppermute | solution.py:55
  32.2 4.3 %collective-permute-start.4 = (bf16[2,128,1024]{2,1,0:T(8,128)(2,1)}, bf16[2,128,1024]{2,1,0:T(8,128)(2,1)S(1)}, u32[]{:S(2)}, u32[]{:S(2)}) collective-permute-start(bf16[2,128,1024]{2,1,0:T(8,128)(2,1)} %get-tuple-element.21), channel_id=1, source_target_pairs={{0,2},{2,4},{4,6},{6,0},{1,3},{3,5},{5,7},{7,1},{8,10},{10,12},{12... | collective-permute-start | bytes 1572872 | tf_op jit(solution)/shard_map/ppermute | solution.py:55
  36.6 1.9 %collective-permute-done.1 = bf16[128,1024]{1,0:T(8,128)(2,1)} collective-permute-done((bf16[128,1024]{1,0:T(8,128)(2,1)S(1)}, bf16[128,1024]{1,0:T(8,128)(2,1)}, u32[]{:S(2)}, u32[]{:S(2)}) %collective-permute-start.1) | collective-permute-done | bytes 262176 | tf_op jit(solution)/shard_map/ppermute | solution.py:55
  38.5 1.9 %collective-permute-start.2 = (bf16[64,16,256]{2,1,0:T(8,128)(2,1)S(1)}, bf16[64,16,256]{2,1,0:T(8,128)(2,1)S(1)}, u32[]{:S(2)}, u32[]{:S(2)}) collective-permute-start(bf16[64,16,256]{2,1,0:T(8,128)(2,1)S(1)} %all-to-all-done.weight), channel_id=1, source_target_pairs={{0,8},{8,0},{1,9},{9,1},{2,10},{10,2},{3,11},{11,3},{4,12},{12,4},... | collective-permute-start | bytes 1572872 | tf_op jit(solution)/shard_map/ppermute | solution.py:64
  40.4 2.2 %collective-permute-start.5 = (bf16[128,1024]{1,0:T(8,128)(2,1)S(1)}, bf16[128,1024]{1,0:T(8,128)(2,1)S(1)}, u32[]{:S(2)}, u32[]{:S(2)}) collective-permute-start(bf16[128,1024]{1,0:T(8,128)(2,1)S(1)} %collective-permute-done), channel_id=1, source_target_pairs={{0,2},{2,4},{4,6},{6,0},{1,3},{3,5},{5,7},{7,1},{8,10},{10,12},{12... | collective-permute-start | bytes 786440 | tf_op jit(solution)/shard_map/ppermute | solution.py:55
  42.6 3.7 %collective-permute-start.6 = (bf16[128,1024]{1,0:T(8,128)(2,1)}, bf16[128,1024]{1,0:T(8,128)(2,1)S(1)}, u32[]{:S(2)}, u32[]{:S(2)}) collective-permute-start(bf16[128,1024]{1,0:T(8,128)(2,1)} %collective-permute-done.1), channel_id=1, source_target_pairs={{0,6},{2,0},{4,2},{6,4},{1,7},{3,1},{5,3},{7,5},{8,14},{10,8},{12,... | collective-permute-start | bytes 786440 | tf_op jit(solution)/shard_map/ppermute | solution.py:55
  46.2 6.2 %collective-permute-done.5.over = bf16[128,1024]{1,0:T(8,128)(2,1)S(1)} collective-permute-done((bf16[128,1024]{1,0:T(8,128)(2,1)S(1)}, bf16[128,1024]{1,0:T(8,128)(2,1)S(1)}, u32[]{:S(2)}, u32[]{:S(2)}) %collective-permute-start.5) | collective-permute-done | bytes 262176 | tf_op jit(solution)/shard_map/ppermute | solution.py:55
  52.5 1.9 %collective-permute-done.6.under = bf16[128,1024]{1,0:T(8,128)(2,1)S(1)} collective-permute-done((bf16[128,1024]{1,0:T(8,128)(2,1)}, bf16[128,1024]{1,0:T(8,128)(2,1)S(1)}, u32[]{:S(2)}, u32[]{:S(2)}) %collective-permute-start.6) | collective-permute-done | bytes 262176 | tf_op jit(solution)/shard_map/ppermute | solution.py:55
  54.4 1.3 project.1
  55.7 8.9 %all_to_all.25.parts = bf16[4,128,256]{2,1,0:T(8,128)(2,1)S(1)} all-to-all(bf16[4,128,256]{2,1,0:T(8,128)(2,1)S(1)} %project.1), channel_id=1, replica_groups=mesh['zh'=4,'yh'=4,'yl'=2,'core'=2,'x'=4,'zl'=2] {'x'}, dimensions={0} | all-to-all | bytes 524288 | tf_op jit(solution)/shard_map/all_to_all | solution.py:51
  64.6 4.4 %collective-permute-start.8 = (bf16[128,256]{1,0:T(8,128)(2,1)S(1)}, bf16[128,256]{1,0:T(8,128)(2,1)S(1)}, u32[]{:S(2)}, u32[]{:S(2)}) collective-permute-start(bf16[128,256]{1,0:T(8,128)(2,1)S(1)} %summed.3.refs_0_.own), channel_id=1, source_target_pairs={{0,32},{16,48},{32,64},{48,80},{64,96},{80,112},{96,128},{112,144}... | collective-permute-start | bytes 196616 | tf_op jit(solution)/shard_map/ppermute | solution.py:60
  69.0 3.4 %collective-permute-start.7 = (bf16[128,256]{1,0:T(8,128)(2,1)S(1)}, bf16[128,256]{1,0:T(8,128)(2,1)S(1)}, u32[]{:S(2)}, u32[]{:S(2)}) collective-permute-start(bf16[128,256]{1,0:T(8,128)(2,1)S(1)} %summed.3.refs_0_.own), channel_id=1, source_target_pairs={{0,16},{16,32},{32,48},{48,64},{64,80},{80,96},{96,112},{112,128},... | collective-permute-start | bytes 196616 | tf_op jit(solution)/shard_map/ppermute | solution.py:60
  72.4 1.9 %collective-permute-done.7.refs_1_.near = bf16[128,256]{1,0:T(8,128)(2,1)S(1)} collective-permute-done((bf16[128,256]{1,0:T(8,128)(2,1)S(1)}, bf16[128,256]{1,0:T(8,128)(2,1)S(1)}, u32[]{:S(2)}, u32[]{:S(2)}) %collective-permute-start.7) | collective-permute-done | bytes 65568 | tf_op jit(solution)/shard_map/ppermute | solution.py:60
  74.3 1.9 %collective-permute-start.9 = (bf16[3,128,256]{2,1,0:T(8,128)(2,1)S(1)}, bf16[3,128,256]{2,1,0:T(8,128)(2,1)S(1)}, u32[]{:S(2)}, u32[]{:S(2)}) collective-permute-start(bf16[3,128,256]{2,1,0:T(8,128)(2,1)S(1)} %stacked.1), channel_id=1, source_target_pairs={{0,8},{8,0},{1,9},{9,1},{2,10},{10,2},{3,11},{11,3},{4,12},{12,4},... | collective-permute-start | bytes 589832 | tf_op jit(solution)/shard_map/ppermute | solution.py:64
  76.3 1.4 collective-permute-done.9.other
  77.7 6.6 %attention.1 = (bf16[128,2048]{1,0:T(8,128)(2,1)}, bf16[128,2048]{1,0:T(8,128)(2,1)}, f32[3,128,256]{2,1,0:T(8,128)S(1)}, bf16[2,128,256]{2,1,0:T(8,128)(2,1)S(1)}) custom-call(s32[3]{0:T(128)S(1)} %pad_add_fusion.place, s32[1,32]{1,0:T(1,128)S(1)} %copy-done.4, bf16[128,2048]{1,0:T(8,128)(2,1)S(1)} %bitcast.9, bf16[128,2048]{1,0:T(8,128)(2,1)S(1)} %bitcast.11, ...), custom_call_target="tpu_custom_call" | custom-call | flops 2147483648 | bytes 3145728 | tf_op jit(solution)/shard_map/attention/pallas_call | solution.py:290
  84.3 2.0 %collective-permute-start.10 = (bf16[2,128,256]{2,1,0:T(8,128)(2,1)S(1)}, bf16[2,128,256]{2,1,0:T(8,128)(2,1)S(1)}, u32[]{:S(2)}, u32[]{:S(2)}) collective-permute-start(bf16[2,128,256]{2,1,0:T(8,128)(2,1)S(1)} %get-tuple-element.25), channel_id=1, source_target_pairs={{0,8},{8,0},{1,9},{9,1},{2,10},{10,2},{3,11},{11,3},{4,12},{12,4},... | collective-permute-start | bytes 393224 | tf_op jit(solution)/shard_map/ppermute | solution.py:64
  86.3 1.2 collective-permute-done.10.back
  88.1 1.3 collective-permute-start.11
  89.4 1.3 collective-permute-start.12
  90.7 4.3 %collective-permute-done.11.near = bf16[128,256]{1,0:T(8,128)(2,1)S(1)} collective-permute-done((bf16[128,256]{1,0:T(8,128)(2,1)S(1)}, bf16[128,256]{1,0:T(8,128)(2,1)S(1)}, u32[]{:S(2)}, u32[]{:S(2)}) %collective-permute-start.11) | collective-permute-done | bytes 65568 | tf_op jit(solution)/shard_map/ppermute | solution.py:60
  95.0 5.1 %collective-permute-done.12.far = bf16[128,256]{1,0:T(8,128)(2,1)S(1)} collective-permute-done((bf16[128,256]{1,0:T(8,128)(2,1)S(1)}, bf16[128,256]{1,0:T(8,128)(2,1)S(1)}, u32[]{:S(2)}, u32[]{:S(2)}) %collective-permute-start.12) | collective-permute-done | bytes 65568 | tf_op jit(solution)/shard_map/ppermute | solution.py:60
  100.2 9.1 %all_to_all.26.grads = bf16[4,128,256]{2,1,0:T(8,128)(2,1)S(1)} all-to-all(bf16[4,128,256]{2,1,0:T(8,128)(2,1)S(1)} %gathered.1), channel_id=1, replica_groups=mesh['zh'=4,'yh'=4,'yl'=2,'core'=2,'x'=4,'zl'=2] {'x'}, dimensions={0} | all-to-all | bytes 524288 | tf_op jit(solution)/shard_map/all_to_all | solution.py:51
  110.4 1.9 %collective-permute-start.13 = (bf16[4,16,16,256]{3,2,1,0:T(8,128)(2,1)S(1)}, bf16[4,16,16,256]{3,2,1,0:T(8,128)(2,1)S(1)}, u32[]{:S(2)}, u32[]{:S(2)}) collective-permute-start(bf16[4,16,16,256]{3,2,1,0:T(8,128)(2,1)S(1)} %weight_grad.3), channel_id=1, source_target_pairs={{0,8},{8,0},{1,9},{9,1},{2,10},{10,2},{3,11},{11,3},{4,12},{12,4},... | collective-permute-start | bytes 1572872 | tf_op jit(solution)/shard_map/ppermute | solution.py:64
  112.3 1.1 weight_grad.2.one
  114.3 11.5 %all_to_all.27.parts = bf16[4,16,16,256]{3,2,1,0:T(8,128)(2,1)S(1)} all-to-all(bf16[4,16,16,256]{3,2,1,0:T(8,128)(2,1)S(1)} %added.1), channel_id=1, replica_groups=mesh['zh'=4,'yh'=4,'yl'=2,'core'=2,'x'=4,'zl'=2] {'yl','zl'}, dimensions={0} | all-to-all | bytes 1048576 | tf_op jit(solution)/shard_map/all_to_all | solution.py:51
  125.9 24.4 %all_to_all.28.parts = bf16[16,16,256]{2,1,0:T(8,128)(2,1)S(1)} all-to-all(bf16[16,16,256]{2,1,0:T(8,128)(2,1)S(1)} %summed.4), channel_id=1, replica_groups=mesh['zh'=4,'yh'=4,'yl'=2,'core'=2,'x'=4,'zl'=2] {'zh','yh'}, dimensions={0} | all-to-all | bytes 262144 | tf_op jit(solution)/shard_map/all_to_all | solution.py:51
  (26 shorter events, 5.0 us)
Async XLA Ops:
  0.6 0.7 copy-start.2
  2.2 36.3 %all-to-all-start = ((bf16[64,16,256]{2,1,0:T(8,128)(2,1)}), bf16[64,16,256]{2,1,0:T(8,128)(2,1)S(1)}, u32[]{:S(2)}, u32[]{:S(2)}) async-start(bf16[64,16,256]{2,1,0:T(8,128)(2,1)} %spread.1), calls=%async_computation | async-start | bytes 1048576 | tf_op jit(solution)/shard_map/all_to_all | solution.py:51
  18.8 35.6 %copy-start = (bf16[1,128,2048]{2,1,0:T(8,128)(2,1)S(1)}, bf16[1,128,2048]{2,1,0:T(8,128)(2,1)}, u32[]{:S(2)}) copy-start(bf16[1,128,2048]{2,1,0:T(8,128)(2,1)} %param.6) | copy-start | bytes 1572868
  18.8 35.6 %copy-start.1 = (bf16[1,128,2048]{2,1,0:T(8,128)(2,1)S(1)}, bf16[1,128,2048]{2,1,0:T(8,128)(2,1)}, u32[]{:S(2)}) copy-start(bf16[1,128,2048]{2,1,0:T(8,128)(2,1)} %param.8) | copy-start | bytes 1572868
  18.9 1.7 %copy-start.3 = (bf16[1,128,8192]{2,1,0:T(8,128)(2,1)S(1)}, bf16[1,128,8192]{2,1,0:T(8,128)(2,1)}, u32[]{:S(2)}) copy-start(bf16[1,128,8192]{2,1,0:T(8,128)(2,1)} %param.5) | copy-start | bytes 6291460
  23.6 12.9 %collective-permute-start = (bf16[128,1024]{1,0:T(8,128)(2,1)S(1)}, bf16[128,1024]{1,0:T(8,128)(2,1)S(1)}, u32[]{:S(2)}, u32[]{:S(2)}) collective-permute-start(bf16[128,1024]{1,0:T(8,128)(2,1)S(1)} %get-tuple-element.16), channel_id=1, source_target_pairs={{0,2},{2,4},{4,6},{6,0},{1,3},{3,5},{5,7},{7,1},{8,10},{10,12},{12... | collective-permute-start | bytes 786440 | tf_op jit(solution)/shard_map/ppermute | solution.py:55
  26.0 12.5 %collective-permute-start.1 = (bf16[128,1024]{1,0:T(8,128)(2,1)S(1)}, bf16[128,1024]{1,0:T(8,128)(2,1)}, u32[]{:S(2)}, u32[]{:S(2)}) collective-permute-start(bf16[128,1024]{1,0:T(8,128)(2,1)S(1)} %get-tuple-element.17), channel_id=1, source_target_pairs={{0,6},{2,0},{4,2},{6,4},{1,7},{3,1},{5,3},{7,5},{8,14},{10,8},{12,... | collective-permute-start | bytes 786440 | tf_op jit(solution)/shard_map/ppermute | solution.py:55
  29.5 24.9 %collective-permute-start.3 = (bf16[2,128,1024]{2,1,0:T(8,128)(2,1)}, bf16[2,128,1024]{2,1,0:T(8,128)(2,1)S(1)}, u32[]{:S(2)}, u32[]{:S(2)}) collective-permute-start(bf16[2,128,1024]{2,1,0:T(8,128)(2,1)} %get-tuple-element.20), channel_id=1, source_target_pairs={{0,6},{2,0},{4,2},{6,4},{1,7},{3,1},{5,3},{7,5},{8,14},{10,8},{12,... | collective-permute-start | bytes 1572872 | tf_op jit(solution)/shard_map/ppermute | solution.py:55
  32.2 22.1 %collective-permute-start.4 = (bf16[2,128,1024]{2,1,0:T(8,128)(2,1)}, bf16[2,128,1024]{2,1,0:T(8,128)(2,1)S(1)}, u32[]{:S(2)}, u32[]{:S(2)}) collective-permute-start(bf16[2,128,1024]{2,1,0:T(8,128)(2,1)} %get-tuple-element.21), channel_id=1, source_target_pairs={{0,2},{2,4},{4,6},{6,0},{1,3},{3,5},{5,7},{7,1},{8,10},{10,12},{12... | collective-permute-start | bytes 1572872 | tf_op jit(solution)/shard_map/ppermute | solution.py:55
  38.5 15.9 %collective-permute-start.2 = (bf16[64,16,256]{2,1,0:T(8,128)(2,1)S(1)}, bf16[64,16,256]{2,1,0:T(8,128)(2,1)S(1)}, u32[]{:S(2)}, u32[]{:S(2)}) collective-permute-start(bf16[64,16,256]{2,1,0:T(8,128)(2,1)S(1)} %all-to-all-done.weight), channel_id=1, source_target_pairs={{0,8},{8,0},{1,9},{9,1},{2,10},{10,2},{3,11},{11,3},{4,12},{12,4},... | collective-permute-start | bytes 1572872 | tf_op jit(solution)/shard_map/ppermute | solution.py:64
  40.4 12.1 %collective-permute-start.5 = (bf16[128,1024]{1,0:T(8,128)(2,1)S(1)}, bf16[128,1024]{1,0:T(8,128)(2,1)S(1)}, u32[]{:S(2)}, u32[]{:S(2)}) collective-permute-start(bf16[128,1024]{1,0:T(8,128)(2,1)S(1)} %collective-permute-done), channel_id=1, source_target_pairs={{0,2},{2,4},{4,6},{6,0},{1,3},{3,5},{5,7},{7,1},{8,10},{10,12},{12... | collective-permute-start | bytes 786440 | tf_op jit(solution)/shard_map/ppermute | solution.py:55
  42.6 11.8 %collective-permute-start.6 = (bf16[128,1024]{1,0:T(8,128)(2,1)}, bf16[128,1024]{1,0:T(8,128)(2,1)S(1)}, u32[]{:S(2)}, u32[]{:S(2)}) collective-permute-start(bf16[128,1024]{1,0:T(8,128)(2,1)} %collective-permute-done.1), channel_id=1, source_target_pairs={{0,6},{2,0},{4,2},{6,4},{1,7},{3,1},{5,3},{7,5},{8,14},{10,8},{12,... | collective-permute-start | bytes 786440 | tf_op jit(solution)/shard_map/ppermute | solution.py:55
  54.4 23.3 %copy-start.4 = (s32[1,32]{1,0:T(1,128)S(1)}, s32[1,32]{1,0:T(1,128)}, u32[]{:S(2)}) copy-start(s32[1,32]{1,0:T(1,128)} %lengths.1) | copy-start | bytes 388
  64.6 7.8 %collective-permute-start.8 = (bf16[128,256]{1,0:T(8,128)(2,1)S(1)}, bf16[128,256]{1,0:T(8,128)(2,1)S(1)}, u32[]{:S(2)}, u32[]{:S(2)}) collective-permute-start(bf16[128,256]{1,0:T(8,128)(2,1)S(1)} %summed.3.refs_0_.own), channel_id=1, source_target_pairs={{0,32},{16,48},{32,64},{48,80},{64,96},{80,112},{96,128},{112,144}... | collective-permute-start | bytes 196616 | tf_op jit(solution)/shard_map/ppermute | solution.py:60
  69.0 5.3 %collective-permute-start.7 = (bf16[128,256]{1,0:T(8,128)(2,1)S(1)}, bf16[128,256]{1,0:T(8,128)(2,1)S(1)}, u32[]{:S(2)}, u32[]{:S(2)}) collective-permute-start(bf16[128,256]{1,0:T(8,128)(2,1)S(1)} %summed.3.refs_0_.own), channel_id=1, source_target_pairs={{0,16},{16,32},{32,48},{48,64},{64,80},{80,96},{96,112},{112,128},... | collective-permute-start | bytes 196616 | tf_op jit(solution)/shard_map/ppermute | solution.py:60
  74.3 3.3 %collective-permute-start.9 = (bf16[3,128,256]{2,1,0:T(8,128)(2,1)S(1)}, bf16[3,128,256]{2,1,0:T(8,128)(2,1)S(1)}, u32[]{:S(2)}, u32[]{:S(2)}) collective-permute-start(bf16[3,128,256]{2,1,0:T(8,128)(2,1)S(1)} %stacked.1), channel_id=1, source_target_pairs={{0,8},{8,0},{1,9},{9,1},{2,10},{10,2},{3,11},{11,3},{4,12},{12,4},... | collective-permute-start | bytes 589832 | tf_op jit(solution)/shard_map/ppermute | solution.py:64
  84.3 3.2 %collective-permute-start.10 = (bf16[2,128,256]{2,1,0:T(8,128)(2,1)S(1)}, bf16[2,128,256]{2,1,0:T(8,128)(2,1)S(1)}, u32[]{:S(2)}, u32[]{:S(2)}) collective-permute-start(bf16[2,128,256]{2,1,0:T(8,128)(2,1)S(1)} %get-tuple-element.25), channel_id=1, source_target_pairs={{0,8},{8,0},{1,9},{9,1},{2,10},{10,2},{3,11},{11,3},{4,12},{12,4},... | collective-permute-start | bytes 393224 | tf_op jit(solution)/shard_map/ppermute | solution.py:64
  88.1 6.9 %collective-permute-start.11 = (bf16[128,256]{1,0:T(8,128)(2,1)S(1)}, bf16[128,256]{1,0:T(8,128)(2,1)S(1)}, u32[]{:S(2)}, u32[]{:S(2)}) collective-permute-start(bf16[128,256]{1,0:T(8,128)(2,1)S(1)} %get-tuple-element.27), channel_id=1, source_target_pairs={{16,0},{32,16},{48,32},{64,48},{80,64},{96,80},{112,96},{128,112},... | collective-permute-start | bytes 196616 | tf_op jit(solution)/shard_map/ppermute | solution.py:60
  89.4 10.7 %collective-permute-start.12 = (bf16[128,256]{1,0:T(8,128)(2,1)S(1)}, bf16[128,256]{1,0:T(8,128)(2,1)S(1)}, u32[]{:S(2)}, u32[]{:S(2)}) collective-permute-start(bf16[128,256]{1,0:T(8,128)(2,1)S(1)} %get-tuple-element.28), channel_id=1, source_target_pairs={{32,0},{48,16},{64,32},{80,48},{96,64},{112,80},{128,96},{144,112}... | collective-permute-start | bytes 196616 | tf_op jit(solution)/shard_map/ppermute | solution.py:60
  110.4 3.8 %collective-permute-start.13 = (bf16[4,16,16,256]{3,2,1,0:T(8,128)(2,1)S(1)}, bf16[4,16,16,256]{3,2,1,0:T(8,128)(2,1)S(1)}, u32[]{:S(2)}, u32[]{:S(2)}) collective-permute-start(bf16[4,16,16,256]{3,2,1,0:T(8,128)(2,1)S(1)} %weight_grad.3), channel_id=1, source_target_pairs={{0,8},{8,0},{1,9},{9,1},{2,10},{10,2},{3,11},{11,3},{4,12},{12,4},... | collective-permute-start | bytes 1572872 | tf_op jit(solution)/shard_map/ppermute | solution.py:64

commit v5 on v4

--- a/solution.py
+++ b/solution.py
@@ -17,7 +17,7 @@
 HEAD = 128
 WIDTH = 2 * HEAD
 BF16, F32 = jnp.bfloat16, jnp.float32
-TOGETHER = 8
+TOGETHER = 16
 LOG2E = 1.4426950408889634
 VMEM_LIMIT = 20 << 20
 SMALL_LIMIT = 8 << 20
@@ -311,7 +311,7 @@
     ring = CHIPS * ZL
     weight = exchanged(spread(kv_weight, ring), CHIP + ("zl",))
     pieces, halfway = team_pieces(*cut)
-    weight, _ = lax.optimization_barrier((weight, halfway))
+    weight, _ = lax.optimization_barrier((weight, halfway[0]))
     weight_other = to_other_core(weight)
     part = exchanged(project(place, weight, weight_other, pieces, queries_in[0], out_grad[0]), "x")
     kv = summed(part, BF16)

time: 153 us -> 152 us (level)
  no operation moved by 1% of the time
where the time goes in v5:
time: 152 us; the launch traced here: 150 us
  blocking collectives  54.6 us (36%)
  starting transfers between devices  53.2 us (35%)
  waiting for transfers between devices  23.9 us (16%)
  Pallas kernels  15.3 us (10%)
  local copies, waits for them, and re-layouts  2.37 us (2%)
    all_to_all x4, blocking collectives, exchanged(): return lax.all_to_all(blocks, axes, 0, 0, tiled=False)  54.6 us
    ppermute x6, starting transfers between devices, to_team(): return lax.ppermute(piece, 'x', [(x, (x + step) % X) for x in range(X)])  18.7 us
    all_to_all x1, starting transfers between devices, exchanged(): return lax.all_to_all(blocks, axes, 0, 0, tiled=False)  16.6 us
    ppermute x4, waiting for transfers between devices, to_chip(): lax.ppermute(block, CHIP, [(i, i + hop) for i in chips if i + hop in chips])  11.4 us
    ppermute x4, starting transfers between devices, to_chip(): lax.ppermute(block, CHIP, [(i, i + hop) for i in chips if i + hop in chips])  10.1 us
    ppermute x6, waiting for transfers between devices, to_team(): return lax.ppermute(piece, 'x', [(x, (x + step) % X) for x in range(X)])  8.65 us
    ppermute x4, starting transfers between devices, to_other_core(): return lax.ppermute(block, 'core', [(0, 1), (1, 0)])  7.79 us
    pallas_call x1, Pallas kernels, attention(): pl.pallas_call(attention_kernel, in_specs=[smem(), smem()] + [vmem()] * 6...  6.42 us
  transfers between devices with their start and end apart: 15, of which 9 were waited for; matrix products, arithmetic and copies ran while one was open for 0% of the time, Pallas kernels for 3%

profile of v5, /device:TPU:6, one launch (start us, length us, event | category | flops | bytes accessed | tf_op | source)
XLA Modules:
  0.0 150.3 jit_solution(12837133880353972539)
XLA Ops:
  2.2 16.6 %all-to-all-start = ((bf16[64,16,256]{2,1,0:T(8,128)(2,1)}), bf16[64,16,256]{2,1,0:T(8,128)(2,1)S(1)}, u32[]{:S(2)}, u32[]{:S(2)}) async-start(bf16[64,16,256]{2,1,0:T(8,128)(2,1)} %spread.1), calls=%async_computation | async-start | bytes 1048576 | tf_op jit(solution)/shard_map/all_to_all | solution.py:51
  18.9 1.7 %copy-done.3 = bf16[1,128,8192]{2,1,0:T(8,128)(2,1)S(1)} copy-done((bf16[1,128,8192]{2,1,0:T(8,128)(2,1)S(1)}, bf16[1,128,8192]{2,1,0:T(8,128)(2,1)}, u32[]{:S(2)}) %copy-start.3) | copy-done | bytes 2097176
  20.5 3.1 %pieces.1 = (bf16[2,128,1024]{2,1,0:T(8,128)(2,1)S(1)}, bf16[2,128,1024]{2,1,0:T(8,128)(2,1)}, bf16[2,128,1024]{2,1,0:T(8,128)(2,1)}, bf16[128,1024]{1,0:T(8,128)(2,1)S(1)}, bf16[128,1024]{1,0:T(8,128)(2,1)S(1)}) custom-call(s32[3]{0:T(128)S(1)} %pad_add_fusion.place, bf16[128,8192]{1,0:T(8,128)(2,1)S(1)} %bitcast.12), custom_call_target="tpu_custom_call" | custom-call | flops 1073741824 | bytes 4194304 | tf_op jit(solution)/shard_map/pieces/pallas_call | solution.py:91
  23.6 2.4 %collective-permute-start = (bf16[128,1024]{1,0:T(8,128)(2,1)S(1)}, bf16[128,1024]{1,0:T(8,128)(2,1)}, u32[]{:S(2)}, u32[]{:S(2)}) collective-permute-start(bf16[128,1024]{1,0:T(8,128)(2,1)S(1)} %get-tuple-element.16), channel_id=1, source_target_pairs={{0,2},{2,4},{4,6},{6,0},{1,3},{3,5},{5,7},{7,1},{8,10},{10,12},{12... | collective-permute-start | bytes 786440 | tf_op jit(solution)/shard_map/ppermute | solution.py:55
  26.0 3.5 %collective-permute-start.5 = (bf16[128,1024]{1,0:T(8,128)(2,1)S(1)}, bf16[128,1024]{1,0:T(8,128)(2,1)}, u32[]{:S(2)}, u32[]{:S(2)}) collective-permute-start(bf16[128,1024]{1,0:T(8,128)(2,1)S(1)} %get-tuple-element.21), channel_id=1, source_target_pairs={{0,6},{2,0},{4,2},{6,4},{1,7},{3,1},{5,3},{7,5},{8,14},{10,8},{12,... | collective-permute-start | bytes 786440 | tf_op jit(solution)/shard_map/ppermute | solution.py:55
  29.5 2.7 %collective-permute-start.2 = (bf16[2,128,1024]{2,1,0:T(8,128)(2,1)}, bf16[2,128,1024]{2,1,0:T(8,128)(2,1)S(1)}, u32[]{:S(2)}, u32[]{:S(2)}) collective-permute-start(bf16[2,128,1024]{2,1,0:T(8,128)(2,1)} %get-tuple-element.19), channel_id=1, source_target_pairs={{0,6},{2,0},{4,2},{6,4},{1,7},{3,1},{5,3},{7,5},{8,14},{10,8},{12,... | collective-permute-start | bytes 1572872 | tf_op jit(solution)/shard_map/ppermute | solution.py:55
  32.2 4.3 %collective-permute-start.3 = (bf16[2,128,1024]{2,1,0:T(8,128)(2,1)}, bf16[2,128,1024]{2,1,0:T(8,128)(2,1)S(1)}, u32[]{:S(2)}, u32[]{:S(2)}) collective-permute-start(bf16[2,128,1024]{2,1,0:T(8,128)(2,1)} %get-tuple-element.20), channel_id=1, source_target_pairs={{0,2},{2,4},{4,6},{6,0},{1,3},{3,5},{5,7},{7,1},{8,10},{10,12},{12... | collective-permute-start | bytes 1572872 | tf_op jit(solution)/shard_map/ppermute | solution.py:55
  37.0 1.9 %collective-permute-start.1 = (bf16[64,16,256]{2,1,0:T(8,128)(2,1)S(1)}, bf16[64,16,256]{2,1,0:T(8,128)(2,1)S(1)}, u32[]{:S(2)}, u32[]{:S(2)}) collective-permute-start(bf16[64,16,256]{2,1,0:T(8,128)(2,1)S(1)} %all-to-all-done.weight), channel_id=1, source_target_pairs={{0,8},{8,0},{1,9},{9,1},{2,10},{10,2},{3,11},{11,3},{4,12},{12,4},... | collective-permute-start | bytes 1572872 | tf_op jit(solution)/shard_map/ppermute | solution.py:64
  38.9 2.4 %collective-permute-start.4 = (bf16[128,1024]{1,0:T(8,128)(2,1)}, bf16[128,1024]{1,0:T(8,128)(2,1)S(1)}, u32[]{:S(2)}, u32[]{:S(2)}) collective-permute-start(bf16[128,1024]{1,0:T(8,128)(2,1)} %collective-permute-done), channel_id=1, source_target_pairs={{0,2},{2,4},{4,6},{6,0},{1,3},{3,5},{5,7},{7,1},{8,10},{10,12},{12... | collective-permute-start | bytes 786440 | tf_op jit(solution)/shard_map/ppermute | solution.py:55
  41.4 3.5 %collective-permute-start.6 = (bf16[128,1024]{1,0:T(8,128)(2,1)}, bf16[128,1024]{1,0:T(8,128)(2,1)S(1)}, u32[]{:S(2)}, u32[]{:S(2)}) collective-permute-start(bf16[128,1024]{1,0:T(8,128)(2,1)} %collective-permute-done.5), channel_id=1, source_target_pairs={{0,6},{2,0},{4,2},{6,4},{1,7},{3,1},{5,3},{7,5},{8,14},{10,8},{12,... | collective-permute-start | bytes 786440 | tf_op jit(solution)/shard_map/ppermute | solution.py:55
  44.8 7.7 %collective-permute-done.4.over = bf16[128,1024]{1,0:T(8,128)(2,1)S(1)} collective-permute-done((bf16[128,1024]{1,0:T(8,128)(2,1)}, bf16[128,1024]{1,0:T(8,128)(2,1)S(1)}, u32[]{:S(2)}, u32[]{:S(2)}) %collective-permute-start.4) | collective-permute-done | bytes 262176 | tf_op jit(solution)/shard_map/ppermute | solution.py:55
  52.5 0.9 collective-permute-done.6.under
  53.5 1.3 project.1
  54.8 9.7 %all_to_all.25.parts = bf16[4,128,256]{2,1,0:T(8,128)(2,1)S(1)} all-to-all(bf16[4,128,256]{2,1,0:T(8,128)(2,1)S(1)} %project.1), channel_id=1, replica_groups=mesh['zh'=4,'yh'=4,'yl'=2,'core'=2,'x'=4,'zl'=2] {'x'}, dimensions={0} | all-to-all | bytes 524288 | tf_op jit(solution)/shard_map/all_to_all | solution.py:51
  64.5 4.1 %collective-permute-start.8 = (bf16[128,256]{1,0:T(8,128)(2,1)S(1)}, bf16[128,256]{1,0:T(8,128)(2,1)S(1)}, u32[]{:S(2)}, u32[]{:S(2)}) collective-permute-start(bf16[128,256]{1,0:T(8,128)(2,1)S(1)} %summed.3.refs_0_.own), channel_id=1, source_target_pairs={{0,32},{16,48},{32,64},{48,80},{64,96},{80,112},{96,128},{112,144}... | collective-permute-start | bytes 196616 | tf_op jit(solution)/shard_map/ppermute | solution.py:60
  68.6 3.4 %collective-permute-start.7 = (bf16[128,256]{1,0:T(8,128)(2,1)S(1)}, bf16[128,256]{1,0:T(8,128)(2,1)S(1)}, u32[]{:S(2)}, u32[]{:S(2)}) collective-permute-start(bf16[128,256]{1,0:T(8,128)(2,1)S(1)} %summed.3.refs_0_.own), channel_id=1, source_target_pairs={{0,16},{16,32},{32,48},{48,64},{64,80},{80,96},{96,112},{112,128},... | collective-permute-start | bytes 196616 | tf_op jit(solution)/shard_map/ppermute | solution.py:60
  72.0 2.0 %collective-permute-done.7.refs_1_.near = bf16[128,256]{1,0:T(8,128)(2,1)S(1)} collective-permute-done((bf16[128,256]{1,0:T(8,128)(2,1)S(1)}, bf16[128,256]{1,0:T(8,128)(2,1)S(1)}, u32[]{:S(2)}, u32[]{:S(2)}) %collective-permute-start.7) | collective-permute-done | bytes 65568 | tf_op jit(solution)/shard_map/ppermute | solution.py:60
  74.0 1.9 %collective-permute-start.9 = (bf16[3,128,256]{2,1,0:T(8,128)(2,1)S(1)}, bf16[3,128,256]{2,1,0:T(8,128)(2,1)S(1)}, u32[]{:S(2)}, u32[]{:S(2)}) collective-permute-start(bf16[3,128,256]{2,1,0:T(8,128)(2,1)S(1)} %stacked.1), channel_id=1, source_target_pairs={{0,8},{8,0},{1,9},{9,1},{2,10},{10,2},{3,11},{11,3},{4,12},{12,4},... | collective-permute-start | bytes 589832 | tf_op jit(solution)/shard_map/ppermute | solution.py:64
  75.9 1.4 collective-permute-done.9.other
  77.3 6.4 %attention.1 = (bf16[128,2048]{1,0:T(8,128)(2,1)}, bf16[128,2048]{1,0:T(8,128)(2,1)}, f32[3,128,256]{2,1,0:T(8,128)S(1)}, bf16[2,128,256]{2,1,0:T(8,128)(2,1)S(1)}) custom-call(s32[3]{0:T(128)S(1)} %pad_add_fusion.place, s32[1,32]{1,0:T(1,128)S(1)} %copy-done.4, bf16[128,2048]{1,0:T(8,128)(2,1)S(1)} %bitcast.9, bf16[128,2048]{1,0:T(8,128)(2,1)S(1)} %bitcast.11, ...), custom_call_target="tpu_custom_call" | custom-call | flops 2147483648 | bytes 3145728 | tf_op jit(solution)/shard_map/attention/pallas_call | solution.py:290
  83.7 2.0 %collective-permute-start.10 = (bf16[2,128,256]{2,1,0:T(8,128)(2,1)S(1)}, bf16[2,128,256]{2,1,0:T(8,128)(2,1)S(1)}, u32[]{:S(2)}, u32[]{:S(2)}) collective-permute-start(bf16[2,128,256]{2,1,0:T(8,128)(2,1)S(1)} %get-tuple-element.25), channel_id=1, source_target_pairs={{0,8},{8,0},{1,9},{9,1},{2,10},{10,2},{3,11},{11,3},{4,12},{12,4},... | collective-permute-start | bytes 393224 | tf_op jit(solution)/shard_map/ppermute | solution.py:64
  85.8 1.2 collective-permute-done.10.back
  87.6 1.3 collective-permute-start.11
  88.9 1.3 collective-permute-start.12
  90.2 4.3 %collective-permute-done.11.near = bf16[128,256]{1,0:T(8,128)(2,1)S(1)} collective-permute-done((bf16[128,256]{1,0:T(8,128)(2,1)S(1)}, bf16[128,256]{1,0:T(8,128)(2,1)S(1)}, u32[]{:S(2)}, u32[]{:S(2)}) %collective-permute-start.11) | collective-permute-done | bytes 65568 | tf_op jit(solution)/shard_map/ppermute | solution.py:60
  94.4 5.1 %collective-permute-done.12.far = bf16[128,256]{1,0:T(8,128)(2,1)S(1)} collective-permute-done((bf16[128,256]{1,0:T(8,128)(2,1)S(1)}, bf16[128,256]{1,0:T(8,128)(2,1)S(1)}, u32[]{:S(2)}, u32[]{:S(2)}) %collective-permute-start.12) | collective-permute-done | bytes 65568 | tf_op jit(solution)/shard_map/ppermute | solution.py:60
  99.6 9.1 %all_to_all.26.grads = bf16[4,128,256]{2,1,0:T(8,128)(2,1)S(1)} all-to-all(bf16[4,128,256]{2,1,0:T(8,128)(2,1)S(1)} %gathered.1), channel_id=1, replica_groups=mesh['zh'=4,'yh'=4,'yl'=2,'core'=2,'x'=4,'zl'=2] {'x'}, dimensions={0} | all-to-all | bytes 524288 | tf_op jit(solution)/shard_map/all_to_all | solution.py:51
  108.7 1.1 weight_grad.3
  109.8 1.9 %collective-permute-start.13 = (bf16[4,16,16,256]{3,2,1,0:T(8,128)(2,1)S(1)}, bf16[4,16,16,256]{3,2,1,0:T(8,128)(2,1)S(1)}, u32[]{:S(2)}, u32[]{:S(2)}) collective-permute-start(bf16[4,16,16,256]{3,2,1,0:T(8,128)(2,1)S(1)} %weight_grad.3), channel_id=1, source_target_pairs={{0,8},{8,0},{1,9},{9,1},{2,10},{10,2},{3,11},{11,3},{4,12},{12,4},... | collective-permute-start | bytes 1572872 | tf_op jit(solution)/shard_map/ppermute | solution.py:64
  111.7 1.1 weight_grad.2.one
  113.7 11.5 %all_to_all.27.parts = bf16[4,16,16,256]{3,2,1,0:T(8,128)(2,1)S(1)} all-to-all(bf16[4,16,16,256]{3,2,1,0:T(8,128)(2,1)S(1)} %added.1), channel_id=1, replica_groups=mesh['zh'=4,'yh'=4,'yl'=2,'core'=2,'x'=4,'zl'=2] {'yl','zl'}, dimensions={0} | all-to-all | bytes 1048576 | tf_op jit(solution)/shard_map/all_to_all | solution.py:51
  125.3 24.4 %all_to_all.28.parts = bf16[16,16,256]{2,1,0:T(8,128)(2,1)S(1)} all-to-all(bf16[16,16,256]{2,1,0:T(8,128)(2,1)S(1)} %summed.4), channel_id=1, replica_groups=mesh['zh'=4,'yh'=4,'yl'=2,'core'=2,'x'=4,'zl'=2] {'zh','yh'}, dimensions={0} | all-to-all | bytes 262144 | tf_op jit(solution)/shard_map/all_to_all | solution.py:51
  (26 shorter events, 4.3 us)
Async XLA Ops:
  0.6 0.7 copy-start.2
  2.2 34.9 %all-to-all-start = ((bf16[64,16,256]{2,1,0:T(8,128)(2,1)}), bf16[64,16,256]{2,1,0:T(8,128)(2,1)S(1)}, u32[]{:S(2)}, u32[]{:S(2)}) async-start(bf16[64,16,256]{2,1,0:T(8,128)(2,1)} %spread.1), calls=%async_computation | async-start | bytes 1048576 | tf_op jit(solution)/shard_map/all_to_all | solution.py:51
  18.8 34.7 %copy-start = (bf16[1,128,2048]{2,1,0:T(8,128)(2,1)S(1)}, bf16[1,128,2048]{2,1,0:T(8,128)(2,1)}, u32[]{:S(2)}) copy-start(bf16[1,128,2048]{2,1,0:T(8,128)(2,1)} %param.6) | copy-start | bytes 1572868
  18.8 34.7 %copy-start.1 = (bf16[1,128,2048]{2,1,0:T(8,128)(2,1)S(1)}, bf16[1,128,2048]{2,1,0:T(8,128)(2,1)}, u32[]{:S(2)}) copy-start(bf16[1,128,2048]{2,1,0:T(8,128)(2,1)} %param.8) | copy-start | bytes 1572868
  18.9 1.7 %copy-start.3 = (bf16[1,128,8192]{2,1,0:T(8,128)(2,1)S(1)}, bf16[1,128,8192]{2,1,0:T(8,128)(2,1)}, u32[]{:S(2)}) copy-start(bf16[1,128,8192]{2,1,0:T(8,128)(2,1)} %param.5) | copy-start | bytes 6291460
  23.6 12.9 %collective-permute-start = (bf16[128,1024]{1,0:T(8,128)(2,1)S(1)}, bf16[128,1024]{1,0:T(8,128)(2,1)}, u32[]{:S(2)}, u32[]{:S(2)}) collective-permute-start(bf16[128,1024]{1,0:T(8,128)(2,1)S(1)} %get-tuple-element.16), channel_id=1, source_target_pairs={{0,2},{2,4},{4,6},{6,0},{1,3},{3,5},{5,7},{7,1},{8,10},{10,12},{12... | collective-permute-start | bytes 786440 | tf_op jit(solution)/shard_map/ppermute | solution.py:55
  26.0 15.3 %collective-permute-start.5 = (bf16[128,1024]{1,0:T(8,128)(2,1)S(1)}, bf16[128,1024]{1,0:T(8,128)(2,1)}, u32[]{:S(2)}, u32[]{:S(2)}) collective-permute-start(bf16[128,1024]{1,0:T(8,128)(2,1)S(1)} %get-tuple-element.21), channel_id=1, source_target_pairs={{0,6},{2,0},{4,2},{6,4},{1,7},{3,1},{5,3},{7,5},{8,14},{10,8},{12,... | collective-permute-start | bytes 786440 | tf_op jit(solution)/shard_map/ppermute | solution.py:55
  29.5 24.0 %collective-permute-start.2 = (bf16[2,128,1024]{2,1,0:T(8,128)(2,1)}, bf16[2,128,1024]{2,1,0:T(8,128)(2,1)S(1)}, u32[]{:S(2)}, u32[]{:S(2)}) collective-permute-start(bf16[2,128,1024]{2,1,0:T(8,128)(2,1)} %get-tuple-element.19), channel_id=1, source_target_pairs={{0,6},{2,0},{4,2},{6,4},{1,7},{3,1},{5,3},{7,5},{8,14},{10,8},{12,... | collective-permute-start | bytes 1572872 | tf_op jit(solution)/shard_map/ppermute | solution.py:55
  32.2 21.2 %collective-permute-start.3 = (bf16[2,128,1024]{2,1,0:T(8,128)(2,1)}, bf16[2,128,1024]{2,1,0:T(8,128)(2,1)S(1)}, u32[]{:S(2)}, u32[]{:S(2)}) collective-permute-start(bf16[2,128,1024]{2,1,0:T(8,128)(2,1)} %get-tuple-element.20), channel_id=1, source_target_pairs={{0,2},{2,4},{4,6},{6,0},{1,3},{3,5},{5,7},{7,1},{8,10},{10,12},{12... | collective-permute-start | bytes 1572872 | tf_op jit(solution)/shard_map/ppermute | solution.py:55
  37.0 16.4 %collective-permute-start.1 = (bf16[64,16,256]{2,1,0:T(8,128)(2,1)S(1)}, bf16[64,16,256]{2,1,0:T(8,128)(2,1)S(1)}, u32[]{:S(2)}, u32[]{:S(2)}) collective-permute-start(bf16[64,16,256]{2,1,0:T(8,128)(2,1)S(1)} %all-to-all-done.weight), channel_id=1, source_target_pairs={{0,8},{8,0},{1,9},{9,1},{2,10},{10,2},{3,11},{11,3},{4,12},{12,4},... | collective-permute-start | bytes 1572872 | tf_op jit(solution)/shard_map/ppermute | solution.py:64
  38.9 13.6 %collective-permute-start.4 = (bf16[128,1024]{1,0:T(8,128)(2,1)}, bf16[128,1024]{1,0:T(8,128)(2,1)S(1)}, u32[]{:S(2)}, u32[]{:S(2)}) collective-permute-start(bf16[128,1024]{1,0:T(8,128)(2,1)} %collective-permute-done), channel_id=1, source_target_pairs={{0,2},{2,4},{4,6},{6,0},{1,3},{3,5},{5,7},{7,1},{8,10},{10,12},{12... | collective-permute-start | bytes 786440 | tf_op jit(solution)/shard_map/ppermute | solution.py:55
  41.4 12.1 %collective-permute-start.6 = (bf16[128,1024]{1,0:T(8,128)(2,1)}, bf16[128,1024]{1,0:T(8,128)(2,1)S(1)}, u32[]{:S(2)}, u32[]{:S(2)}) collective-permute-start(bf16[128,1024]{1,0:T(8,128)(2,1)} %collective-permute-done.5), channel_id=1, source_target_pairs={{0,6},{2,0},{4,2},{6,4},{1,7},{3,1},{5,3},{7,5},{8,14},{10,8},{12,... | collective-permute-start | bytes 786440 | tf_op jit(solution)/shard_map/ppermute | solution.py:55
  53.5 23.8 %copy-start.4 = (s32[1,32]{1,0:T(1,128)S(1)}, s32[1,32]{1,0:T(1,128)}, u32[]{:S(2)}) copy-start(s32[1,32]{1,0:T(1,128)} %lengths.1) | copy-start | bytes 388
  64.5 7.5 %collective-permute-start.8 = (bf16[128,256]{1,0:T(8,128)(2,1)S(1)}, bf16[128,256]{1,0:T(8,128)(2,1)S(1)}, u32[]{:S(2)}, u32[]{:S(2)}) collective-permute-start(bf16[128,256]{1,0:T(8,128)(2,1)S(1)} %summed.3.refs_0_.own), channel_id=1, source_target_pairs={{0,32},{16,48},{32,64},{48,80},{64,96},{80,112},{96,128},{112,144}... | collective-permute-start | bytes 196616 | tf_op jit(solution)/shard_map/ppermute | solution.py:60
  68.6 5.4 %collective-permute-start.7 = (bf16[128,256]{1,0:T(8,128)(2,1)S(1)}, bf16[128,256]{1,0:T(8,128)(2,1)S(1)}, u32[]{:S(2)}, u32[]{:S(2)}) collective-permute-start(bf16[128,256]{1,0:T(8,128)(2,1)S(1)} %summed.3.refs_0_.own), channel_id=1, source_target_pairs={{0,16},{16,32},{32,48},{48,64},{64,80},{80,96},{96,112},{112,128},... | collective-permute-start | bytes 196616 | tf_op jit(solution)/shard_map/ppermute | solution.py:60
  74.0 3.3 %collective-permute-start.9 = (bf16[3,128,256]{2,1,0:T(8,128)(2,1)S(1)}, bf16[3,128,256]{2,1,0:T(8,128)(2,1)S(1)}, u32[]{:S(2)}, u32[]{:S(2)}) collective-permute-start(bf16[3,128,256]{2,1,0:T(8,128)(2,1)S(1)} %stacked.1), channel_id=1, source_target_pairs={{0,8},{8,0},{1,9},{9,1},{2,10},{10,2},{3,11},{11,3},{4,12},{12,4},... | collective-permute-start | bytes 589832 | tf_op jit(solution)/shard_map/ppermute | solution.py:64
  83.7 3.2 %collective-permute-start.10 = (bf16[2,128,256]{2,1,0:T(8,128)(2,1)S(1)}, bf16[2,128,256]{2,1,0:T(8,128)(2,1)S(1)}, u32[]{:S(2)}, u32[]{:S(2)}) collective-permute-start(bf16[2,128,256]{2,1,0:T(8,128)(2,1)S(1)} %get-tuple-element.25), channel_id=1, source_target_pairs={{0,8},{8,0},{1,9},{9,1},{2,10},{10,2},{3,11},{11,3},{4,12},{12,4},... | collective-permute-start | bytes 393224 | tf_op jit(solution)/shard_map/ppermute | solution.py:64
  87.6 6.9 %collective-permute-start.11 = (bf16[128,256]{1,0:T(8,128)(2,1)S(1)}, bf16[128,256]{1,0:T(8,128)(2,1)S(1)}, u32[]{:S(2)}, u32[]{:S(2)}) collective-permute-start(bf16[128,256]{1,0:T(8,128)(2,1)S(1)} %get-tuple-element.27), channel_id=1, source_target_pairs={{16,0},{32,16},{48,32},{64,48},{80,64},{96,80},{112,96},{128,112},... | collective-permute-start | bytes 196616 | tf_op jit(solution)/shard_map/ppermute | solution.py:60
  88.9 10.7 %collective-permute-start.12 = (bf16[128,256]{1,0:T(8,128)(2,1)S(1)}, bf16[128,256]{1,0:T(8,128)(2,1)S(1)}, u32[]{:S(2)}, u32[]{:S(2)}) collective-permute-start(bf16[128,256]{1,0:T(8,128)(2,1)S(1)} %get-tuple-element.28), channel_id=1, source_target_pairs={{32,0},{48,16},{64,32},{80,48},{96,64},{112,80},{128,96},{144,112}... | collective-permute-start | bytes 196616 | tf_op jit(solution)/shard_map/ppermute | solution.py:60
  109.8 3.8 %collective-permute-start.13 = (bf16[4,16,16,256]{3,2,1,0:T(8,128)(2,1)S(1)}, bf16[4,16,16,256]{3,2,1,0:T(8,128)(2,1)S(1)}, u32[]{:S(2)}, u32[]{:S(2)}) collective-permute-start(bf16[4,16,16,256]{3,2,1,0:T(8,128)(2,1)S(1)} %weight_grad.3), channel_id=1, source_target_pairs={{0,8},{8,0},{1,9},{9,1},{2,10},{10,2},{3,11},{11,3},{4,12},{12,4},... | collective-permute-start | bytes 1572872 | tf_op jit(solution)/shard_map/ppermute | solution.py:64

commit v6 on v5

--- a/solution.py
+++ b/solution.py
@@ -113,26 +113,44 @@
     return [(0, own[half]), (1, after[half]), (3, before[half]), (2, (over, under)[half][...])]
 
 
-def project_kernel(place, weight, weight_other, own, after, before, over, under, early_q, early_g, out):
+def projected(parts, weights):
+    rows = [w[...].reshape(CHIPS * 32, WIDTH) for w in weights]
+    total = jnp.dot(parts[0], rows[0], preferred_element_type=F32)
+    return (total + jnp.dot(parts[1], rows[1], preferred_element_type=F32)).astype(BF16)
+
+
+def project_kernel(place, weight, weight_other, own, after, before, early_q, early_g, out):
     del early_q, early_g
-    refs = (own, after, before, over, under)
-    rows = [w[...].reshape(CHIPS * 32, WIDTH) for w in (weight, weight_other)]
-    for (step, first), (_, second) in zip(halves(refs, 0), halves(refs, 1)):
-        part = jnp.dot(first, rows[0], preferred_element_type=F32)
-        part += jnp.dot(second, rows[1], preferred_element_type=F32)
-        out[(place[1] + step) % X] = part.astype(BF16)
+    for step, piece in ((0, own), (1, after), (3, before)):
+        out[(place[1] + step) % X] = projected((piece[0], piece[1]), (weight, weight_other))
+
+
+def project_last_kernel(place, weight, weight_other, over, under, parts, out):
+    del parts
+    out[(place[1] + 2) % X] = projected((over[...], under[...]), (weight, weight_other))
 
 
 def project(place, weight, weight_other, pieces, *early):
-    return pl.pallas_call(
+    shape = jax.ShapeDtypeStruct((X, COUNT, WIDTH), BF16)
+    parts = pl.pallas_call(
         project_kernel,
-        in_specs=[smem()] + [vmem()] * 9,
+        in_specs=[smem()] + [vmem()] * 7,
         out_specs=vmem(),
-        out_shape=jax.ShapeDtypeStruct((X, COUNT, WIDTH), BF16),
-        compiler_params=params(),
-        cost_estimate=pl.CostEstimate(flops=1 << 29, bytes_accessed=3 << 20, transcendentals=0),
+        out_shape=shape,
+        compiler_params=params(),
+        cost_estimate=pl.CostEstimate(flops=3 << 27, bytes_accessed=3 << 20, transcendentals=0),
         name="project",
-    )(place, weight, weight_other, *pieces, *early)
+    )(place, weight, weight_other, *pieces[:3], *early)
+    return pl.pallas_call(
+        project_last_kernel,
+        in_specs=[smem()] + [vmem()] * 5,
+        out_specs=vmem(),
+        out_shape=shape,
+        input_output_aliases={5: 0},
+        compiler_params=params(),
+        cost_estimate=pl.CostEstimate(flops=1 << 27, bytes_accessed=1 << 20, transcendentals=0),
+        name="project_last",
+    )(place, weight, weight_other, *pieces[3:], parts)
 
 
 def weight_grad_kernel(half, place, grads, own, after, before, over, under, out, total):

time: 152 us -> 158 us (1.039)
  waiting for transfers between devices: 23.9 us -> 31 us
    ppermute x6, waiting for transfers between devices: 8.65 us -> 13 us  [to_team(): return lax.ppermute(piece, 'x', [(x, (x + step) % X) for x in range(X)])]
    all_to_all x1, waiting for transfers between devices: 0.47 us -> 3.6 us  [exchanged(): return lax.all_to_all(blocks, axes, 0, 0, tiled=False)]
  transfers between devices with their start and end apart: 15 -> 15, of which waited for: 9 -> 10; matrix products, arithmetic and copies ran while one was open for 0% -> 0% of each run, Pallas kernels for 3% -> 3%
where the time goes in v6:
time: 158 us; the launch traced here: 156 us
  blocking collectives  53.2 us (34%)
  starting transfers between devices  52.8 us (33%)
  waiting for transfers between devices  31 us (20%)
  Pallas kernels  16.1 us (10%)
  local copies, waits for them, and re-layouts  2.37 us (2%)
    all_to_all x4, blocking collectives, exchanged(): return lax.all_to_all(blocks, axes, 0, 0, tiled=False)  53.2 us
    ppermute x6, starting transfers between devices, to_team(): return lax.ppermute(piece, 'x', [(x, (x + step) % X) for x in range(X)])  18.4 us
    all_to_all x1, starting transfers between devices, exchanged(): return lax.all_to_all(blocks, axes, 0, 0, tiled=False)  16.6 us
    ppermute x6, waiting for transfers between devices, to_team(): return lax.ppermute(piece, 'x', [(x, (x + step) % X) for x in range(X)])  13 us
    ppermute x4, waiting for transfers between devices, to_chip(): lax.ppermute(block, CHIP, [(i, i + hop) for i in chips if i + hop in chips])  11.1 us
    ppermute x4, starting transfers between devices, to_chip(): lax.ppermute(block, CHIP, [(i, i + hop) for i in chips if i + hop in chips])  10 us
    ppermute x4, starting transfers between devices, to_other_core(): return lax.ppermute(block, 'core', [(0, 1), (1, 0)])  7.79 us
    pallas_call x1, Pallas kernels, attention(): pl.pallas_call(attention_kernel, in_specs=[smem(), smem()] + [vmem()] * 6...  6.48 us
  transfers between devices with their start and end apart: 15, of which 10 were waited for; matrix products, arithmetic and copies ran while one was open for 0% of the time, Pallas kernels for 3%

profile of v6, /device:TPU:6, one launch (start us, length us, event | category | flops | bytes accessed | tf_op | source)
XLA Modules:
  0.0 156.4 jit_solution(15737871352847389633)
XLA Ops:
  2.2 16.6 %all-to-all-start = ((bf16[64,16,256]{2,1,0:T(8,128)(2,1)}), bf16[64,16,256]{2,1,0:T(8,128)(2,1)S(1)}, u32[]{:S(2)}, u32[]{:S(2)}) async-start(bf16[64,16,256]{2,1,0:T(8,128)(2,1)} %spread.1), calls=%async_computation | async-start | bytes 1048576 | tf_op jit(solution)/shard_map/all_to_all | solution.py:51
  18.9 1.7 %copy-done.3 = bf16[1,128,8192]{2,1,0:T(8,128)(2,1)S(1)} copy-done((bf16[1,128,8192]{2,1,0:T(8,128)(2,1)S(1)}, bf16[1,128,8192]{2,1,0:T(8,128)(2,1)}, u32[]{:S(2)}) %copy-start.3) | copy-done | bytes 2097176
  20.5 3.1 %pieces.1 = (bf16[2,128,1024]{2,1,0:T(8,128)(2,1)S(1)}, bf16[2,128,1024]{2,1,0:T(8,128)(2,1)}, bf16[2,128,1024]{2,1,0:T(8,128)(2,1)}, bf16[128,1024]{1,0:T(8,128)(2,1)S(1)}, bf16[128,1024]{1,0:T(8,128)(2,1)S(1)}) custom-call(s32[3]{0:T(128)S(1)} %pad_add_fusion.place, bf16[128,8192]{1,0:T(8,128)(2,1)S(1)} %bitcast.12), custom_call_target="tpu_custom_call" | custom-call | flops 1073741824 | bytes 4194304 | tf_op jit(solution)/shard_map/pieces/pallas_call | solution.py:91
  23.6 2.4 %collective-permute-start = (bf16[128,1024]{1,0:T(8,128)(2,1)S(1)}, bf16[128,1024]{1,0:T(8,128)(2,1)}, u32[]{:S(2)}, u32[]{:S(2)}) collective-permute-start(bf16[128,1024]{1,0:T(8,128)(2,1)S(1)} %get-tuple-element.16), channel_id=1, source_target_pairs={{0,2},{2,4},{4,6},{6,0},{1,3},{3,5},{5,7},{7,1},{8,10},{10,12},{12... | collective-permute-start | bytes 786440 | tf_op jit(solution)/shard_map/ppermute | solution.py:55
  26.0 3.5 %collective-permute-start.5 = (bf16[2,128,1024]{2,1,0:T(8,128)(2,1)}, bf16[2,128,1024]{2,1,0:T(8,128)(2,1)S(1)}, u32[]{:S(2)}, u32[]{:S(2)}) collective-permute-start(bf16[2,128,1024]{2,1,0:T(8,128)(2,1)} %get-tuple-element.20), channel_id=1, source_target_pairs={{0,6},{2,0},{4,2},{6,4},{1,7},{3,1},{5,3},{7,5},{8,14},{10,8},{12,... | collective-permute-start | bytes 1572872 | tf_op jit(solution)/shard_map/ppermute | solution.py:55
  29.5 3.6 %collective-permute-start.6 = (bf16[2,128,1024]{2,1,0:T(8,128)(2,1)}, bf16[2,128,1024]{2,1,0:T(8,128)(2,1)S(1)}, u32[]{:S(2)}, u32[]{:S(2)}) collective-permute-start(bf16[2,128,1024]{2,1,0:T(8,128)(2,1)} %get-tuple-element.21), channel_id=1, source_target_pairs={{0,2},{2,4},{4,6},{6,0},{1,3},{3,5},{5,7},{7,1},{8,10},{10,12},{12... | collective-permute-start | bytes 1572872 | tf_op jit(solution)/shard_map/ppermute | solution.py:55
  33.4 3.6 %all-to-all-done.weight = bf16[64,16,256]{2,1,0:T(8,128)(2,1)S(1)} async-done(((bf16[64,16,256]{2,1,0:T(8,128)(2,1)}), bf16[64,16,256]{2,1,0:T(8,128)(2,1)S(1)}, u32[]{:S(2)}, u32[]{:S(2)}) %all-to-all-start) | async-done | bytes 524320 | tf_op jit(solution)/shard_map/all_to_all | solution.py:51
  37.0 1.9 %collective-permute-start.1 = (bf16[64,16,256]{2,1,0:T(8,128)(2,1)S(1)}, bf16[64,16,256]{2,1,0:T(8,128)(2,1)S(1)}, u32[]{:S(2)}, u32[]{:S(2)}) collective-permute-start(bf16[64,16,256]{2,1,0:T(8,128)(2,1)S(1)} %all-to-all-done.weight), channel_id=1, source_target_pairs={{0,8},{8,0},{1,9},{9,1},{2,10},{10,2},{3,11},{11,3},{4,12},{12,4},... | collective-permute-start | bytes 1572872 | tf_op jit(solution)/shard_map/ppermute | solution.py:64
  38.9 2.7 %collective-permute-start.3 = (bf16[128,1024]{1,0:T(8,128)(2,1)S(1)}, bf16[128,1024]{1,0:T(8,128)(2,1)S(1)}, u32[]{:S(2)}, u32[]{:S(2)}) collective-permute-start(bf16[128,1024]{1,0:T(8,128)(2,1)S(1)} %get-tuple-element.18), channel_id=1, source_target_pairs={{0,6},{2,0},{4,2},{6,4},{1,7},{3,1},{5,3},{7,5},{8,14},{10,8},{12,... | collective-permute-start | bytes 786440 | tf_op jit(solution)/shard_map/ppermute | solution.py:55
  41.7 4.3 %collective-permute-start.2 = (bf16[128,1024]{1,0:T(8,128)(2,1)}, bf16[128,1024]{1,0:T(8,128)(2,1)S(1)}, u32[]{:S(2)}, u32[]{:S(2)}) collective-permute-start(bf16[128,1024]{1,0:T(8,128)(2,1)} %collective-permute-done), channel_id=1, source_target_pairs={{0,2},{2,4},{4,6},{6,0},{1,3},{3,5},{5,7},{7,1},{8,10},{10,12},{12... | collective-permute-start | bytes 786440 | tf_op jit(solution)/shard_map/ppermute | solution.py:55
  46.0 4.7 %collective-permute-done.3 = bf16[128,1024]{1,0:T(8,128)(2,1)S(1)} collective-permute-done((bf16[128,1024]{1,0:T(8,128)(2,1)S(1)}, bf16[128,1024]{1,0:T(8,128)(2,1)S(1)}, u32[]{:S(2)}, u32[]{:S(2)}) %collective-permute-start.3) | collective-permute-done | bytes 262176 | tf_op jit(solution)/shard_map/ppermute | solution.py:55
  50.8 1.9 %collective-permute-start.4 = (bf16[128,1024]{1,0:T(8,128)(2,1)S(1)}, bf16[128,1024]{1,0:T(8,128)(2,1)S(1)}, u32[]{:S(2)}, u32[]{:S(2)}) collective-permute-start(bf16[128,1024]{1,0:T(8,128)(2,1)S(1)} %collective-permute-done.3), channel_id=1, source_target_pairs={{0,6},{2,0},{4,2},{6,4},{1,7},{3,1},{5,3},{7,5},{8,14},{10,8},{12,... | collective-permute-start | bytes 786440 | tf_op jit(solution)/shard_map/ppermute | solution.py:55
  52.7 1.1 project.1.parts
  53.9 7.9 %collective-permute-done.4.under = bf16[128,1024]{1,0:T(8,128)(2,1)S(1)} collective-permute-done((bf16[128,1024]{1,0:T(8,128)(2,1)S(1)}, bf16[128,1024]{1,0:T(8,128)(2,1)S(1)}, u32[]{:S(2)}, u32[]{:S(2)}) %collective-permute-start.4) | collective-permute-done | bytes 262176 | tf_op jit(solution)/shard_map/ppermute | solution.py:55
  62.6 8.9 %all_to_all.25.parts = bf16[4,128,256]{2,1,0:T(8,128)(2,1)S(1)} all-to-all(bf16[4,128,256]{2,1,0:T(8,128)(2,1)S(1)} %project_last.1), channel_id=1, replica_groups=mesh['zh'=4,'yh'=4,'yl'=2,'core'=2,'x'=4,'zl'=2] {'x'}, dimensions={0} | all-to-all | bytes 524288 | tf_op jit(solution)/shard_map/all_to_all | solution.py:51
  71.6 4.2 %collective-permute-start.8 = (bf16[128,256]{1,0:T(8,128)(2,1)S(1)}, bf16[128,256]{1,0:T(8,128)(2,1)S(1)}, u32[]{:S(2)}, u32[]{:S(2)}) collective-permute-start(bf16[128,256]{1,0:T(8,128)(2,1)S(1)} %summed.3.refs_0_.own), channel_id=1, source_target_pairs={{0,32},{16,48},{32,64},{48,80},{64,96},{80,112},{96,128},{112,144}... | collective-permute-start | bytes 196616 | tf_op jit(solution)/shard_map/ppermute | solution.py:60
  75.8 3.2 %collective-permute-start.7 = (bf16[128,256]{1,0:T(8,128)(2,1)S(1)}, bf16[128,256]{1,0:T(8,128)(2,1)S(1)}, u32[]{:S(2)}, u32[]{:S(2)}) collective-permute-start(bf16[128,256]{1,0:T(8,128)(2,1)S(1)} %summed.3.refs_0_.own), channel_id=1, source_target_pairs={{0,16},{16,32},{32,48},{48,64},{64,80},{80,96},{96,112},{112,128},... | collective-permute-start | bytes 196616 | tf_op jit(solution)/shard_map/ppermute | solution.py:60
  79.0 2.2 %collective-permute-done.7.refs_1_.near = bf16[128,256]{1,0:T(8,128)(2,1)S(1)} collective-permute-done((bf16[128,256]{1,0:T(8,128)(2,1)S(1)}, bf16[128,256]{1,0:T(8,128)(2,1)S(1)}, u32[]{:S(2)}, u32[]{:S(2)}) %collective-permute-start.7) | collective-permute-done | bytes 65568 | tf_op jit(solution)/shard_map/ppermute | solution.py:60
  81.2 1.9 %collective-permute-start.9 = (bf16[3,128,256]{2,1,0:T(8,128)(2,1)S(1)}, bf16[3,128,256]{2,1,0:T(8,128)(2,1)S(1)}, u32[]{:S(2)}, u32[]{:S(2)}) collective-permute-start(bf16[3,128,256]{2,1,0:T(8,128)(2,1)S(1)} %stacked.1), channel_id=1, source_target_pairs={{0,8},{8,0},{1,9},{9,1},{2,10},{10,2},{3,11},{11,3},{4,12},{12,4},... | collective-permute-start | bytes 589832 | tf_op jit(solution)/shard_map/ppermute | solution.py:64
  83.1 1.4 collective-permute-done.9.other
  84.6 6.5 %attention.1 = (bf16[128,2048]{1,0:T(8,128)(2,1)}, bf16[128,2048]{1,0:T(8,128)(2,1)}, f32[3,128,256]{2,1,0:T(8,128)S(1)}, bf16[2,128,256]{2,1,0:T(8,128)(2,1)S(1)}) custom-call(s32[3]{0:T(128)S(1)} %pad_add_fusion.place, s32[1,32]{1,0:T(1,128)S(1)} %copy-done.4, bf16[128,2048]{1,0:T(8,128)(2,1)S(1)} %bitcast.9, bf16[128,2048]{1,0:T(8,128)(2,1)S(1)} %bitcast.11, ...), custom_call_target="tpu_custom_call" | custom-call | flops 2147483648 | bytes 3145728 | tf_op jit(solution)/shard_map/attention/pallas_call | solution.py:308
  91.0 2.0 %collective-permute-start.10 = (bf16[2,128,256]{2,1,0:T(8,128)(2,1)S(1)}, bf16[2,128,256]{2,1,0:T(8,128)(2,1)S(1)}, u32[]{:S(2)}, u32[]{:S(2)}) collective-permute-start(bf16[2,128,256]{2,1,0:T(8,128)(2,1)S(1)} %get-tuple-element.25), channel_id=1, source_target_pairs={{0,8},{8,0},{1,9},{9,1},{2,10},{10,2},{3,11},{11,3},{4,12},{12,4},... | collective-permute-start | bytes 393224 | tf_op jit(solution)/shard_map/ppermute | solution.py:64
  93.1 1.2 collective-permute-done.10.back
  94.9 1.3 collective-permute-start.11
  96.2 1.3 collective-permute-start.12
  97.5 4.3 %collective-permute-done.11.near = bf16[128,256]{1,0:T(8,128)(2,1)S(1)} collective-permute-done((bf16[128,256]{1,0:T(8,128)(2,1)S(1)}, bf16[128,256]{1,0:T(8,128)(2,1)S(1)}, u32[]{:S(2)}, u32[]{:S(2)}) %collective-permute-start.11) | collective-permute-done | bytes 65568 | tf_op jit(solution)/shard_map/ppermute | solution.py:60
  101.8 4.6 %collective-permute-done.12.far = bf16[128,256]{1,0:T(8,128)(2,1)S(1)} collective-permute-done((bf16[128,256]{1,0:T(8,128)(2,1)S(1)}, bf16[128,256]{1,0:T(8,128)(2,1)S(1)}, u32[]{:S(2)}, u32[]{:S(2)}) %collective-permute-start.12) | collective-permute-done | bytes 65568 | tf_op jit(solution)/shard_map/ppermute | solution.py:60
  106.4 9.1 %all_to_all.26.grads = bf16[4,128,256]{2,1,0:T(8,128)(2,1)S(1)} all-to-all(bf16[4,128,256]{2,1,0:T(8,128)(2,1)S(1)} %gathered.1), channel_id=1, replica_groups=mesh['zh'=4,'yh'=4,'yl'=2,'core'=2,'x'=4,'zl'=2] {'x'}, dimensions={0} | all-to-all | bytes 524288 | tf_op jit(solution)/shard_map/all_to_all | solution.py:51
  116.6 1.9 %collective-permute-start.13 = (bf16[4,16,16,256]{3,2,1,0:T(8,128)(2,1)S(1)}, bf16[4,16,16,256]{3,2,1,0:T(8,128)(2,1)S(1)}, u32[]{:S(2)}, u32[]{:S(2)}) collective-permute-start(bf16[4,16,16,256]{3,2,1,0:T(8,128)(2,1)S(1)} %weight_grad.3), channel_id=1, source_target_pairs={{0,8},{8,0},{1,9},{9,1},{2,10},{10,2},{3,11},{11,3},{4,12},{12,4},... | collective-permute-start | bytes 1572872 | tf_op jit(solution)/shard_map/ppermute | solution.py:64
  118.5 1.1 weight_grad.2.one
  120.5 11.5 %all_to_all.27.parts = bf16[4,16,16,256]{3,2,1,0:T(8,128)(2,1)S(1)} all-to-all(bf16[4,16,16,256]{3,2,1,0:T(8,128)(2,1)S(1)} %added.1), channel_id=1, replica_groups=mesh['zh'=4,'yh'=4,'yl'=2,'core'=2,'x'=4,'zl'=2] {'yl','zl'}, dimensions={0} | all-to-all | bytes 1048576 | tf_op jit(solution)/shard_map/all_to_all | solution.py:51
  132.1 23.7 %all_to_all.28.parts = bf16[16,16,256]{2,1,0:T(8,128)(2,1)S(1)} all-to-all(bf16[16,16,256]{2,1,0:T(8,128)(2,1)S(1)} %summed.4), channel_id=1, replica_groups=mesh['zh'=4,'yh'=4,'yl'=2,'core'=2,'x'=4,'zl'=2] {'zh','yh'}, dimensions={0} | all-to-all | bytes 262144 | tf_op jit(solution)/shard_map/all_to_all | solution.py:51
  (27 shorter events, 6.2 us)
Async XLA Ops:
  0.6 0.7 copy-start.2
  2.2 34.9 %all-to-all-start = ((bf16[64,16,256]{2,1,0:T(8,128)(2,1)}), bf16[64,16,256]{2,1,0:T(8,128)(2,1)S(1)}, u32[]{:S(2)}, u32[]{:S(2)}) async-start(bf16[64,16,256]{2,1,0:T(8,128)(2,1)} %spread.1), calls=%async_computation | async-start | bytes 1048576 | tf_op jit(solution)/shard_map/all_to_all | solution.py:51
  18.8 34.0 %copy-start = (bf16[1,128,2048]{2,1,0:T(8,128)(2,1)S(1)}, bf16[1,128,2048]{2,1,0:T(8,128)(2,1)}, u32[]{:S(2)}) copy-start(bf16[1,128,2048]{2,1,0:T(8,128)(2,1)} %param.6) | copy-start | bytes 1572868
  18.8 34.0 %copy-start.1 = (bf16[1,128,2048]{2,1,0:T(8,128)(2,1)S(1)}, bf16[1,128,2048]{2,1,0:T(8,128)(2,1)}, u32[]{:S(2)}) copy-start(bf16[1,128,2048]{2,1,0:T(8,128)(2,1)} %param.8) | copy-start | bytes 1572868
  18.9 1.7 %copy-start.3 = (bf16[1,128,8192]{2,1,0:T(8,128)(2,1)S(1)}, bf16[1,128,8192]{2,1,0:T(8,128)(2,1)}, u32[]{:S(2)}) copy-start(bf16[1,128,8192]{2,1,0:T(8,128)(2,1)} %param.5) | copy-start | bytes 6291460
  23.6 9.8 %collective-permute-start = (bf16[128,1024]{1,0:T(8,128)(2,1)S(1)}, bf16[128,1024]{1,0:T(8,128)(2,1)}, u32[]{:S(2)}, u32[]{:S(2)}) collective-permute-start(bf16[128,1024]{1,0:T(8,128)(2,1)S(1)} %get-tuple-element.16), channel_id=1, source_target_pairs={{0,2},{2,4},{4,6},{6,0},{1,3},{3,5},{5,7},{7,1},{8,10},{10,12},{12... | collective-permute-start | bytes 786440 | tf_op jit(solution)/shard_map/ppermute | solution.py:55
  26.0 26.7 %collective-permute-start.5 = (bf16[2,128,1024]{2,1,0:T(8,128)(2,1)}, bf16[2,128,1024]{2,1,0:T(8,128)(2,1)S(1)}, u32[]{:S(2)}, u32[]{:S(2)}) collective-permute-start(bf16[2,128,1024]{2,1,0:T(8,128)(2,1)} %get-tuple-element.20), channel_id=1, source_target_pairs={{0,6},{2,0},{4,2},{6,4},{1,7},{3,1},{5,3},{7,5},{8,14},{10,8},{12,... | collective-permute-start | bytes 1572872 | tf_op jit(solution)/shard_map/ppermute | solution.py:55
  29.5 23.2 %collective-permute-start.6 = (bf16[2,128,1024]{2,1,0:T(8,128)(2,1)}, bf16[2,128,1024]{2,1,0:T(8,128)(2,1)S(1)}, u32[]{:S(2)}, u32[]{:S(2)}) collective-permute-start(bf16[2,128,1024]{2,1,0:T(8,128)(2,1)} %get-tuple-element.21), channel_id=1, source_target_pairs={{0,2},{2,4},{4,6},{6,0},{1,3},{3,5},{5,7},{7,1},{8,10},{10,12},{12... | collective-permute-start | bytes 1572872 | tf_op jit(solution)/shard_map/ppermute | solution.py:55
  37.0 15.7 %collective-permute-start.1 = (bf16[64,16,256]{2,1,0:T(8,128)(2,1)S(1)}, bf16[64,16,256]{2,1,0:T(8,128)(2,1)S(1)}, u32[]{:S(2)}, u32[]{:S(2)}) collective-permute-start(bf16[64,16,256]{2,1,0:T(8,128)(2,1)S(1)} %all-to-all-done.weight), channel_id=1, source_target_pairs={{0,8},{8,0},{1,9},{9,1},{2,10},{10,2},{3,11},{11,3},{4,12},{12,4},... | collective-permute-start | bytes 1572872 | tf_op jit(solution)/shard_map/ppermute | solution.py:64
  38.9 11.8 %collective-permute-start.3 = (bf16[128,1024]{1,0:T(8,128)(2,1)S(1)}, bf16[128,1024]{1,0:T(8,128)(2,1)S(1)}, u32[]{:S(2)}, u32[]{:S(2)}) collective-permute-start(bf16[128,1024]{1,0:T(8,128)(2,1)S(1)} %get-tuple-element.18), channel_id=1, source_target_pairs={{0,6},{2,0},{4,2},{6,4},{1,7},{3,1},{5,3},{7,5},{8,14},{10,8},{12,... | collective-permute-start | bytes 786440 | tf_op jit(solution)/shard_map/ppermute | solution.py:55
  41.7 12.2 %collective-permute-start.2 = (bf16[128,1024]{1,0:T(8,128)(2,1)}, bf16[128,1024]{1,0:T(8,128)(2,1)S(1)}, u32[]{:S(2)}, u32[]{:S(2)}) collective-permute-start(bf16[128,1024]{1,0:T(8,128)(2,1)} %collective-permute-done), channel_id=1, source_target_pairs={{0,2},{2,4},{4,6},{6,0},{1,3},{3,5},{5,7},{7,1},{8,10},{10,12},{12... | collective-permute-start | bytes 786440 | tf_op jit(solution)/shard_map/ppermute | solution.py:55
  50.8 11.0 %collective-permute-start.4 = (bf16[128,1024]{1,0:T(8,128)(2,1)S(1)}, bf16[128,1024]{1,0:T(8,128)(2,1)S(1)}, u32[]{:S(2)}, u32[]{:S(2)}) collective-permute-start(bf16[128,1024]{1,0:T(8,128)(2,1)S(1)} %collective-permute-done.3), channel_id=1, source_target_pairs={{0,6},{2,0},{4,2},{6,4},{1,7},{3,1},{5,3},{7,5},{8,14},{10,8},{12,... | collective-permute-start | bytes 786440 | tf_op jit(solution)/shard_map/ppermute | solution.py:55
  53.9 30.7 %copy-start.4 = (s32[1,32]{1,0:T(1,128)S(1)}, s32[1,32]{1,0:T(1,128)}, u32[]{:S(2)}) copy-start(s32[1,32]{1,0:T(1,128)} %lengths.1) | copy-start | bytes 388
  71.6 7.4 %collective-permute-start.8 = (bf16[128,256]{1,0:T(8,128)(2,1)S(1)}, bf16[128,256]{1,0:T(8,128)(2,1)S(1)}, u32[]{:S(2)}, u32[]{:S(2)}) collective-permute-start(bf16[128,256]{1,0:T(8,128)(2,1)S(1)} %summed.3.refs_0_.own), channel_id=1, source_target_pairs={{0,32},{16,48},{32,64},{48,80},{64,96},{80,112},{96,128},{112,144}... | collective-permute-start | bytes 196616 | tf_op jit(solution)/shard_map/ppermute | solution.py:60
  75.8 5.4 %collective-permute-start.7 = (bf16[128,256]{1,0:T(8,128)(2,1)S(1)}, bf16[128,256]{1,0:T(8,128)(2,1)S(1)}, u32[]{:S(2)}, u32[]{:S(2)}) collective-permute-start(bf16[128,256]{1,0:T(8,128)(2,1)S(1)} %summed.3.refs_0_.own), channel_id=1, source_target_pairs={{0,16},{16,32},{32,48},{48,64},{64,80},{80,96},{96,112},{112,128},... | collective-permute-start | bytes 196616 | tf_op jit(solution)/shard_map/ppermute | solution.py:60
  81.2 3.3 %collective-permute-start.9 = (bf16[3,128,256]{2,1,0:T(8,128)(2,1)S(1)}, bf16[3,128,256]{2,1,0:T(8,128)(2,1)S(1)}, u32[]{:S(2)}, u32[]{:S(2)}) collective-permute-start(bf16[3,128,256]{2,1,0:T(8,128)(2,1)S(1)} %stacked.1), channel_id=1, source_target_pairs={{0,8},{8,0},{1,9},{9,1},{2,10},{10,2},{3,11},{11,3},{4,12},{12,4},... | collective-permute-start | bytes 589832 | tf_op jit(solution)/shard_map/ppermute | solution.py:64
  91.0 3.2 %collective-permute-start.10 = (bf16[2,128,256]{2,1,0:T(8,128)(2,1)S(1)}, bf16[2,128,256]{2,1,0:T(8,128)(2,1)S(1)}, u32[]{:S(2)}, u32[]{:S(2)}) collective-permute-start(bf16[2,128,256]{2,1,0:T(8,128)(2,1)S(1)} %get-tuple-element.25), channel_id=1, source_target_pairs={{0,8},{8,0},{1,9},{9,1},{2,10},{10,2},{3,11},{11,3},{4,12},{12,4},... | collective-permute-start | bytes 393224 | tf_op jit(solution)/shard_map/ppermute | solution.py:64
  94.9 6.9 %collective-permute-start.11 = (bf16[128,256]{1,0:T(8,128)(2,1)S(1)}, bf16[128,256]{1,0:T(8,128)(2,1)S(1)}, u32[]{:S(2)}, u32[]{:S(2)}) collective-permute-start(bf16[128,256]{1,0:T(8,128)(2,1)S(1)} %get-tuple-element.27), channel_id=1, source_target_pairs={{16,0},{32,16},{48,32},{64,48},{80,64},{96,80},{112,96},{128,112},... | collective-permute-start | bytes 196616 | tf_op jit(solution)/shard_map/ppermute | solution.py:60
  96.2 10.2 %collective-permute-start.12 = (bf16[128,256]{1,0:T(8,128)(2,1)S(1)}, bf16[128,256]{1,0:T(8,128)(2,1)S(1)}, u32[]{:S(2)}, u32[]{:S(2)}) collective-permute-start(bf16[128,256]{1,0:T(8,128)(2,1)S(1)} %get-tuple-element.28), channel_id=1, source_target_pairs={{32,0},{48,16},{64,32},{80,48},{96,64},{112,80},{128,96},{144,112}... | collective-permute-start | bytes 196616 | tf_op jit(solution)/shard_map/ppermute | solution.py:60
  116.6 3.8 %collective-permute-start.13 = (bf16[4,16,16,256]{3,2,1,0:T(8,128)(2,1)S(1)}, bf16[4,16,16,256]{3,2,1,0:T(8,128)(2,1)S(1)}, u32[]{:S(2)}, u32[]{:S(2)}) collective-permute-start(bf16[4,16,16,256]{3,2,1,0:T(8,128)(2,1)S(1)} %weight_grad.3), channel_id=1, source_target_pairs={{0,8},{8,0},{1,9},{9,1},{2,10},{10,2},{3,11},{11,3},{4,12},{12,4},... | collective-permute-start | bytes 1572872 | tf_op jit(solution)/shard_map/ppermute | solution.py:64

commit v7 on v6

--- a/solution.py
+++ b/solution.py
@@ -329,7 +329,7 @@
     ring = CHIPS * ZL
     weight = exchanged(spread(kv_weight, ring), CHIP + ("zl",))
     pieces, halfway = team_pieces(*cut)
-    weight, _ = lax.optimization_barrier((weight, halfway[0]))
+    weight, _ = lax.optimization_barrier((weight, halfway))
     weight_other = to_other_core(weight)
     part = exchanged(project(place, weight, weight_other, pieces, queries_in[0], out_grad[0]), "x")
     kv = summed(part, BF16)

time: 158 us -> 152 us (0.962)
  waiting for transfers between devices: 31 us -> 23.6 us
    ppermute x6, waiting for transfers between devices: 13 us -> 8.84 us  [to_team(): return lax.ppermute(piece, 'x', [(x, (x + step) % X) for x in range(X)])]
    all_to_all x1, waiting for transfers between devices: 3.6 us -> 0.01 us  [exchanged(): return lax.all_to_all(blocks, axes, 0, 0, tiled=False)]
  transfers between devices with their start and end apart: 15 -> 15, of which waited for: 10 -> 11; matrix products, arithmetic and copies ran while one was open for 0% -> 0% of each run, Pallas kernels for 3% -> 4%
where the time goes in v7:
time: 152 us; the launch traced here: 150 us
  blocking collectives  53.9 us (35%)
  starting transfers between devices  53.4 us (35%)
  waiting for transfers between devices  23.6 us (16%)
  Pallas kernels  16.1 us (11%)
  local copies, waits for them, and re-layouts  2.37 us (2%)
    all_to_all x4, blocking collectives, exchanged(): return lax.all_to_all(blocks, axes, 0, 0, tiled=False)  53.9 us
    ppermute x6, starting transfers between devices, to_team(): return lax.ppermute(piece, 'x', [(x, (x + step) % X) for x in range(X)])  18.7 us
    all_to_all x1, starting transfers between devices, exchanged(): return lax.all_to_all(blocks, axes, 0, 0, tiled=False)  16.6 us
    ppermute x4, waiting for transfers between devices, to_chip(): lax.ppermute(block, CHIP, [(i, i + hop) for i in chips if i + hop in chips])  11.4 us
    ppermute x4, starting transfers between devices, to_chip(): lax.ppermute(block, CHIP, [(i, i + hop) for i in chips if i + hop in chips])  10.3 us
    ppermute x6, waiting for transfers between devices, to_team(): return lax.ppermute(piece, 'x', [(x, (x + step) % X) for x in range(X)])  8.84 us
    ppermute x4, starting transfers between devices, to_other_core(): return lax.ppermute(block, 'core', [(0, 1), (1, 0)])  7.79 us
    pallas_call x1, Pallas kernels, attention(): pl.pallas_call(attention_kernel, in_specs=[smem(), smem()] + [vmem()] * 6...  6.48 us
  transfers between devices with their start and end apart: 15, of which 11 were waited for; matrix products, arithmetic and copies ran while one was open for 0% of the time, Pallas kernels for 4%

profile of v7, /device:TPU:6, one launch (start us, length us, event | category | flops | bytes accessed | tf_op | source)
XLA Modules:
  0.0 150.4 jit_solution(15354784169408985903)
XLA Ops:
  2.2 16.6 %all-to-all-start = ((bf16[64,16,256]{2,1,0:T(8,128)(2,1)}), bf16[64,16,256]{2,1,0:T(8,128)(2,1)S(1)}, u32[]{:S(2)}, u32[]{:S(2)}) async-start(bf16[64,16,256]{2,1,0:T(8,128)(2,1)} %spread.1), calls=%async_computation | async-start | bytes 1048576 | tf_op jit(solution)/shard_map/all_to_all | solution.py:51
  18.9 1.7 %copy-done.3 = bf16[1,128,8192]{2,1,0:T(8,128)(2,1)S(1)} copy-done((bf16[1,128,8192]{2,1,0:T(8,128)(2,1)S(1)}, bf16[1,128,8192]{2,1,0:T(8,128)(2,1)}, u32[]{:S(2)}) %copy-start.3) | copy-done | bytes 2097176
  20.5 3.1 %pieces.1 = (bf16[2,128,1024]{2,1,0:T(8,128)(2,1)S(1)}, bf16[2,128,1024]{2,1,0:T(8,128)(2,1)}, bf16[2,128,1024]{2,1,0:T(8,128)(2,1)}, bf16[128,1024]{1,0:T(8,128)(2,1)S(1)}, bf16[128,1024]{1,0:T(8,128)(2,1)S(1)}) custom-call(s32[3]{0:T(128)S(1)} %pad_add_fusion.place, bf16[128,8192]{1,0:T(8,128)(2,1)S(1)} %bitcast.12), custom_call_target="tpu_custom_call" | custom-call | flops 1073741824 | bytes 4194304 | tf_op jit(solution)/shard_map/pieces/pallas_call | solution.py:91
  23.6 2.4 %collective-permute-start = (bf16[128,1024]{1,0:T(8,128)(2,1)S(1)}, bf16[128,1024]{1,0:T(8,128)(2,1)S(1)}, u32[]{:S(2)}, u32[]{:S(2)}) collective-permute-start(bf16[128,1024]{1,0:T(8,128)(2,1)S(1)} %get-tuple-element.16), channel_id=1, source_target_pairs={{0,2},{2,4},{4,6},{6,0},{1,3},{3,5},{5,7},{7,1},{8,10},{10,12},{12... | collective-permute-start | bytes 786440 | tf_op jit(solution)/shard_map/ppermute | solution.py:55
  26.0 3.5 %collective-permute-start.1 = (bf16[128,1024]{1,0:T(8,128)(2,1)S(1)}, bf16[128,1024]{1,0:T(8,128)(2,1)}, u32[]{:S(2)}, u32[]{:S(2)}) collective-permute-start(bf16[128,1024]{1,0:T(8,128)(2,1)S(1)} %get-tuple-element.17), channel_id=1, source_target_pairs={{0,6},{2,0},{4,2},{6,4},{1,7},{3,1},{5,3},{7,5},{8,14},{10,8},{12,... | collective-permute-start | bytes 786440 | tf_op jit(solution)/shard_map/ppermute | solution.py:55
  29.5 2.7 %collective-permute-start.5 = (bf16[2,128,1024]{2,1,0:T(8,128)(2,1)}, bf16[2,128,1024]{2,1,0:T(8,128)(2,1)S(1)}, u32[]{:S(2)}, u32[]{:S(2)}) collective-permute-start(bf16[2,128,1024]{2,1,0:T(8,128)(2,1)} %get-tuple-element.20), channel_id=1, source_target_pairs={{0,6},{2,0},{4,2},{6,4},{1,7},{3,1},{5,3},{7,5},{8,14},{10,8},{12,... | collective-permute-start | bytes 1572872 | tf_op jit(solution)/shard_map/ppermute | solution.py:55
  32.2 4.3 %collective-permute-start.6 = (bf16[2,128,1024]{2,1,0:T(8,128)(2,1)}, bf16[2,128,1024]{2,1,0:T(8,128)(2,1)S(1)}, u32[]{:S(2)}, u32[]{:S(2)}) collective-permute-start(bf16[2,128,1024]{2,1,0:T(8,128)(2,1)} %get-tuple-element.21), channel_id=1, source_target_pairs={{0,2},{2,4},{4,6},{6,0},{1,3},{3,5},{5,7},{7,1},{8,10},{10,12},{12... | collective-permute-start | bytes 1572872 | tf_op jit(solution)/shard_map/ppermute | solution.py:55
  36.6 1.9 %collective-permute-done.1 = bf16[128,1024]{1,0:T(8,128)(2,1)} collective-permute-done((bf16[128,1024]{1,0:T(8,128)(2,1)S(1)}, bf16[128,1024]{1,0:T(8,128)(2,1)}, u32[]{:S(2)}, u32[]{:S(2)}) %collective-permute-start.1) | collective-permute-done | bytes 262176 | tf_op jit(solution)/shard_map/ppermute | solution.py:55
  38.5 1.9 %collective-permute-start.2 = (bf16[64,16,256]{2,1,0:T(8,128)(2,1)S(1)}, bf16[64,16,256]{2,1,0:T(8,128)(2,1)S(1)}, u32[]{:S(2)}, u32[]{:S(2)}) collective-permute-start(bf16[64,16,256]{2,1,0:T(8,128)(2,1)S(1)} %all-to-all-done.weight), channel_id=1, source_target_pairs={{0,8},{8,0},{1,9},{9,1},{2,10},{10,2},{3,11},{11,3},{4,12},{12,4},... | collective-permute-start | bytes 1572872 | tf_op jit(solution)/shard_map/ppermute | solution.py:64
  40.4 2.2 %collective-permute-start.3 = (bf16[128,1024]{1,0:T(8,128)(2,1)S(1)}, bf16[128,1024]{1,0:T(8,128)(2,1)S(1)}, u32[]{:S(2)}, u32[]{:S(2)}) collective-permute-start(bf16[128,1024]{1,0:T(8,128)(2,1)S(1)} %collective-permute-done), channel_id=1, source_target_pairs={{0,2},{2,4},{4,6},{6,0},{1,3},{3,5},{5,7},{7,1},{8,10},{10,12},{12... | collective-permute-start | bytes 786440 | tf_op jit(solution)/shard_map/ppermute | solution.py:55
  42.6 3.7 %collective-permute-start.4 = (bf16[128,1024]{1,0:T(8,128)(2,1)}, bf16[128,1024]{1,0:T(8,128)(2,1)S(1)}, u32[]{:S(2)}, u32[]{:S(2)}) collective-permute-start(bf16[128,1024]{1,0:T(8,128)(2,1)} %collective-permute-done.1), channel_id=1, source_target_pairs={{0,6},{2,0},{4,2},{6,4},{1,7},{3,1},{5,3},{7,5},{8,14},{10,8},{12,... | collective-permute-start | bytes 786440 | tf_op jit(solution)/shard_map/ppermute | solution.py:55
  46.2 1.6 %collective-permute-done.5.after = bf16[2,128,1024]{2,1,0:T(8,128)(2,1)S(1)} collective-permute-done((bf16[2,128,1024]{2,1,0:T(8,128)(2,1)}, bf16[2,128,1024]{2,1,0:T(8,128)(2,1)S(1)}, u32[]{:S(2)}, u32[]{:S(2)}) %collective-permute-start.5) | collective-permute-done | bytes 524320 | tf_op jit(solution)/shard_map/ppermute | solution.py:55
  47.8 1.4 collective-permute-done.6.before
  50.4 2.1 %collective-permute-done.3.over = bf16[128,1024]{1,0:T(8,128)(2,1)S(1)} collective-permute-done((bf16[128,1024]{1,0:T(8,128)(2,1)S(1)}, bf16[128,1024]{1,0:T(8,128)(2,1)S(1)}, u32[]{:S(2)}, u32[]{:S(2)}) %collective-permute-start.3) | collective-permute-done | bytes 262176 | tf_op jit(solution)/shard_map/ppermute | solution.py:55
  52.5 1.9 %collective-permute-done.4.under = bf16[128,1024]{1,0:T(8,128)(2,1)S(1)} collective-permute-done((bf16[128,1024]{1,0:T(8,128)(2,1)}, bf16[128,1024]{1,0:T(8,128)(2,1)S(1)}, u32[]{:S(2)}, u32[]{:S(2)}) %collective-permute-start.4) | collective-permute-done | bytes 262176 | tf_op jit(solution)/shard_map/ppermute | solution.py:55
  55.2 8.9 %all_to_all.25.parts = bf16[4,128,256]{2,1,0:T(8,128)(2,1)S(1)} all-to-all(bf16[4,128,256]{2,1,0:T(8,128)(2,1)S(1)} %project_last.1), channel_id=1, replica_groups=mesh['zh'=4,'yh'=4,'yl'=2,'core'=2,'x'=4,'zl'=2] {'x'}, dimensions={0} | all-to-all | bytes 524288 | tf_op jit(solution)/shard_map/all_to_all | solution.py:51
  64.1 4.4 %collective-permute-start.8 = (bf16[128,256]{1,0:T(8,128)(2,1)S(1)}, bf16[128,256]{1,0:T(8,128)(2,1)S(1)}, u32[]{:S(2)}, u32[]{:S(2)}) collective-permute-start(bf16[128,256]{1,0:T(8,128)(2,1)S(1)} %summed.3.refs_0_.own), channel_id=1, source_target_pairs={{0,32},{16,48},{32,64},{48,80},{64,96},{80,112},{96,128},{112,144}... | collective-permute-start | bytes 196616 | tf_op jit(solution)/shard_map/ppermute | solution.py:60
  68.5 3.4 %collective-permute-start.7 = (bf16[128,256]{1,0:T(8,128)(2,1)S(1)}, bf16[128,256]{1,0:T(8,128)(2,1)S(1)}, u32[]{:S(2)}, u32[]{:S(2)}) collective-permute-start(bf16[128,256]{1,0:T(8,128)(2,1)S(1)} %summed.3.refs_0_.own), channel_id=1, source_target_pairs={{0,16},{16,32},{32,48},{48,64},{64,80},{80,96},{96,112},{112,128},... | collective-permute-start | bytes 196616 | tf_op jit(solution)/shard_map/ppermute | solution.py:60
  71.9 2.0 %collective-permute-done.7.refs_1_.near = bf16[128,256]{1,0:T(8,128)(2,1)S(1)} collective-permute-done((bf16[128,256]{1,0:T(8,128)(2,1)S(1)}, bf16[128,256]{1,0:T(8,128)(2,1)S(1)}, u32[]{:S(2)}, u32[]{:S(2)}) %collective-permute-start.7) | collective-permute-done | bytes 65568 | tf_op jit(solution)/shard_map/ppermute | solution.py:60
  73.9 1.9 %collective-permute-start.9 = (bf16[3,128,256]{2,1,0:T(8,128)(2,1)S(1)}, bf16[3,128,256]{2,1,0:T(8,128)(2,1)S(1)}, u32[]{:S(2)}, u32[]{:S(2)}) collective-permute-start(bf16[3,128,256]{2,1,0:T(8,128)(2,1)S(1)} %stacked.1), channel_id=1, source_target_pairs={{0,8},{8,0},{1,9},{9,1},{2,10},{10,2},{3,11},{11,3},{4,12},{12,4},... | collective-permute-start | bytes 589832 | tf_op jit(solution)/shard_map/ppermute | solution.py:64
  75.8 1.4 collective-permute-done.9.other
  77.2 6.5 %attention.1 = (bf16[128,2048]{1,0:T(8,128)(2,1)}, bf16[128,2048]{1,0:T(8,128)(2,1)}, f32[3,128,256]{2,1,0:T(8,128)S(1)}, bf16[2,128,256]{2,1,0:T(8,128)(2,1)S(1)}) custom-call(s32[3]{0:T(128)S(1)} %pad_add_fusion.place, s32[1,32]{1,0:T(1,128)S(1)} %copy-done.4, bf16[128,2048]{1,0:T(8,128)(2,1)S(1)} %bitcast.9, bf16[128,2048]{1,0:T(8,128)(2,1)S(1)} %bitcast.11, ...), custom_call_target="tpu_custom_call" | custom-call | flops 2147483648 | bytes 3145728 | tf_op jit(solution)/shard_map/attention/pallas_call | solution.py:308
  83.7 2.0 %collective-permute-start.10 = (bf16[2,128,256]{2,1,0:T(8,128)(2,1)S(1)}, bf16[2,128,256]{2,1,0:T(8,128)(2,1)S(1)}, u32[]{:S(2)}, u32[]{:S(2)}) collective-permute-start(bf16[2,128,256]{2,1,0:T(8,128)(2,1)S(1)} %get-tuple-element.25), channel_id=1, source_target_pairs={{0,8},{8,0},{1,9},{9,1},{2,10},{10,2},{3,11},{11,3},{4,12},{12,4},... | collective-permute-start | bytes 393224 | tf_op jit(solution)/shard_map/ppermute | solution.py:64
  85.8 1.2 collective-permute-done.10.back
  87.5 1.3 collective-permute-start.11
  88.8 1.3 collective-permute-start.12
  90.1 4.3 %collective-permute-done.11.near = bf16[128,256]{1,0:T(8,128)(2,1)S(1)} collective-permute-done((bf16[128,256]{1,0:T(8,128)(2,1)S(1)}, bf16[128,256]{1,0:T(8,128)(2,1)S(1)}, u32[]{:S(2)}, u32[]{:S(2)}) %collective-permute-start.11) | collective-permute-done | bytes 65568 | tf_op jit(solution)/shard_map/ppermute | solution.py:60
  94.4 5.1 %collective-permute-done.12.far = bf16[128,256]{1,0:T(8,128)(2,1)S(1)} collective-permute-done((bf16[128,256]{1,0:T(8,128)(2,1)S(1)}, bf16[128,256]{1,0:T(8,128)(2,1)S(1)}, u32[]{:S(2)}, u32[]{:S(2)}) %collective-permute-start.12) | collective-permute-done | bytes 65568 | tf_op jit(solution)/shard_map/ppermute | solution.py:60
  99.6 9.1 %all_to_all.26.grads = bf16[4,128,256]{2,1,0:T(8,128)(2,1)S(1)} all-to-all(bf16[4,128,256]{2,1,0:T(8,128)(2,1)S(1)} %gathered.1), channel_id=1, replica_groups=mesh['zh'=4,'yh'=4,'yl'=2,'core'=2,'x'=4,'zl'=2] {'x'}, dimensions={0} | all-to-all | bytes 524288 | tf_op jit(solution)/shard_map/all_to_all | solution.py:51
  109.8 1.9 %collective-permute-start.13 = (bf16[4,16,16,256]{3,2,1,0:T(8,128)(2,1)S(1)}, bf16[4,16,16,256]{3,2,1,0:T(8,128)(2,1)S(1)}, u32[]{:S(2)}, u32[]{:S(2)}) collective-permute-start(bf16[4,16,16,256]{3,2,1,0:T(8,128)(2,1)S(1)} %weight_grad.3), channel_id=1, source_target_pairs={{0,8},{8,0},{1,9},{9,1},{2,10},{10,2},{3,11},{11,3},{4,12},{12,4},... | collective-permute-start | bytes 1572872 | tf_op jit(solution)/shard_map/ppermute | solution.py:64
  113.7 11.5 %all_to_all.27.parts = bf16[4,16,16,256]{3,2,1,0:T(8,128)(2,1)S(1)} all-to-all(bf16[4,16,16,256]{3,2,1,0:T(8,128)(2,1)S(1)} %added.1), channel_id=1, replica_groups=mesh['zh'=4,'yh'=4,'yl'=2,'core'=2,'x'=4,'zl'=2] {'yl','zl'}, dimensions={0} | all-to-all | bytes 1048576 | tf_op jit(solution)/shard_map/all_to_all | solution.py:51
  125.3 24.4 %all_to_all.28.parts = bf16[16,16,256]{2,1,0:T(8,128)(2,1)S(1)} all-to-all(bf16[16,16,256]{2,1,0:T(8,128)(2,1)S(1)} %summed.4), channel_id=1, replica_groups=mesh['zh'=4,'yh'=4,'yl'=2,'core'=2,'x'=4,'zl'=2] {'zh','yh'}, dimensions={0} | all-to-all | bytes 262144 | tf_op jit(solution)/shard_map/all_to_all | solution.py:51
  (27 shorter events, 8.1 us)
Async XLA Ops:
  0.6 0.7 copy-start.2
  2.2 36.3 %all-to-all-start = ((bf16[64,16,256]{2,1,0:T(8,128)(2,1)}), bf16[64,16,256]{2,1,0:T(8,128)(2,1)S(1)}, u32[]{:S(2)}, u32[]{:S(2)}) async-start(bf16[64,16,256]{2,1,0:T(8,128)(2,1)} %spread.1), calls=%async_computation | async-start | bytes 1048576 | tf_op jit(solution)/shard_map/all_to_all | solution.py:51
  18.8 30.5 %copy-start = (bf16[1,128,2048]{2,1,0:T(8,128)(2,1)S(1)}, bf16[1,128,2048]{2,1,0:T(8,128)(2,1)}, u32[]{:S(2)}) copy-start(bf16[1,128,2048]{2,1,0:T(8,128)(2,1)} %param.6) | copy-start | bytes 1572868
  18.8 30.5 %copy-start.1 = (bf16[1,128,2048]{2,1,0:T(8,128)(2,1)S(1)}, bf16[1,128,2048]{2,1,0:T(8,128)(2,1)}, u32[]{:S(2)}) copy-start(bf16[1,128,2048]{2,1,0:T(8,128)(2,1)} %param.8) | copy-start | bytes 1572868
  18.9 1.7 %copy-start.3 = (bf16[1,128,8192]{2,1,0:T(8,128)(2,1)S(1)}, bf16[1,128,8192]{2,1,0:T(8,128)(2,1)}, u32[]{:S(2)}) copy-start(bf16[1,128,8192]{2,1,0:T(8,128)(2,1)} %param.5) | copy-start | bytes 6291460
  23.6 12.9 %collective-permute-start = (bf16[128,1024]{1,0:T(8,128)(2,1)S(1)}, bf16[128,1024]{1,0:T(8,128)(2,1)S(1)}, u32[]{:S(2)}, u32[]{:S(2)}) collective-permute-start(bf16[128,1024]{1,0:T(8,128)(2,1)S(1)} %get-tuple-element.16), channel_id=1, source_target_pairs={{0,2},{2,4},{4,6},{6,0},{1,3},{3,5},{5,7},{7,1},{8,10},{10,12},{12... | collective-permute-start | bytes 786440 | tf_op jit(solution)/shard_map/ppermute | solution.py:55
  26.0 12.5 %collective-permute-start.1 = (bf16[128,1024]{1,0:T(8,128)(2,1)S(1)}, bf16[128,1024]{1,0:T(8,128)(2,1)}, u32[]{:S(2)}, u32[]{:S(2)}) collective-permute-start(bf16[128,1024]{1,0:T(8,128)(2,1)S(1)} %get-tuple-element.17), channel_id=1, source_target_pairs={{0,6},{2,0},{4,2},{6,4},{1,7},{3,1},{5,3},{7,5},{8,14},{10,8},{12,... | collective-permute-start | bytes 786440 | tf_op jit(solution)/shard_map/ppermute | solution.py:55
  29.5 18.4 %collective-permute-start.5 = (bf16[2,128,1024]{2,1,0:T(8,128)(2,1)}, bf16[2,128,1024]{2,1,0:T(8,128)(2,1)S(1)}, u32[]{:S(2)}, u32[]{:S(2)}) collective-permute-start(bf16[2,128,1024]{2,1,0:T(8,128)(2,1)} %get-tuple-element.20), channel_id=1, source_target_pairs={{0,6},{2,0},{4,2},{6,4},{1,7},{3,1},{5,3},{7,5},{8,14},{10,8},{12,... | collective-permute-start | bytes 1572872 | tf_op jit(solution)/shard_map/ppermute | solution.py:55
  32.2 17.0 %collective-permute-start.6 = (bf16[2,128,1024]{2,1,0:T(8,128)(2,1)}, bf16[2,128,1024]{2,1,0:T(8,128)(2,1)S(1)}, u32[]{:S(2)}, u32[]{:S(2)}) collective-permute-start(bf16[2,128,1024]{2,1,0:T(8,128)(2,1)} %get-tuple-element.21), channel_id=1, source_target_pairs={{0,2},{2,4},{4,6},{6,0},{1,3},{3,5},{5,7},{7,1},{8,10},{10,12},{12... | collective-permute-start | bytes 1572872 | tf_op jit(solution)/shard_map/ppermute | solution.py:55
  38.5 10.8 %collective-permute-start.2 = (bf16[64,16,256]{2,1,0:T(8,128)(2,1)S(1)}, bf16[64,16,256]{2,1,0:T(8,128)(2,1)S(1)}, u32[]{:S(2)}, u32[]{:S(2)}) collective-permute-start(bf16[64,16,256]{2,1,0:T(8,128)(2,1)S(1)} %all-to-all-done.weight), channel_id=1, source_target_pairs={{0,8},{8,0},{1,9},{9,1},{2,10},{10,2},{3,11},{11,3},{4,12},{12,4},... | collective-permute-start | bytes 1572872 | tf_op jit(solution)/shard_map/ppermute | solution.py:64
  40.4 12.1 %collective-permute-start.3 = (bf16[128,1024]{1,0:T(8,128)(2,1)S(1)}, bf16[128,1024]{1,0:T(8,128)(2,1)S(1)}, u32[]{:S(2)}, u32[]{:S(2)}) collective-permute-start(bf16[128,1024]{1,0:T(8,128)(2,1)S(1)} %collective-permute-done), channel_id=1, source_target_pairs={{0,2},{2,4},{4,6},{6,0},{1,3},{3,5},{5,7},{7,1},{8,10},{10,12},{12... | collective-permute-start | bytes 786440 | tf_op jit(solution)/shard_map/ppermute | solution.py:55
  42.6 11.8 %collective-permute-start.4 = (bf16[128,1024]{1,0:T(8,128)(2,1)}, bf16[128,1024]{1,0:T(8,128)(2,1)S(1)}, u32[]{:S(2)}, u32[]{:S(2)}) collective-permute-start(bf16[128,1024]{1,0:T(8,128)(2,1)} %collective-permute-done.1), channel_id=1, source_target_pairs={{0,6},{2,0},{4,2},{6,4},{1,7},{3,1},{5,3},{7,5},{8,14},{10,8},{12,... | collective-permute-start | bytes 786440 | tf_op jit(solution)/shard_map/ppermute | solution.py:55
  50.4 26.9 %copy-start.4 = (s32[1,32]{1,0:T(1,128)S(1)}, s32[1,32]{1,0:T(1,128)}, u32[]{:S(2)}) copy-start(s32[1,32]{1,0:T(1,128)} %lengths.1) | copy-start | bytes 388
  64.1 7.8 %collective-permute-start.8 = (bf16[128,256]{1,0:T(8,128)(2,1)S(1)}, bf16[128,256]{1,0:T(8,128)(2,1)S(1)}, u32[]{:S(2)}, u32[]{:S(2)}) collective-permute-start(bf16[128,256]{1,0:T(8,128)(2,1)S(1)} %summed.3.refs_0_.own), channel_id=1, source_target_pairs={{0,32},{16,48},{32,64},{48,80},{64,96},{80,112},{96,128},{112,144}... | collective-permute-start | bytes 196616 | tf_op jit(solution)/shard_map/ppermute | solution.py:60
  68.5 5.3 %collective-permute-start.7 = (bf16[128,256]{1,0:T(8,128)(2,1)S(1)}, bf16[128,256]{1,0:T(8,128)(2,1)S(1)}, u32[]{:S(2)}, u32[]{:S(2)}) collective-permute-start(bf16[128,256]{1,0:T(8,128)(2,1)S(1)} %summed.3.refs_0_.own), channel_id=1, source_target_pairs={{0,16},{16,32},{32,48},{48,64},{64,80},{80,96},{96,112},{112,128},... | collective-permute-start | bytes 196616 | tf_op jit(solution)/shard_map/ppermute | solution.py:60
  73.9 3.3 %collective-permute-start.9 = (bf16[3,128,256]{2,1,0:T(8,128)(2,1)S(1)}, bf16[3,128,256]{2,1,0:T(8,128)(2,1)S(1)}, u32[]{:S(2)}, u32[]{:S(2)}) collective-permute-start(bf16[3,128,256]{2,1,0:T(8,128)(2,1)S(1)} %stacked.1), channel_id=1, source_target_pairs={{0,8},{8,0},{1,9},{9,1},{2,10},{10,2},{3,11},{11,3},{4,12},{12,4},... | collective-permute-start | bytes 589832 | tf_op jit(solution)/shard_map/ppermute | solution.py:64
  83.7 3.2 %collective-permute-start.10 = (bf16[2,128,256]{2,1,0:T(8,128)(2,1)S(1)}, bf16[2,128,256]{2,1,0:T(8,128)(2,1)S(1)}, u32[]{:S(2)}, u32[]{:S(2)}) collective-permute-start(bf16[2,128,256]{2,1,0:T(8,128)(2,1)S(1)} %get-tuple-element.25), channel_id=1, source_target_pairs={{0,8},{8,0},{1,9},{9,1},{2,10},{10,2},{3,11},{11,3},{4,12},{12,4},... | collective-permute-start | bytes 393224 | tf_op jit(solution)/shard_map/ppermute | solution.py:64
  87.5 6.9 %collective-permute-start.11 = (bf16[128,256]{1,0:T(8,128)(2,1)S(1)}, bf16[128,256]{1,0:T(8,128)(2,1)S(1)}, u32[]{:S(2)}, u32[]{:S(2)}) collective-permute-start(bf16[128,256]{1,0:T(8,128)(2,1)S(1)} %get-tuple-element.27), channel_id=1, source_target_pairs={{16,0},{32,16},{48,32},{64,48},{80,64},{96,80},{112,96},{128,112},... | collective-permute-start | bytes 196616 | tf_op jit(solution)/shard_map/ppermute | solution.py:60
  88.8 10.7 %collective-permute-start.12 = (bf16[128,256]{1,0:T(8,128)(2,1)S(1)}, bf16[128,256]{1,0:T(8,128)(2,1)S(1)}, u32[]{:S(2)}, u32[]{:S(2)}) collective-permute-start(bf16[128,256]{1,0:T(8,128)(2,1)S(1)} %get-tuple-element.28), channel_id=1, source_target_pairs={{32,0},{48,16},{64,32},{80,48},{96,64},{112,80},{128,96},{144,112}... | collective-permute-start | bytes 196616 | tf_op jit(solution)/shard_map/ppermute | solution.py:60
  109.8 3.8 %collective-permute-start.13 = (bf16[4,16,16,256]{3,2,1,0:T(8,128)(2,1)S(1)}, bf16[4,16,16,256]{3,2,1,0:T(8,128)(2,1)S(1)}, u32[]{:S(2)}, u32[]{:S(2)}) collective-permute-start(bf16[4,16,16,256]{3,2,1,0:T(8,128)(2,1)S(1)} %weight_grad.3), channel_id=1, source_target_pairs={{0,8},{8,0},{1,9},{9,1},{2,10},{10,2},{3,11},{11,3},{4,12},{12,4},... | collective-permute-start | bytes 1572872 | tf_op jit(solution)/shard_map/ppermute | solution.py:64
